TPU v7x, 32 devices: a whole 2x2x4 slice. The times are simulated.
32 devices in a mesh: dp: 16 (over z, y, core), branch: 2 (over x).
Axes of the slice: x: 2, y: 2, z: 4, core: 2. Of those that a mesh axis runs over, the one named last changes fastest.
Arguments:
- tokens: bfloat16 [16384, 1024], P(('dp', 'branch')), may hold values from -6 to 6
- lengths: int32 [16], P('dp'), may hold values from 30 to 1024, as said below
- norm_gain: bfloat16 [1024], replicated, may hold values from 0.5 to 1.5
- norm_shift: bfloat16 [1024], replicated, may hold values from -3 to 3
- qkv_weight: bfloat16 [1024, 3072], replicated, may hold values from -0.1875 to 0.1875
- proj_weight: bfloat16 [1024, 1024], replicated, may hold values from -2 to 2
- up_weight: bfloat16 [1024, 4096], replicated, may hold values from -0.1875 to 0.1875
- inner_bias: bfloat16 [4096], replicated, may hold values from -3 to 3
- down_weight: bfloat16 [4096, 1024], replicated, may hold values from -0.09375 to 0.09375
- outer_bias: bfloat16 [1024], replicated, may hold values from -3 to 3
- cotangent: bfloat16 [16384, 1024], P(('dp', 'branch')), may hold values from -6 to 6
Outputs:
- layer_out: bfloat16 [16384, 1024], P(('dp', 'branch'))
- tokens_grad: float32 [16384, 1024], P(('dp', 'branch'))
- gain_grad: float32 [1024], P(('dp', 'branch'))
- shift_grad: float32 [1024], P(('dp', 'branch'))
- qkv_grad: float32 [1024, 3072], P(('dp', 'branch'))
- proj_grad: float32 [1024, 1024], P(('dp', 'branch'))
- up_grad: float32 [1024, 4096], P(('dp', 'branch'))
- inner_grad: float32 [4096], P(('dp', 'branch'))
- down_grad: float32 [4096, 1024], P(('dp', 'branch'))
- outer_grad: float32 [1024], P(('dp', 'branch'))
Inputs may be any that keep to these rules, and one draw needn't show every extreme that they name: `lengths`: length of each sequence; some sequence has length 1024 in every draw.
All inputs are finite; a program needn't handle non-finite values.
Results may differ from a plain program's by a relative error of at most 0.0095.
Values may be sent and summed in bfloat16 or wider, within the bound.
No kernel may reach another device: no remote copies, remote signals or barrier semaphores. Data moves between devices by JAX's collectives and lax.ppermute only.
A program may use at most 320 MiB of HBM per device.

v0:
```python
import functools
import math

import jax
import jax.numpy as jnp
from jax import lax
from jax.experimental import pallas as pl
from jax.experimental.pallas import tpu as pltpu
from jax.sharding import PartitionSpec as P

D = 1024
HEADS = 16
HEAD_DIM = 64
ROT_DIM = 32
FF = 4096
SEQ_LEN = 1024
HALF = HEADS // 2 * HEAD_DIM
FF_HALF = FF // 2
LANES = 128
QB = 256
ROWS = 128
FB = 512
EPS = 1e-05
BF = jnp.bfloat16
F32 = jnp.float32


def params(mb=24):
    return pltpu.CompilerParams(vmem_limit_bytes=mb << 20)


def cost(flops, nbytes, trans=0):
    return pl.CostEstimate(flops=int(flops) // 1000, bytes_accessed=int(nbytes) // 1000, transcendentals=0)


def in_hbm(shape, dtype):
    return pltpu.HBM(tuple(shape), dtype)


def dot_nn(a, b):
    return jnp.dot(a, b, preferred_element_type=F32)


def dot_nt(a, b):
    return lax.dot_general(a, b, (((1,), (1,)), ((), ())), preferred_element_type=F32)


def dot_tn(a, b):
    return lax.dot_general(a, b, (((0,), (0,)), ((), ())), preferred_element_type=F32)


def rotary_tables():
    lane = jnp.arange(LANES, dtype=jnp.int32)
    channel = lane % HEAD_DIM
    frequency = jnp.power(10000.0, -(2.0 * (channel // 2).astype(F32)) / ROT_DIM)
    frequency = jnp.where(channel < ROT_DIM, frequency, 0.0)
    step = 32
    index = jnp.arange(2 * step, dtype=jnp.int32)
    position = jnp.where(index < step, index * (SEQ_LEN // step), index - step).astype(F32)
    angles = position[:, None] * frequency[None, :]
    cosine, sine = lax.optimization_barrier((jnp.cos(angles), jnp.sin(angles)))
    high_cosine, high_sine = cosine[:step, None], sine[:step, None]
    low_cosine, low_sine = cosine[None, step:], sine[None, step:]
    even = (lane % 2 == 0)[None, None, :]
    sine = high_sine * low_cosine + high_cosine * low_sine
    cosine = high_cosine * low_cosine - high_sine * low_sine
    return cosine.reshape(SEQ_LEN, LANES), jnp.where(even, -sine, sine).reshape(SEQ_LEN, LANES)


def rotate(x, cosine, sine):
    even = lax.broadcasted_iota(jnp.int32, x.shape, 1) % 2 == 0
    swapped = jnp.where(even, pltpu.roll(x, LANES - 1, 1), pltpu.roll(x, 1, 1))
    return x * cosine + swapped * sine


def unrotate(y, cosine, sine):
    even = lax.broadcasted_iota(jnp.int32, y.shape, 1) % 2 == 0
    swapped = jnp.where(even, pltpu.roll(y, LANES - 1, 1), pltpu.roll(y, 1, 1))
    return y * cosine - swapped * sine


def head_lanes(shape, head):
    lane = lax.broadcasted_iota(jnp.int32, shape, 1)
    own = (lane >= HEAD_DIM) if head else (lane < HEAD_DIM)
    spare = lane - (0 if head else HEAD_DIM)
    return own, spare


def keys_with_bias(k, head, length):
    own, spare = head_lanes(k.shape, head)
    row = lax.broadcasted_iota(jnp.int32, k.shape, 0)
    bias = jnp.where(row < length, 0.0, -1e30)
    extra = jnp.where(spare < 3, 1.0, jnp.where(spare == 3, bias, 0.0))
    return jnp.where(own, k.astype(F32), extra).astype(BF)


def attend_kernel(info_ref, q_ref, k_ref, v_ref, o_ref, qe_ref):
    length = info_ref[1]
    q = q_ref[0].astype(F32)
    k = k_ref[0]
    v = v_ref[0]
    tri = lax.broadcasted_iota(jnp.int32, (QB, QB), 0) >= lax.broadcasted_iota(jnp.int32, (QB, QB), 1)
    outs = []
    for head in range(2):
        own, spare = head_lanes((SEQ_LEN, LANES), head)
        ke = keys_with_bias(k, head, length)
        qe = jnp.where(own, q, jnp.where(spare == 3, 1.0, 0.0)).astype(BF)
        parts = []
        for b in range(SEQ_LEN // QB):
            lo, hi = b * QB, (b + 1) * QB
            s = dot_nt(qe[lo:hi], ke[:hi])
            diag = jnp.where(tri, s[:, lo:hi], -1e30)
            s = diag if b == 0 else jnp.concatenate([s[:, :lo], diag], axis=1)
            top = jnp.max(s, axis=1, keepdims=True)
            p = jnp.exp(s - top)
            total = jnp.sum(p, axis=1, keepdims=True)
            parts.append(dot_nn(p.astype(BF), v[:hi]) * (1.0 / total))
            lse = jnp.broadcast_to(top + jnp.log(total), (QB, LANES))
            first = lse.astype(BF).astype(F32)
            second = (lse - first).astype(BF).astype(F32)
            third = lse - first - second
            own_b, spare_b = head_lanes((QB, LANES), head)
            extra = jnp.where(
                spare_b == 0,
                -first,
                jnp.where(
                    spare_b == 1,
                    -second,
                    jnp.where(spare_b == 2, -third, jnp.where(spare_b == 3, 1.0, 0.0)),
                ),
            )
            qe_ref[head, lo:hi, :] = jnp.where(own_b, q[lo:hi], extra).astype(BF)
        outs.append(jnp.concatenate(parts, axis=0))
    own, _ = head_lanes((SEQ_LEN, LANES), 0)
    o_ref[...] = jnp.where(own, outs[0], outs[1]).astype(BF)


def attend_call(info, qkv):
    pairs = HALF // LANES
    spec = [pl.BlockSpec((1, SEQ_LEN, LANES), lambda p, n, t=t: (t, 0, p)) for t in range(3)]
    return pl.pallas_call(
        attend_kernel,
        grid_spec=pltpu.PrefetchScalarGridSpec(
            num_scalar_prefetch=1,
            grid=(pairs,),
            in_specs=spec,
            out_specs=[
                pl.BlockSpec((SEQ_LEN, LANES), lambda p, n: (0, p)),
                pl.BlockSpec((2, SEQ_LEN, LANES), lambda p, n: (p, 0, 0)),
            ],
        ),
        out_shape=[
            in_hbm((SEQ_LEN, HALF), BF),
            in_hbm((HEADS // 2, SEQ_LEN, LANES), BF),
        ],
        compiler_params=params(),
        cost_estimate=cost(
            2 * pairs * 10 * SEQ_LEN * SEQ_LEN * LANES, 2 * SEQ_LEN * HALF * 3, 4 * SEQ_LEN * SEQ_LEN
        ),
        name="attend",
    )(info, qkv, qkv, qkv)


def attend_back_kernel(info_ref, qe_ref, k_ref, v_ref, o_ref, g_ref, cos_ref, sin_ref, d_ref, dk_ref, dv_ref):
    length = info_ref[1]
    k = k_ref[0]
    v = v_ref[0]
    g = g_ref[...].astype(F32)
    o = o_ref[...].astype(F32)
    tri = lax.broadcasted_iota(jnp.int32, (QB, QB), 0) >= lax.broadcasted_iota(jnp.int32, (QB, QB), 1)
    queries = []
    for head in range(2):
        own, spare = head_lanes((SEQ_LEN, LANES), head)
        ke = keys_with_bias(k, head, length)
        ve = jnp.where(own, v.astype(F32), jnp.where(spare < 3, 1.0, 0.0)).astype(BF)
        inner = jnp.sum(jnp.where(own, g * o, 0.0), axis=1, keepdims=True)
        inner = jnp.broadcast_to(inner, (SEQ_LEN, LANES))
        first = inner.astype(BF).astype(F32)
        second = (inner - first).astype(BF).astype(F32)
        third = inner - first - second
        extra = jnp.where(
            spare == 0,
            -first,
            jnp.where(spare == 1, -second, jnp.where(spare == 2, -third, 0.0)),
        )
        ge = jnp.where(own, g, extra).astype(BF)
        parts = []
        for b in range(SEQ_LEN // QB):
            lo, hi = b * QB, (b + 1) * QB
            qb = qe_ref[head, lo:hi, :]
            gb = ge[lo:hi]
            s = dot_nt(qb, ke[:hi])
            diag = jnp.where(tri, s[:, lo:hi], -1e30)
            s = diag if b == 0 else jnp.concatenate([s[:, :lo], diag], axis=1)
            p = jnp.exp(s)
            ds = (p * dot_nt(gb, ve[:hi])).astype(BF)
            parts.append(dot_nn(ds, k[:hi]))
            dk = dot_tn(ds, qb)
            dv = dot_tn(p.astype(BF), gb)
            if b > 0:
                dk_ref[head, :lo] += dk[:lo]
                dv_ref[head, :lo] += dv[:lo]
            dk_ref[head, lo:hi] = dk[lo:hi]
            dv_ref[head, lo:hi] = dv[lo:hi]
        queries.append(jnp.concatenate(parts, axis=0))
    own, _ = head_lanes((SEQ_LEN, LANES), 0)
    cosine, sine = cos_ref[...], sin_ref[...]
    dq = jnp.where(own, queries[0], queries[1]) * HEAD_DIM**-0.5
    d_ref[0] = unrotate(dq, cosine, sine).astype(BF)
    d_ref[1] = unrotate(jnp.where(own, dk_ref[0], dk_ref[1]), cosine, sine).astype(BF)
    d_ref[2] = jnp.where(own, dv_ref[0], dv_ref[1]).astype(BF)


def attend_back_call(info, qe, qkv, context, grad_context, cosine, sine):
    pairs = HALF // LANES
    table = pl.BlockSpec((SEQ_LEN, LANES), lambda p, n: (0, 0))
    return pl.pallas_call(
        attend_back_kernel,
        grid_spec=pltpu.PrefetchScalarGridSpec(
            num_scalar_prefetch=1,
            grid=(pairs,),
            in_specs=[
                pl.BlockSpec((2, SEQ_LEN, LANES), lambda p, n: (p, 0, 0)),
                pl.BlockSpec((1, SEQ_LEN, LANES), lambda p, n: (1, 0, p)),
                pl.BlockSpec((1, SEQ_LEN, LANES), lambda p, n: (2, 0, p)),
                pl.BlockSpec((SEQ_LEN, LANES), lambda p, n: (0, p)),
                pl.BlockSpec((SEQ_LEN, LANES), lambda p, n: (0, p)),
                table,
                table,
            ],
            out_specs=pl.BlockSpec((3, SEQ_LEN, LANES), lambda p, n: (0, 0, p)),
            scratch_shapes=[
                pltpu.VMEM((2, SEQ_LEN, LANES), F32),
                pltpu.VMEM((2, SEQ_LEN, LANES), F32),
            ],
        ),
        out_shape=jax.ShapeDtypeStruct((3, SEQ_LEN, HALF), BF),
        compiler_params=params(),
        cost_estimate=cost(
            2 * pairs * 12 * SEQ_LEN * SEQ_LEN * LANES, 2 * SEQ_LEN * HALF * 4, 4 * SEQ_LEN * SEQ_LEN
        ),
        name="attend_back",
    )(info, qe, qkv, qkv, context, grad_context, cosine, sine)


def gelu_parts(v):
    c = math.sqrt(2.0 / math.pi)
    square = v * v
    half = 0.5 + 0.5 * jnp.tanh(v * (c + (c * 0.044715) * square))
    hidden = v * half
    slope = half * (1.0 + (v - hidden) * (2.0 * c + (6.0 * c * 0.044715) * square))
    return hidden, slope


def normalize(x):
    x = x.astype(F32)
    centred = x - jnp.mean(x, axis=1, keepdims=True)
    rstd = lax.rsqrt(jnp.mean(centred * centred, axis=1, keepdims=True) + EPS)
    return centred * rstd, rstd


def masked_rows(g, start, length):
    row = start + lax.broadcasted_iota(jnp.int32, g.shape, 0)
    return jnp.where(row < length, g.astype(F32), 0.0)


def joined(refs, axis):
    return refs[0][...] if len(refs) == 1 else jnp.concatenate([r[...] for r in refs], axis=axis)


def weight_specs(plan, rows_too=True):
    splits, wide, pick = plan["splits"], FB // plan["splits"], plan["pick"]
    specs = [pl.BlockSpec((D, wide), lambda s, *a, i=i: (0, pick(s, a, i))) for i in range(splits)]
    specs += [pl.BlockSpec((wide, D), lambda s, *a, i=i: (pick(s, a, i), 0)) for i in range(splits)]
    if rows_too:
        specs += [pl.BlockSpec((1, wide), lambda s, *a, i=i: (0, pick(s, a, i))) for i in range(splits)]
    return specs


def accumulate(ref, value):
    @pl.when(pl.program_id(0) == 0)
    def _():
        ref[...] = value

    @pl.when(pl.program_id(0) > 0)
    def _():
        ref[...] += value


def mlp_own_kernel(splits, info_ref, cls_ref, t_ref, c_ref, gain_ref, shift_ref, *refs):
    ups, downs, biases = refs[:splits], refs[splits : 2 * splits], refs[2 * splits : 3 * splits]
    x_ref, h_ref, g_ref, gb_ref, e_ref, gn_ref, outer_ref = refs[3 * splits :]

    @pl.when(pl.program_id(0) == 0)
    def _():
        outer_ref[...] = jnp.zeros_like(outer_ref)

        @pl.loop(0, t_ref.shape[0] // ROWS)
        def _(r):
            at = pl.ds(pl.multiple_of(r * ROWS, ROWS), ROWS)
            hat, _ = normalize(t_ref[at, :])
            x_ref[at, :] = (hat * gain_ref[...].astype(F32) + shift_ref[...].astype(F32)).astype(BF)
            g = masked_rows(c_ref[at, :], info_ref[0] * c_ref.shape[0] + r * ROWS, info_ref[1])
            g_ref[at, :] = g.astype(BF)
            outer_ref[...] += jnp.sum(g, axis=0, keepdims=True)

    up, down, bias = joined(ups, 1), joined(downs, 0), joined(biases, 1)
    before = dot_nn(x_ref[...], up) + bias.astype(F32)
    hidden, slope = gelu_parts(before)
    hidden = hidden.astype(BF)
    grad_before = (dot_nt(g_ref[...], down) * slope).astype(BF)
    h_ref[...] = hidden
    gb_ref[...] = grad_before
    accumulate(e_ref, dot_nn(hidden, down))
    accumulate(gn_ref, dot_nt(grad_before, up))


def mlp_own_call(info, plan, tokens, cotangent, gain, shift):
    rows, splits = tokens.shape[0], plan["splits"]
    fixed = lambda s, *a: (0, 0)
    up, down, bias = plan["weights"]
    whole = pl.BlockSpec((rows, D), fixed)
    wide = pl.BlockSpec((rows, FB), lambda s, *a: (0, s))
    return pl.pallas_call(
        functools.partial(mlp_own_kernel, splits),
        grid_spec=pltpu.PrefetchScalarGridSpec(
            num_scalar_prefetch=2,
            grid=(FF_HALF // FB,),
            in_specs=[whole, whole, pl.BlockSpec((1, D), fixed), pl.BlockSpec((1, D), fixed)] + weight_specs(plan),
            out_specs=[whole, wide, whole, wide, whole, whole, pl.BlockSpec((1, D), fixed)],
        ),
        out_shape=[
            jax.ShapeDtypeStruct((2 * rows, D), BF),
            in_hbm((2 * rows, FF_HALF), BF),
            in_hbm((rows, D), BF),
            in_hbm((rows, FF_HALF), BF),
            in_hbm((rows, D), F32),
            in_hbm((rows, D), F32),
            jax.ShapeDtypeStruct((1, D), F32),
        ],
        compiler_params=params(),
        cost_estimate=cost(8 * rows * D * FF_HALF, 12 * rows * D + 4 * D * FF_HALF, rows * FF_HALF),
        name="mlp_own",
    )(info, plan["classes"], tokens, cotangent, gain, shift, *([up] * splits), *([down] * splits), *([bias] * splits))


def mlp_forward_kernel(splits, info_ref, cls_ref, t_ref, gain_ref, shift_ref, *refs):
    ups, downs, biases = refs[:splits], refs[splits : 2 * splits], refs[2 * splits : 3 * splits]
    x_ref, h_ref, slope_ref, e_ref = refs[3 * splits + 2 :]

    @pl.when(pl.program_id(0) == 0)
    def _():
        @pl.loop(0, t_ref.shape[0] // ROWS)
        def _(r):
            at = pl.ds(pl.multiple_of(r * ROWS, ROWS), ROWS)
            hat, _ = normalize(t_ref[at, :])
            x_ref[at, :] = (hat * gain_ref[...].astype(F32) + shift_ref[...].astype(F32)).astype(BF)

    up, down, bias = joined(ups, 1), joined(downs, 0), joined(biases, 1)
    before = dot_nn(x_ref[...], up) + bias.astype(F32)
    hidden, slope = gelu_parts(before)
    hidden = hidden.astype(BF)
    h_ref[...] = hidden
    slope_ref[...] = slope.astype(BF)
    accumulate(e_ref, dot_nn(hidden, down))


def mlp_forward_call(info, plan, tokens, gain, shift, normed, hidden):
    rows, splits = tokens.shape[0], plan["splits"]
    fixed = lambda s, *a: (0, 0)
    up, down, bias = plan["weights"]
    whole = pl.BlockSpec((rows, D), fixed)
    anywhere = pl.BlockSpec(memory_space=pl.ANY)
    first = 5 + 3 * splits
    return pl.pallas_call(
        functools.partial(mlp_forward_kernel, splits),
        grid_spec=pltpu.PrefetchScalarGridSpec(
            num_scalar_prefetch=2,
            grid=(FF_HALF // FB,),
            in_specs=[whole, pl.BlockSpec((1, D), fixed), pl.BlockSpec((1, D), fixed)]
            + weight_specs(plan)
            + [anywhere, anywhere],
            out_specs=[
                pl.BlockSpec((rows, D), lambda s, *a: (1, 0)),
                pl.BlockSpec((rows, FB), lambda s, *a: (1, s)),
                pl.BlockSpec((rows, FB), lambda s, *a: (0, s)),
                whole,
            ],
        ),
        out_shape=[
            jax.ShapeDtypeStruct((2 * rows, D), BF),
            in_hbm((2 * rows, FF_HALF), BF),
            in_hbm((rows, FF_HALF), BF),
            in_hbm((rows, D), F32),
        ],
        input_output_aliases={first: 0, first + 1: 1},
        compiler_params=params(),
        cost_estimate=cost(4 * rows * D * FF_HALF, 12 * rows * D + 4 * D * FF_HALF, rows * FF_HALF),
        name="mlp_forward",
    )(info, plan["classes"], tokens, gain, shift, *([up] * splits), *([down] * splits), *([bias] * splits), normed, hidden)


def down_grad_kernel(splits, pieces, info_ref, cls_ref, sub_ref, h_ref, go_ref, c_ref, g_ref, *grads):
    rows = c_ref.shape[0]
    step = pl.program_id(0)

    @pl.when(step == 0)
    def _():
        g_ref[:rows] = go_ref[...]
        g_ref[rows:] = masked_rows(c_ref[...], (1 - info_ref[0]) * rows, info_ref[1]).astype(BF)

    grad_down = dot_tn(h_ref[...], g_ref[...]).astype(BF)
    if not pieces:
        grads[0][...] = grad_down
        return
    down_keep, down_send = grads
    block = FB // splits

    @pl.when(step < 2)
    def _():
        for i in range(splits):
            down_send[sub_ref[i]] = grad_down[i * block : (i + 1) * block]

    @pl.when(step >= 2)
    def _():
        for i in range(splits):
            down_keep[sub_ref[i]] = grad_down[i * block : (i + 1) * block]


def down_grad_call(info, plan, hidden, grads_own, cotangent):
    rows, splits, pieces = cotangent.shape[0], plan["splits"], plan["pieces"]
    fixed = lambda s, *a: (0, 0)
    whole = pl.BlockSpec((rows, D), fixed)
    out_specs = [pl.BlockSpec((2 * rows, D), fixed)]
    out_shape = [in_hbm((2 * rows, D), BF)]
    if pieces:
        half, down_rows = pieces // 2, FF_HALF // pieces
        out_specs += [
            pl.BlockSpec((splits, down_rows, D), lambda s, *a: (jnp.maximum(s - 2, 0), 0, 0)),
            pl.BlockSpec((splits, down_rows, D), lambda s, *a: (jnp.minimum(s, 1), 0, 0)),
        ]
        out_shape += [in_hbm((half, down_rows, D), BF)] * 2
    else:
        out_specs += [pl.BlockSpec((FB, D), lambda s, *a: (s, 0))]
        out_shape += [in_hbm((FF_HALF, D), BF)]
    return pl.pallas_call(
        functools.partial(down_grad_kernel, splits, pieces),
        grid_spec=pltpu.PrefetchScalarGridSpec(
            num_scalar_prefetch=3,
            grid=(FF_HALF // FB,),
            in_specs=[pl.BlockSpec((2 * rows, FB), lambda s, *a: (0, s)), whole, whole],
            out_specs=out_specs,
        ),
        out_shape=out_shape,
        compiler_params=params(),
        cost_estimate=cost(4 * rows * D * FF_HALF, 8 * rows * D + 2 * D * FF_HALF + 4 * rows * FF_HALF),
        name="down_grad",
    )(info, plan["classes"], plan["subs"], hidden, grads_own, cotangent)


def mlp_back_kernel(splits, pieces, info_ref, cls_ref, ord_ref, x_ref, slope_ref, g_ref, gb_ref, *refs):
    ups, downs = refs[:splits], refs[splits : 2 * splits]
    gn_ref, inner_ref, *grads = refs[2 * splits : -2 if pieces else -1]
    gball_ref = refs[-2 if pieces else -1]
    rows = g_ref.shape[0]
    up, down = joined(ups, 1), joined(downs, 0)
    grad_before = (dot_nt(g_ref[...], down) * slope_ref[...].astype(F32)).astype(BF)
    gball_ref[:rows] = gb_ref[...]
    gball_ref[rows:] = grad_before
    accumulate(gn_ref, dot_nt(grad_before, up))
    inner_ref[...] = jnp.sum(gball_ref[...].astype(F32), axis=0, keepdims=True)
    grad_up = dot_tn(x_ref[...], gball_ref[...]).astype(BF)
    if not pieces:
        grads[0][...] = grad_up
        return
    up_keep, up_send = grads
    upall_ref = refs[-1]
    upall_ref[...] = grad_up.reshape(upall_ref.shape)
    for q in range(pieces // 2):
        up_keep[q] = upall_ref[ord_ref[q]]
        up_send[q] = upall_ref[ord_ref[q + pieces // 2]]


def mlp_back_call(info, plan, normed, slope, grads, gb_own):
    rows, splits, pieces = gb_own.shape[0], plan["splits"], plan["pieces"]
    fixed = lambda s, *a: (0, 0)
    up, down, _ = plan["weights"]
    whole = pl.BlockSpec((rows, D), fixed)
    wide = pl.BlockSpec((rows, FB), lambda s, *a: (0, s))
    out_specs = [whole, pl.BlockSpec((1, FB), lambda s, i, cls, *a: (0, cls[s]))]
    out_shape = [in_hbm((rows, D), F32), jax.ShapeDtypeStruct((1, FF_HALF), F32)]
    scratch = [pltpu.VMEM((2 * rows, FB), BF)]
    if pieces:
        shape = (pieces // 2, D // pieces, FB)
        out_specs += [pl.BlockSpec(shape, lambda s, i, cls, *a: (0, 0, cls[s]))] * 2
        out_shape += [in_hbm(shape[:2] + (FF_HALF,), BF)] * 2
        scratch.append(pltpu.VMEM((pieces, D // pieces, FB), BF))
    else:
        out_specs += [pl.BlockSpec((D, FB), lambda s, *a: (0, s))]
        out_shape += [in_hbm((D, FF_HALF), BF)]
    return pl.pallas_call(
        functools.partial(mlp_back_kernel, splits, pieces),
        grid_spec=pltpu.PrefetchScalarGridSpec(
            num_scalar_prefetch=3,
            grid=(FF_HALF // FB,),
            in_specs=[
                pl.BlockSpec((2 * rows, D), fixed),
                wide,
                pl.BlockSpec((rows, D), lambda s, *a: (1, 0)),
                wide,
            ]
            + weight_specs(plan, False),
            out_specs=out_specs,
            scratch_shapes=scratch,
        ),
        out_shape=out_shape,
        compiler_params=params(),
        cost_estimate=cost(8 * rows * D * FF_HALF, 12 * rows * D + 6 * D * FF_HALF + 4 * rows * FF_HALF),
        name="mlp_back",
    )(info, plan["classes"], plan["order"], normed, slope, grads, gb_own, *([up] * splits), *([down] * splits))


def qkv_half_kernel(place_ref, info_ref, x_ref, w_ref, cos_ref, sin_ref, *refs):
    o_ref = refs[-1]
    t = pl.program_id(0)
    chunk = 2 * LANES

    @pl.when(t == 2)
    def _():
        for c in range(0, HALF, chunk):
            o_ref[0, :, c : c + chunk] = dot_nn(x_ref[...], w_ref[:, c : c + chunk]).astype(BF)

    @pl.when(t < 2)
    def _():
        scale = jnp.where(t == 0, HEAD_DIM**-0.5, 1.0)
        cosine = cos_ref[...] * scale
        sine = sin_ref[...] * scale
        for c in range(0, HALF, chunk):
            mixed = dot_nn(x_ref[...], w_ref[:, c : c + chunk])
            for e in range(0, chunk, LANES):
                o_ref[0, :, c + e : c + e + LANES] = rotate(mixed[:, e : e + LANES], cosine, sine).astype(BF)


def qkv_half_call(place, info, half, normed, w, cosine, sine, qkv=None):
    rows = normed.shape[0] // 2
    table = pl.BlockSpec((rows, LANES), lambda t, p, i: (p[0], 0))
    more = [] if qkv is None else [qkv]
    return pl.pallas_call(
        qkv_half_kernel,
        grid_spec=pltpu.PrefetchScalarGridSpec(
            num_scalar_prefetch=2,
            grid=(3,),
            in_specs=[
                pl.BlockSpec((rows, D), lambda t, p, i: (half, 0)),
                pl.BlockSpec((D, HALF), lambda t, p, i: (0, 2 * t + i[0])),
                table,
                table,
            ]
            + [pl.BlockSpec(memory_space=pl.ANY)] * len(more),
            out_specs=pl.BlockSpec((1, rows, HALF), lambda t, p, i: (t, p[0], 0)),
        ),
        out_shape=in_hbm((3, 2 * rows, HALF), BF),
        input_output_aliases={6: 0} if more else {},
        compiler_params=params(),
        cost_estimate=cost(2 * rows * D * 3 * HALF, 2 * (rows * D + D * 3 * HALF + rows * 3 * HALF)),
        name="qkv",
    )(place, info, normed, w, cosine, sine, *more)


def send_out_kernel(place_ref, info_ref, c_ref, w_ref, e_ref, o_ref):
    o_ref[...] = (dot_nn(c_ref[...], w_ref[...]) + e_ref[...]).astype(BF)


def finish_out_kernel(place_ref, info_ref, c_ref, w_ref, e_ref, t_ref, r_ref, bias_ref, o_ref):
    total = dot_nn(c_ref[...], w_ref[...]) + e_ref[...] + bias_ref[...].astype(F32)
    o_ref[...] = (total + t_ref[...].astype(F32) + r_ref[...].astype(F32)).astype(BF)


def out_call(place, info, context, proj, expanded, rest=()):
    rows, block = expanded.shape[0], 256
    steps = rows // block
    row = pl.BlockSpec((block, D), lambda s, p, i: (s, 0))
    return pl.pallas_call(
        finish_out_kernel if rest else send_out_kernel,
        grid_spec=pltpu.PrefetchScalarGridSpec(
            num_scalar_prefetch=2,
            grid=(steps,),
            in_specs=[
                pl.BlockSpec((block, HALF), lambda s, p, i: (p[0] * steps + s, 0)),
                pl.BlockSpec((HALF, D), lambda s, p, i: (i[0], 0)),
                row,
            ]
            + ([row, row, pl.BlockSpec((1, D), lambda s, p, i: (0, 0))] if rest else []),
            out_specs=row,
        ),
        out_shape=in_hbm((rows, D), BF),
        compiler_params=params(),
        cost_estimate=cost(2 * rows * D * HALF, 8 * rows * D + 2 * HALF * D),
        name="finish_out" if rest else "send_out",
    )(place, info, context, proj, expanded, *rest)


def proj_back_kernel(info_ref, ord_ref, g_ref, c_ref, w_ref, gc_ref, *refs):
    acc_ref = refs[-2] if len(refs) > 2 else refs[-1]
    gc_ref[...] = dot_nt(g_ref[...], w_ref[...]).astype(BF)
    part = dot_tn(c_ref[...], g_ref[...])

    @pl.when(pl.program_id(0) == 0)
    def _():
        acc_ref[...] = part

    @pl.when(pl.program_id(0) == 1)
    def _():
        total = (acc_ref[...] + part).astype(BF)
        if len(refs) == 2:
            refs[0][...] = total
        else:
            keep, send, all_ref = refs[0], refs[1], refs[3]
            all_ref[...] = total.reshape(all_ref.shape)
            half = keep.shape[0]
            for q in range(half):
                keep[q] = all_ref[ord_ref[q]]
                send[q] = all_ref[ord_ref[q + half]]


def proj_back_call(info, plan, order, grads, context, proj):
    rows, pieces = grads.shape[0] // 2, plan["pieces"]
    scratch = [pltpu.VMEM((HALF, D), F32)]
    if pieces:
        shape = (pieces // 2, HALF // pieces, D)
        out_specs = [pl.BlockSpec(shape, lambda h, *a: (0, 0, 0))] * 2
        out_shape = [in_hbm(shape, BF)] * 2
        scratch.append(pltpu.VMEM((pieces, HALF // pieces, D), BF))
    else:
        out_specs = [pl.BlockSpec((HALF, D), lambda h, *a: (0, 0))]
        out_shape = [in_hbm((HALF, D), BF)]
    return pl.pallas_call(
        proj_back_kernel,
        grid_spec=pltpu.PrefetchScalarGridSpec(
            num_scalar_prefetch=2,
            grid=(2,),
            in_specs=[
                pl.BlockSpec((rows, D), lambda h, i, o: (h, 0)),
                pl.BlockSpec((rows, HALF), lambda h, i, o: (jnp.bitwise_xor(h, i[0]), 0)),
                pl.BlockSpec((HALF, D), lambda h, i, o: (i[0], 0)),
            ],
            out_specs=[pl.BlockSpec((rows, HALF), lambda h, i, o: (jnp.bitwise_xor(h, i[0]), 0))] + out_specs,
            scratch_shapes=scratch,
        ),
        out_shape=[in_hbm((2 * rows, HALF), BF)] + out_shape,
        compiler_params=params(),
        cost_estimate=cost(8 * rows * D * HALF, 4 * rows * D + 8 * rows * HALF + 4 * HALF * D),
        name="proj_back",
    )(info, order, grads, context, proj)


def line_of(p, rows, sums, outer, inner_ref):
    low = lax.broadcasted_iota(jnp.int32, (1, LANES), 1) < rows
    at = p // 2 * LANES
    three = [v[:, at : at + LANES] for v in (sums[0:1], sums[1:2], outer)]
    turned = [pltpu.roll(v, rows, 1) for v in three]
    if p % 2:
        three, turned = turned, three
    at = p % 4 * HALF + p // 4 * LANES
    parts = [jnp.where(low, three[0], turned[1]), jnp.where(low, three[2], 0.0), inner_ref[:, at : at + LANES]]
    return jnp.concatenate(parts + [jnp.zeros((1, LANES), F32)], axis=1)


def pair_grad_kernel(info_ref, ord_ref, x_ref, own_ref, their_ref, *refs):
    d = jnp.concatenate([own_ref[0], their_ref[0]], axis=0)
    total = dot_tn(x_ref[...], d).astype(BF)
    if len(refs) == 1:
        refs[0][...] = total
        return
    pk_ref, ps_ref, keep, send, all_ref = refs
    half, rows = keep.shape[0], all_ref.shape[1]
    all_ref[...] = total.reshape(all_ref.shape)
    for q in range(half):
        for out, proj, at in ((keep, pk_ref, q), (send, ps_ref, q + half)):
            out[q, :rows] = all_ref[ord_ref[at]]
            out[q, rows:] = proj[q]


def value_grad_kernel(info_ref, ord_ref, x_ref, own_ref, their_ref, so_ref, st_ref, outer_ref, inner_ref, keep, send,
                      all_ref):
    pieces, rows = all_ref.shape[0], x_ref.shape[1] // all_ref.shape[0]
    half = pieces // 2
    d = jnp.concatenate([own_ref[0], their_ref[0]], axis=0)
    all_ref[:, :rows] = dot_tn(x_ref[...], d).astype(BF).reshape(pieces, rows, HALF)
    sums = so_ref[...] + st_ref[...]
    outer = outer_ref[...]
    for p in range(pieces):
        line = line_of(p, rows, sums, outer, inner_ref)
        all_ref[p, rows:] = jnp.broadcast_to(line, (all_ref.shape[1] - rows, HALF)).astype(BF)
    for q in range(half):
        keep[q] = all_ref[ord_ref[q]]
        send[q] = all_ref[ord_ref[q + half]]


def qkv_grad_call(info, plan, normed, dmix, first, count, extra=()):
    rows, pieces = normed.shape[0] // 2, plan["pieces"]
    in_specs, scratch, kernel = [], [], pair_grad_kernel
    if not pieces:
        extra = ()
        out_specs = [pl.BlockSpec((D, HALF), lambda t, *a: (0, t))]
        out_shape = [in_hbm((D, count * HALF), BF)]
    else:
        height = D // pieces
        if count == 2:
            shape = (pieces // 2, height + HALF // pieces, HALF)
            in_specs = [pl.BlockSpec((pieces // 2, HALF // pieces, HALF), lambda t, *a: (0, 0, t))] * 2
            scratch = [pltpu.VMEM((pieces, height, HALF), BF)]
        else:
            kernel = value_grad_kernel
            shape = (pieces // 2, height + 16, HALF)
            in_specs = [pl.BlockSpec(v.shape, lambda t, *a: (0, 0)) for v in extra]
            scratch = [pltpu.VMEM((pieces, height + 16, HALF), BF)]
        out_specs = [pl.BlockSpec(shape, lambda t, *a: (0, 0, t))] * 2
        out_shape = [in_hbm(shape[:2] + (count * HALF,), BF)] * 2
    return pl.pallas_call(
        kernel,
        grid_spec=pltpu.PrefetchScalarGridSpec(
            num_scalar_prefetch=2,
            grid=(count,),
            in_specs=[
                pl.BlockSpec((2 * rows, D), lambda t, *a: (0, 0)),
                pl.BlockSpec((1, rows, HALF), lambda t, i, *a: (first + t, i[0], 0)),
                pl.BlockSpec((1, rows, HALF), lambda t, i, *a: (first + t, 1 - i[0], 0)),
            ]
            + in_specs,
            out_specs=out_specs,
            scratch_shapes=scratch,
        ),
        out_shape=out_shape,
        compiler_params=params(),
        cost_estimate=cost(4 * rows * D * count * HALF, 4 * rows * D + (4 * rows + 2 * D) * count * HALF),
        name="qkv_grad",
    )(info, plan["order"], normed, dmix, dmix, *extra)


def grad_normed_kernel(place_ref, info_ref, d_ref, wq_ref, wk_ref, wv_ref, base_ref, t_ref, *refs):
    outs, sum_ref = refs[:-1], refs[-1]
    total = base_ref[...]
    for t, w in enumerate((wq_ref, wk_ref, wv_ref)):
        total += dot_nt(d_ref[t], w[...])
    if len(outs) == 1:
        outs[0][...] = total.astype(outs[0].dtype)
    else:
        for r, o_ref in enumerate(outs):

            @pl.when(pl.program_id(0) == r)
            def _(o_ref=o_ref):
                o_ref[...] = total.astype(o_ref.dtype)

    hat, _ = normalize(t_ref[...])
    sums = jnp.concatenate([jnp.sum(total * hat, axis=0, keepdims=True), jnp.sum(total, axis=0, keepdims=True)], axis=0)
    accumulate(sum_ref, sums)


def grad_normed_call(place, info, dmix, w, base, tokens, parts):
    rows, block = base.shape[0], 256
    steps = rows // block
    row = pl.BlockSpec((block, D), lambda r, p, i: (r, 0))
    kind = BF if parts else F32
    count = parts or 1
    return pl.pallas_call(
        grad_normed_kernel,
        grid_spec=pltpu.PrefetchScalarGridSpec(
            num_scalar_prefetch=2,
            grid=(steps,),
            in_specs=[pl.BlockSpec((3, block, HALF), lambda r, p, i: (0, p[0] * steps + r, 0))]
            + [pl.BlockSpec((D, HALF), lambda r, p, i, t=t: (0, 2 * t + i[0])) for t in range(3)]
            + [row, row],
            out_specs=([row] if count == 1 else [pl.BlockSpec((block, D), lambda r, p, i: (0, 0))] * count)
            + [pl.BlockSpec((2, D), lambda r, p, i: (0, 0))],
        ),
        out_shape=[in_hbm((rows // count, D), kind)] * count + [jax.ShapeDtypeStruct((2, D), F32)],
        compiler_params=params(),
        cost_estimate=cost(2 * rows * D * 3 * HALF, 8 * rows * D + 6 * D * HALF + 6 * rows * HALF),
        name="grad_normed",
    )(place, info, dmix, w, w, w, base, tokens)


def assemble_kernel(sources, width, info_ref, mine_ref, their_ref, o_ref):
    first = info_ref[0] == 0
    rows = o_ref.shape[0]
    for k, at in enumerate(sources):
        mine = mine_ref[:, at : at + width]
        theirs = their_ref[:rows, at : at + width].astype(F32)
        o_ref[:, 2 * k * width : (2 * k + 1) * width] = jnp.where(first, mine, theirs)
        o_ref[:, (2 * k + 1) * width : (2 * k + 2) * width] = jnp.where(first, theirs, mine)


def assemble_call(info, mine, theirs, sources, width):
    whole = lambda v: pl.BlockSpec(v.shape, lambda s, i: (0, 0))
    shape = (mine.shape[0], 2 * width * len(sources))
    return pl.pallas_call(
        functools.partial(assemble_kernel, sources, width),
        grid_spec=pltpu.PrefetchScalarGridSpec(
            num_scalar_prefetch=1,
            grid=(1,),
            in_specs=[whole(mine), whole(theirs)],
            out_specs=pl.BlockSpec(shape, lambda s, i: (0, 0)),
        ),
        out_shape=in_hbm(shape, F32),
        compiler_params=params(),
        cost_estimate=cost(1000, 1000),
        name="assemble",
    )(info, mine, theirs)


def finish_grad_kernel(gn_ref, r_ref, t_ref, g_ref, gain_ref, o_ref):
    hat, rstd = normalize(t_ref[...])
    u = (gn_ref[...] + r_ref[...].astype(F32)) * gain_ref[...].astype(F32)
    inner = u - jnp.mean(u, axis=1, keepdims=True) - hat * jnp.mean(u * hat, axis=1, keepdims=True)
    o_ref[...] = g_ref[...].astype(F32) + inner * rstd


def finish_grad_call(grad_normed, received, tokens, grads, gain):
    rows, block = tokens.shape[0], 256
    row = pl.BlockSpec((block, D), lambda r: (r, 0))
    return pl.pallas_call(
        finish_grad_kernel,
        grid=(rows // block,),
        in_specs=[row, row, row, row, pl.BlockSpec((1, D), lambda r: (0, 0))],
        out_specs=row,
        out_shape=in_hbm((rows, D), F32),
        compiler_params=params(),
        cost_estimate=cost(20 * rows * D, 14 * rows * D),
        name="finish_grad",
    )(grad_normed, received, tokens, grads, gain)


class Reduction:
    def __init__(self, keep, send, stages, n_dp):
        self.keep, self.sends, self.stages, self.n_dp = keep, [send], list(stages), n_dp
        self.start()

    def start(self):
        offsets = self.stages.pop(0)
        self.flying = [
            lax.ppermute(part, "dp", [(i, i ^ offset) for i in range(self.n_dp)])
            for part, offset in zip(self.sends, offsets, strict=True)
        ]

    def land(self, *first):
        if first:
            self.keep = after(self.keep, *first)
        kind = self.flying[0].dtype
        pieces = self.keep.shape[0]
        count = pieces // (len(self.stages[0]) + 1) if self.stages else pieces
        parts = []
        for i in range(0, pieces, count):
            total = self.keep[i : i + count].astype(F32)
            for part in self.flying:
                total = total + part[i : i + count].astype(F32)
            parts.append(total)
        if not self.stages:
            self.keep, self.sends = parts[0][0], []
            return (self.keep,)
        parts = [part.astype(kind) for part in parts]
        self.keep, self.sends = parts[0], parts[1:]
        self.start()
        return tuple(parts)

    def finish(self, *first):
        self.land(*first)
        while self.sends:
            self.land()
        return self.keep


def after(x, *done):
    return lax.optimization_barrier((x, *done))[0]


def send_order(stages, me):
    table = [0]
    for offsets in stages:
        table = [r ^ offset for r in table for offset in (0, *offsets)]
    return jnp.bitwise_xor(jnp.array(table, jnp.int32), me)


def pairs_of_bits(bits):
    stages = []
    for i in range(0, len(bits), 2):
        if i + 1 < len(bits):
            stages.append((bits[i], bits[i + 1], bits[i] ^ bits[i + 1]))
        else:
            stages.append((bits[i],))
    return stages


def on_device(n_dp, tokens, lengths, norm_gain, norm_shift, qkv_weight, proj_weight, up_weight, inner_bias,
              down_weight, outer_bias, cotangent):
    j = lax.axis_index("branch").astype(jnp.int32)
    me = lax.axis_index("dp").astype(jnp.int32)
    other = [(0, 1), (1, 0)]
    tokens_their = lax.ppermute(tokens, "branch", other)
    cotangent_their = lax.ppermute(cotangent, "branch", other)
    own, their = j.reshape(1), (1 - j).reshape(1)
    info = jnp.stack([j, lengths[0].astype(jnp.int32)])
    gain, shift = norm_gain.reshape(1, D), norm_shift.reshape(1, D)

    bits = [1 << i for i in range(n_dp.bit_length() - 1)]
    high_stages = pairs_of_bits(bits[2:])
    low_first = [(1,), (2,)] + high_stages
    order = send_order(low_first, me)
    ffb = FF_HALF // n_dp
    fast = ffb == LANES
    if fast:
        splits = FB // LANES
        plan = {
            "splits": splits,
            "pieces": n_dp,
            "pick": lambda s, a, i: 2 * (4 * i + a[1][s]) + a[0][0],
            "classes": jnp.array([1, 3, 0, 2], jnp.int32) ^ (me & 3),
            "subs": jnp.arange(4, dtype=jnp.int32) ^ (me >> 2),
            "weights": (up_weight, down_weight, inner_bias.reshape(1, FF)),
        }
    else:
        plan = {
            "splits": 1,
            "pieces": 0,
            "pick": lambda s, a, i: s,
            "classes": jnp.arange(FF_HALF // FB, dtype=jnp.int32),
            "subs": jnp.zeros((1,), jnp.int32),
            "weights": (
                lax.dynamic_index_in_dim(up_weight.reshape(D, n_dp, 2, ffb), j, 2, False).reshape(D, FF_HALF),
                lax.dynamic_index_in_dim(down_weight.reshape(n_dp, 2, ffb, D), j, 1, False).reshape(FF_HALF, D),
                lax.dynamic_index_in_dim(inner_bias.reshape(n_dp, 2, ffb), j, 1, False).reshape(1, FF_HALF),
            ),
        }
    plan["order"] = order

    def pieces_of(grads, table):
        if len(grads) == 2:
            return grads
        whole = grads[0]
        ordered = jnp.take(whole.reshape(n_dp, whole.shape[0] // n_dp, whole.shape[1]), table, axis=0)
        return ordered[: n_dp // 2], ordered[n_dp // 2 :]

    plan["weights"] = tuple(pltpu.with_memory_space_constraint(w, pltpu.HBM) for w in plan["weights"][:2]) + plan["weights"][2:]
    qkv_weight = pltpu.with_memory_space_constraint(qkv_weight, pltpu.HBM)
    proj_weight = pltpu.with_memory_space_constraint(proj_weight, pltpu.HBM)

    cosine, sine = rotary_tables()
    normed, hidden, grads_own, gb_own, expanded_own, gn_own, outer = mlp_own_call(
        info, plan, tokens, cotangent, gain, shift
    )
    qkv = qkv_half_call(own, info, 0, normed, qkv_weight, cosine, sine)
    info = after(info, qkv)
    normed, hidden, slope, expanded_their = mlp_forward_call(info, plan, tokens_their, gain, shift, normed, hidden)
    info = after(info, slope)
    grads, *down = down_grad_call(info, plan, hidden, grads_own, cotangent_their)
    down = Reduction(*pieces_of(down, order), low_first, n_dp)
    info = after(info, grads)
    gn_their, inner, *up = mlp_back_call(info, plan, normed, slope, grads, gb_own)

    up = Reduction(*pieces_of(up, order), low_first, n_dp)
    info = after(info, *down.land(gn_their), *up.land(gn_their))
    qkv = qkv_half_call(their, info, 1, normed, qkv_weight, cosine, sine, qkv)
    context, qe = attend_call(info, qkv)
    out_their = out_call(their, info, context, proj_weight, expanded_their)

    info = after(info, *down.land(out_their))
    out_received = lax.ppermute(out_their, "branch", other)
    grad_context, *proj = proj_back_call(info, plan, order, grads, context, proj_weight)
    info = after(info, *up.land(grad_context))
    dmix = attend_back_call(info, qe, qkv, context, grad_context, cosine, sine)

    down_grad = down.finish(dmix)
    info = after(info, out_received, down_grad)
    small = D // n_dp
    shard = small // 2
    first = qkv_grad_call(info, plan, normed, dmix, 0, 2, proj)
    if not fast:
        first = jnp.concatenate([first[0].reshape(n_dp, small, D), proj[0].reshape(n_dp, shard, D)], axis=1)
        first = jnp.take(first, order, axis=0)
        first = first[: n_dp // 2], first[n_dp // 2 :]
    info = after(info, *first)
    first = Reduction(*first, low_first, n_dp)
    *gn_send, sums_their = grad_normed_call(their, info, dmix, qkv_weight, gn_their, tokens_their, 1)

    info = after(info, *first.land(*gn_send))
    gn_first = lax.ppermute(gn_send[0], "branch", other)
    gn_own, sums_own = grad_normed_call(own, info, dmix, qkv_weight, gn_own, tokens, 0)
    info = after(info, gn_own)
    layer_out = out_call(
        own, info, context, proj_weight, expanded_own, (tokens, out_received, outer_bias.reshape(1, D))
    )
    info = after(info, layer_out)
    if fast:
        value = qkv_grad_call(info, plan, normed, dmix, 2, 1, (sums_own, sums_their, outer, inner))
    else:
        sums = sums_own + sums_their
        lines = jnp.concatenate([v.reshape(n_dp, small) for v in (sums[0], sums[1], outer)], axis=1)
        lines = jnp.concatenate(
            [jnp.pad(lines, ((0, 0), (0, 2 * LANES - 3 * small))), inner.reshape(n_dp, ffb)], axis=1
        )
        lines = jnp.pad(lines, ((0, 0), (0, HALF - lines.shape[1]))).astype(BF)
        lines = jnp.broadcast_to(lines[:, None], (n_dp, 16, HALF))
        value = qkv_grad_call(info, plan, normed, dmix, 2, 1)[0].reshape(n_dp, small, HALF)
        value = jnp.take(jnp.concatenate([value, lines], axis=1), order, axis=0)
        value = value[: n_dp // 2], value[n_dp // 2 :]
    up.finish(*value)
    landed = first.land(*value)
    value, up.keep, _ = lax.optimization_barrier((tuple(value), up.keep, (*landed, gn_first)))
    value = Reduction(*value, low_first, n_dp)
    up_mine = lax.dynamic_slice_in_dim(up.keep, j * shard, shard, 0)
    up_their = lax.dynamic_slice_in_dim(up.keep, (1 - j) * shard, shard, 0).astype(BF)
    up_their = lax.ppermute(up_their, "branch", other)
    landed = value.land()
    tokens_grad = finish_grad_call(gn_own, after(gn_first, *landed), tokens, grads_own, gain)
    up_mine, up_their, tokens_grad = lax.optimization_barrier((up_mine, up_their, tokens_grad))
    if fast:
        sources = tuple(p % 4 * HALF + p // 4 * LANES for p in range(n_dp))
        up_grad = assemble_call(info, up_mine, up_their, sources, LANES)
    else:
        up_their = up_their.astype(F32)
        low, high = jnp.where(j == 0, up_mine, up_their), jnp.where(j == 0, up_their, up_mine)
        up_grad = jnp.stack([low.reshape(shard, n_dp, ffb), high.reshape(shard, n_dp, ffb)], axis=2).reshape(shard, FF)
    first = first.finish(up_grad)
    value.land(first)
    value = value.finish()
    query_key, proj_piece = first[:small], first[small:]
    piece = jnp.concatenate([query_key, value[:small]], axis=1)
    line = value[small:]
    theirs = lax.dynamic_slice_in_dim(piece, (1 - j) * shard, shard, 0)
    theirs = jnp.concatenate([theirs, jnp.concatenate([line, line, line], axis=1)], axis=0).astype(BF)
    route = [(2 * p + h, n_dp * h + p) for h in range(2) for p in range(n_dp)]
    proj_grad = lax.ppermute(after(proj_piece.astype(BF), theirs), ("dp", "branch"), route).astype(F32)
    theirs = lax.ppermute(theirs, "branch", other)
    mine = lax.dynamic_slice_in_dim(piece, j * shard, shard, 0)
    qkv_grad = assemble_call(info, mine, theirs, (0, HALF, 2 * HALF), HALF) if fast else None
    triple = (line[0] + theirs[shard, :HALF].astype(F32))[: 3 * small].reshape(3, 2, shard)
    triple = lax.dynamic_index_in_dim(triple, j, 1, False)
    if not fast:
        mine = mine.reshape(shard, 3, HALF)
        theirs = theirs[:shard].astype(F32).reshape(shard, 3, HALF)
        qkv_grad = jnp.stack([jnp.where(j == 0, mine, theirs), jnp.where(j == 0, theirs, mine)], axis=2)
        qkv_grad = qkv_grad.reshape(shard, 3 * D)
    return (
        layer_out,
        tokens_grad,
        triple[0],
        triple[1],
        qkv_grad,
        proj_grad,
        up_grad,
        line[0, 2 * LANES : 2 * LANES + ffb],
        down_grad,
        triple[2],
    )


def solution(mesh):
    rows = P(("dp", "branch"), None)
    flat = P(("dp", "branch"))
    return jax.shard_map(
        functools.partial(on_device, mesh.shape["dp"]),
        mesh=mesh,
        in_specs=(rows, P("dp"), P(), P(), P(), P(), P(), P(), P(), P(), rows),
        out_specs=(rows, rows, flat, flat, rows, rows, rows, flat, rows, flat),
        check_vma=False,
    )
```

profile of v0, /device:TPU:11, one launch (start us, length us, event | category | flops | bytes accessed | tf_op | source)
XLA Modules:
  0.0 230.6 jit_solution(10536501167985208057)
XLA Ops:
  1.0 1.2 collective-permute-start.1
  5.9 1.2 copy-done.2
  7.1 1.2 copy-done.19
  8.3 19.0 %mlp_own.1 = (bf16[1024,1024]{1,0:T(8,128)(2,1)S(1)}, bf16[1024,2048]{1,0:T(8,128)(2,1)}, bf16[512,1024]{1,0:T(8,128)(2,1)}, bf16[512,2048]{1,0:T(8,128)(2,1)}, ...) custom-call(s32[2]{0:T(128)S(1)} %pad_add_fusion.info_ref, s32[4]{0:T(128)S(1)} %get-tuple-element.169.cls_ref, ...), custom_call_target="tpu_custom_call" | custom-call | flops 8589934 | bytes 14680 | tf_op jit(solution)/shard_map/mlp_own/pallas_call | solution.py:324
  27.5 6.0 %qkv.2.refs_0_ = bf16[3,1024,512]{2,1,0:T(8,128)(2,1)} custom-call(s32[1]{0:T(128)} %bitcast.place_ref, s32[2]{0:T(128)S(1)} %pad_add_fusion.info_ref, bf16[1024,1024]{1,0:T(8,128)(2,1)S(1)} %get-tuple-element.71.x_ref.refs_12_, bf16[1024,3072]{1,0:T(8,128)(2,1)} %wv_ref.3, f32[1024,128]{1,0:T(8,128)S(1)} %bitcast.27, f32[1024,128]{1,0:T(8,128)S(1)} %negate_select_fusion.sin_ref), custom_call_target="tpu_custom_call" | custom-call | flops 1610612 | bytes 5767 | tf_op jit(solution)/shard_map/qkv/pallas_call | solution.py:548
  33.5 13.0 %mlp_forward.1 = (bf16[1024,1024]{1,0:T(8,128)(2,1)S(1)}, bf16[1024,2048]{1,0:T(8,128)(2,1)}, bf16[512,2048]{1,0:T(8,128)(2,1)}, f32[512,1024]{1,0:T(8,128)}) custom-call(s32[2]{0:T(128)S(1)} %pad_add_fusion.info_ref, s32[4]{0:T(128)S(1)} %get-tuple-element.169.cls_ref, ...), custom_call_target="tpu_custom_call", output_to_operand_aliasing={{0}: (17, {}), {1}: (18, {})} | custom-call | flops 4294967 | bytes 14680 | tf_op jit(solution)/shard_map/mlp_forward/pallas_call | solution.py:375
  47.5 2.2 copy-done.4
  49.7 10.4 %down_grad.1 = (bf16[1024,1024]{1,0:T(8,128)(2,1)}, bf16[8,128,1024]{2,1,0:T(8,128)(2,1)}, bf16[8,128,1024]{2,1,0:T(8,128)(2,1)}) custom-call(s32[2]{0:T(128)S(1)} %pad_add_fusion.info_ref, s32[4]{0:T(128)S(1)} %get-tuple-element.169.cls_ref, s32[4]{0:T(128)S(1)} %get-tuple-element.168.sub_ref, bf16[1024,2048]{1,0:T(8,128)(2,1)S(1)} %copy-done.4, ...), custom_call_target="tpu_custom_call" | custom-call | flops 4294967 | bytes 12582 | tf_op jit(solution)/shard_map/down_grad/pallas_call | solution.py:446
  60.1 1.5 collective-permute-start.2
  61.7 1.6 copy-done.7
  63.3 15.4 %mlp_back.1 = (f32[512,1024]{1,0:T(8,128)}, f32[1,2048]{1,0:T(1,128)S(1)}, bf16[8,64,2048]{2,1,0:T(8,128)(2,1)}, bf16[8,64,2048]{2,1,0:T(8,128)(2,1)}) custom-call(s32[2]{0:T(128)S(1)} %pad_add_fusion.info_ref, s32[4]{0:T(128)S(1)} %get-tuple-element.169.cls_ref, s32[16]{0:T(128)S(1)} %broadcast_xor_fusion.ord_ref, ...), custom_call_target="tpu_custom_call" | custom-call | flops 8589934 | bytes 23068 | tf_op jit(solution)/shard_map/mlp_back/pallas_call | solution.py:501
  78.7 2.3 %add_convert_fusion.2 = (bf16[4,128,1024]{2,1,0:T(8,128)(2,1)}, bf16[4,128,1024]{2,1,0:T(8,128)(2,1)}) fusion(bf16[8,128,1024]{2,1,0:T(8,128)(2,1)S(1)} %collective-permute-done.2, bf16[8,128,1024]{2,1,0:T(8,128)(2,1)S(1)} %copy-done.27), kind=kLoop, calls=%fused_computation.2 | loop fusion | flops 4194304 | bytes 6291456 | tf_op jit(solution)/shard_map/convert_element_type | solution.py:861
  81.1 1.2 collective-permute-start.4
  83.1 2.1 add_convert_fusion
  85.2 1.2 collective-permute-start.5
  86.4 5.9 %qkv.3.q_ref.k_ref.v_ref = bf16[3,1024,512]{2,1,0:T(8,128)(2,1)} custom-call(s32[1]{0:T(128)} %bitcast.3.place_ref, s32[2]{0:T(128)S(1)} %pad_add_fusion.info_ref, bf16[1024,1024]{1,0:T(8,128)(2,1)S(1)} %get-tuple-element.83.x_ref, bf16[1024,3072]{1,0:T(8,128)(2,1)} %wv_ref.3, f32[1024,128]{1,0:T(8,128)S(1)} %bitcast.28, ...), custom_call_target="tpu_custom_call", output_to_operand_aliasing={{}: (6, {})} | custom-call | flops 1610612 | bytes 5767 | tf_op jit(solution)/shard_map/qkv/pallas_call | solution.py:548
  92.3 1.9 copy-done
  94.2 17.0 %attend.1 = (bf16[1024,512]{1,0:T(8,128)(2,1)}, bf16[8,1024,128]{2,1,0:T(8,128)(2,1)}) custom-call(s32[2]{0:T(128)S(1)} %pad_add_fusion.info_ref, bf16[3,1024,512]{2,1,0:T(8,128)(2,1)S(1)} %copy-done, bf16[3,1024,512]{2,1,0:T(8,128)(2,1)S(1)} %copy-done, bf16[3,1024,512]{2,1,0:T(8,128)(2,1)S(1)} %copy-done), custom_call_target="tpu_custom_call" | custom-call | flops 10737418 | bytes 3145 | tf_op jit(solution)/shard_map/attend/pallas_call | solution.py:141
  111.2 1.2 copy-done.5
  112.5 3.5 %send_out.1 = bf16[512,1024]{1,0:T(8,128)(2,1)} custom-call(s32[1]{0:T(128)} %bitcast.3.place_ref, s32[2]{0:T(128)S(1)} %pad_add_fusion.info_ref, bf16[1024,512]{1,0:T(8,128)(2,1)S(1)} %copy-done.5, bf16[1024,1024]{1,0:T(8,128)(2,1)} %w_ref.9, f32[512,1024]{1,0:T(8,128)S(1)} %copy-done.16), custom_call_target="tpu_custom_call" | custom-call | flops 536870 | bytes 5242 | tf_op jit(solution)/shard_map/send_out/pallas_call | solution.py:583
  116.3 1.8 add_convert_fusion.12
  118.1 1.3 collective-permute-start.9
  121.6 6.3 %proj_back.1 = (bf16[1024,512]{1,0:T(8,128)(2,1)}, bf16[8,32,1024]{2,1,0:T(8,128)(2,1)}, bf16[8,32,1024]{2,1,0:T(8,128)(2,1)}) custom-call(s32[2]{0:T(128)S(1)} %pad_add_fusion.info_ref, s32[16]{0:T(128)S(1)} %broadcast_xor_fusion.ord_ref, bf16[1024,1024]{1,0:T(8,128)(2,1)S(1)} %copy-done.8, bf16[1024,512]{1,0:T(8,128)(2,1)S(1)} %copy-done.6, ...), custom_call_target="tpu_custom_call" | custom-call | flops 2147483 | bytes 6291 | tf_op jit(solution)/shard_map/proj_back/pallas_call | solution.py:637
  128.1 1.7 add_convert_fusion.8
  130.2 1.2 copy-done.22
  131.4 19.6 %attend_back.1.own_ref.their_ref.d_ref = bf16[3,1024,512]{2,1,0:T(8,128)(2,1)S(1)} custom-call(s32[2]{0:T(128)S(1)} %pad_add_fusion.info_ref, bf16[8,1024,128]{2,1,0:T(8,128)(2,1)S(1)} %copy-done.18, bf16[3,1024,512]{2,1,0:T(8,128)(2,1)S(1)} %copy-done.1, bf16[3,1024,512]{2,1,0:T(8,128)(2,1)S(1)} %copy-done.1, bf16[1024,512]{1,0:T(8,128)(2,1)S(1)} %copy-done.6, ...), custom_call_target="tpu_custom_call" | custom-call | flops 12884901 | bytes 4194 | tf_op jit(solution)/shard_map/attend_back/pallas_call | solution.py:217
  152.0 4.5 %qkv_grad.2 = (bf16[8,96,1024]{2,1,0:T(8,128)(2,1)}, bf16[8,96,1024]{2,1,0:T(8,128)(2,1)}) custom-call(s32[2]{0:T(128)S(1)} %pad_add_fusion.info_ref, s32[16]{0:T(128)S(1)} %broadcast_xor_fusion.ord_ref, bf16[1024,1024]{1,0:T(8,128)(2,1)S(1)} %get-tuple-element.83.x_ref, bf16[3,1024,512]{2,1,0:T(8,128)(2,1)S(1)} %attend_back.1.own_ref.their_ref.d_ref, ...), custom_call_target="tpu_custom_call" | custom-call | flops 2147483 | bytes 6291 | tf_op jit(solution)/shard_map/qkv_grad/pallas_call | solution.py:720
  156.5 1.4 collective-permute-start.10
  157.9 5.8 %grad_normed.2 = (bf16[512,1024]{1,0:T(8,128)(2,1)}, f32[2,1024]{1,0:T(2,128)S(1)}) custom-call(s32[1]{0:T(128)} %bitcast.3.place_ref, s32[2]{0:T(128)S(1)} %pad_add_fusion.info_ref, bf16[3,1024,512]{2,1,0:T(8,128)(2,1)S(1)} %attend_back.1.own_ref.their_ref.d_ref, bf16[1024,3072]{1,0:T(8,128)(2,1)} %wv_ref.3, bf16[1024,3072]{1,0:T(8,128)(2,1)} %wv_ref.3, ...), custom_call_target="tpu_custom_call" | custom-call | flops 1610612 | bytes 8912 | tf_op jit(solution)/shard_map/grad_normed/pallas_call | solution.py:766
  165.7 1.3 collective-permute-start.13
  167.0 1.2 collective-permute-start.12
  169.4 5.7 %grad_normed.3 = (f32[512,1024]{1,0:T(8,128)}, f32[2,1024]{1,0:T(2,128)S(1)}) custom-call(s32[1]{0:T(128)} %bitcast.place_ref, s32[2]{0:T(128)S(1)} %pad_add_fusion.info_ref, bf16[3,1024,512]{2,1,0:T(8,128)(2,1)S(1)} %attend_back.1.own_ref.their_ref.d_ref, bf16[1024,3072]{1,0:T(8,128)(2,1)} %wv_ref.3, bf16[1024,3072]{1,0:T(8,128)(2,1)} %wv_ref.3, ...), custom_call_target="tpu_custom_call" | custom-call | flops 1610612 | bytes 8912 | tf_op jit(solution)/shard_map/grad_normed/pallas_call | solution.py:766
  175.1 3.6 %finish_out.1 = bf16[512,1024]{1,0:T(8,128)(2,1)} custom-call(s32[1]{0:T(128)} %bitcast.place_ref, s32[2]{0:T(128)S(1)} %pad_add_fusion.info_ref, bf16[1024,512]{1,0:T(8,128)(2,1)S(1)} %copy-done.6, bf16[1024,1024]{1,0:T(8,128)(2,1)} %w_ref.9, f32[512,1024]{1,0:T(8,128)S(1)} %copy-done.17, bf16[512,1024]{1,0:T(8,128)(2,1)S(1)} %copy-done.3, ...), custom_call_target="tpu_custom_call" | custom-call | flops 536870 | bytes 5242 | tf_op jit(solution)/shard_map/finish_out/pallas_call | solution.py:583
  178.8 2.9 %qkv_grad.3 = (bf16[8,80,512]{2,1,0:T(8,128)(2,1)}, bf16[8,80,512]{2,1,0:T(8,128)(2,1)}) custom-call(s32[2]{0:T(128)S(1)} %pad_add_fusion.info_ref, s32[16]{0:T(128)S(1)} %broadcast_xor_fusion.ord_ref, bf16[1024,1024]{1,0:T(8,128)(2,1)S(1)} %get-tuple-element.83.x_ref, bf16[3,1024,512]{2,1,0:T(8,128)(2,1)S(1)} %attend_back.1.own_ref.their_ref.d_ref, ...), custom_call_target="tpu_custom_call" | custom-call | flops 1073741 | bytes 4194 | tf_op jit(solution)/shard_map/qkv_grad/pallas_call | solution.py:720
  181.7 2.5 %collective-permute-done.13 = bf16[1,64,2048]{2,1,0:T(8,128)(2,1)S(1)} collective-permute-done((bf16[1,64,2048]{2,1,0:T(8,128)(2,1)S(1)}, bf16[1,64,2048]{2,1,0:T(8,128)(2,1)S(1)}, u32[]{:S(2)}, u32[]{:S(2)}) %collective-permute-start.13) | collective-permute-done | bytes 262176 | tf_op jit(solution)/shard_map/ppermute | solution.py:842
  184.2 4.8 %collective-permute-done.12 = bf16[1,64,2048]{2,1,0:T(8,128)(2,1)S(1)} collective-permute-done((bf16[1,64,2048]{2,1,0:T(8,128)(2,1)S(1)}, bf16[1,64,2048]{2,1,0:T(8,128)(2,1)S(1)}, u32[]{:S(2)}, u32[]{:S(2)}) %collective-permute-start.12) | collective-permute-done | bytes 262176 | tf_op jit(solution)/shard_map/ppermute | solution.py:842
  191.1 1.4 collective-permute-start.17
  192.7 4.0 %collective-permute-start.23 = (bf16[1,96,1024]{2,1,0:T(8,128)(2,1)S(1)}, bf16[1,96,1024]{2,1,0:T(8,128)(2,1)S(1)}, u32[]{:S(2)}, u32[]{:S(2)}) collective-permute-start(bf16[1,96,1024]{2,1,0:T(8,128)(2,1)S(1)} %get-tuple-element.147), channel_id=1, source_target_pairs={{0,16},{2,18},{4,20},{6,22},{8,24},{10,26},{12,28},{14,30},{16,0},... | collective-permute-start | bytes 589832 | tf_op jit(solution)/shard_map/ppermute | solution.py:842
  197.9 1.4 add_convert_fusion.6
  200.1 1.2 copy-done.21
  201.4 2.5 %finish_grad.1 = f32[512,1024]{1,0:T(8,128)} custom-call(f32[512,1024]{1,0:T(8,128)S(1)} %copy-done.13, bf16[512,1024]{1,0:T(8,128)(2,1)S(1)} %copy-done.21, bf16[512,1024]{1,0:T(8,128)(2,1)S(1)} %copy-done.3, bf16[512,1024]{1,0:T(8,128)(2,1)S(1)} %copy-done.10, bf16[1,1024]{1,0:T(2,128)(2,1)S(1)} %reshape.129.gain_ref), custom_call_target="tpu_custom_call" | custom-call | flops 10485 | bytes 7340 | tf_op jit(solution)/shard_map/finish_grad/pallas_call | solution.py:822
  203.8 1.4 assemble.2
  205.2 2.5 %collective-permute-done.24 = bf16[1,96,1024]{2,1,0:T(8,128)(2,1)S(1)} collective-permute-done((bf16[1,96,1024]{2,1,0:T(8,128)(2,1)}, bf16[1,96,1024]{2,1,0:T(8,128)(2,1)S(1)}, u32[]{:S(2)}, u32[]{:S(2)}) %collective-permute-start.24) | collective-permute-done | bytes 196640 | tf_op jit(solution)/shard_map/ppermute | solution.py:842
  207.7 2.2 collective-permute-done.23
  211.5 4.0 %collective-permute-start.20 = (bf16[1,80,512]{2,1,0:T(8,128)(2,1)S(1)}, bf16[1,80,512]{2,1,0:T(8,128)(2,1)S(1)}, u32[]{:S(2)}, u32[]{:S(2)}) collective-permute-start(bf16[1,80,512]{2,1,0:T(8,128)(2,1)S(1)} %get-tuple-element.154), channel_id=1, source_target_pairs={{0,16},{2,18},{4,20},{6,22},{8,24},{10,26},{12,28},{14,30},{16,0},... | collective-permute-start | bytes 245768 | tf_op jit(solution)/shard_map/ppermute | solution.py:842
  215.5 4.2 %collective-permute-done.20 = bf16[1,80,512]{2,1,0:T(8,128)(2,1)S(1)} collective-permute-done((bf16[1,80,512]{2,1,0:T(8,128)(2,1)S(1)}, bf16[1,80,512]{2,1,0:T(8,128)(2,1)S(1)}, u32[]{:S(2)}, u32[]{:S(2)}) %collective-permute-start.20) | collective-permute-done | bytes 81952 | tf_op jit(solution)/shard_map/ppermute | solution.py:842
  221.2 5.2 %collective-permute-start.26 = (bf16[32,1024]{1,0:T(8,128)(2,1)S(1)}, bf16[32,1024]{1,0:T(8,128)(2,1)S(1)}, u32[]{:S(2)}, u32[]{:S(2)}) collective-permute-start(bf16[32,1024]{1,0:T(8,128)(2,1)S(1)} %fusion.3), channel_id=1, source_target_pairs={{0,0},{2,1},{4,2},{6,3},{8,4},{10,5},{12,6},{14,7},{16,8},{18,9},{... | collective-permute-start | bytes 196616 | tf_op jit(solution)/shard_map/ppermute | solution.py:1032
  229.3 1.3 assemble.3
  (134 shorter events, 22.8 us)
Async XLA Ops:
  0.6 32.9 %collective-permute-start = (bf16[512,1024]{1,0:T(8,128)(2,1)}, bf16[512,1024]{1,0:T(8,128)(2,1)}, u32[]{:S(2)}, u32[]{:S(2)}) collective-permute-start(bf16[512,1024]{1,0:T(8,128)(2,1)} %t_ref.7), channel_id=1, source_target_pairs={{0,1},{1,0},{2,3},{3,2},{4,5},{5,4},{6,7},{7,6},{8,9},{9,8},{10,11... | collective-permute-start | bytes 3145736 | tf_op jit(solution)/shard_map/ppermute | solution.py:899
  1.0 46.6 %collective-permute-start.1 = (bf16[512,1024]{1,0:T(8,128)(2,1)}, bf16[512,1024]{1,0:T(8,128)(2,1)}, u32[]{:S(2)}, u32[]{:S(2)}) collective-permute-start(bf16[512,1024]{1,0:T(8,128)(2,1)} %c_ref.1), channel_id=1, source_target_pairs={{0,1},{1,0},{2,3},{3,2},{4,5},{5,4},{6,7},{7,6},{8,9},{9,8},{10,11... | collective-permute-start | bytes 3145736 | tf_op jit(solution)/shard_map/ppermute | solution.py:900
  33.5 14.0 %copy-start.9 = (bf16[512,1024]{1,0:T(8,128)(2,1)S(1)}, bf16[512,1024]{1,0:T(8,128)(2,1)}, u32[]{:S(2)}) copy-start(bf16[512,1024]{1,0:T(8,128)(2,1)} %get-tuple-element.79.go_ref.g_ref) | copy-start | bytes 3145732
  49.7 11.9 %copy-start.31 = (s32[16]{0:T(128)S(1)}, s32[16]{0:T(128)}, u32[]{:S(2)}) copy-start(s32[16]{0:T(128)} %constant.75.clone) | copy-start | bytes 196
  49.7 11.9 %copy-start.14 = (bf16[512,2048]{1,0:T(8,128)(2,1)S(1)}, bf16[512,2048]{1,0:T(8,128)(2,1)}, u32[]{:S(2)}) copy-start(bf16[512,2048]{1,0:T(8,128)(2,1)} %get-tuple-element.84.gb_ref) | copy-start | bytes 6291460
  49.7 11.9 %copy-start.15 = (bf16[512,2048]{1,0:T(8,128)(2,1)S(1)}, bf16[512,2048]{1,0:T(8,128)(2,1)}, u32[]{:S(2)}) copy-start(bf16[512,2048]{1,0:T(8,128)(2,1)} %get-tuple-element.76.slope_ref) | copy-start | bytes 6291460
  60.1 18.6 %collective-permute-start.2 = (bf16[8,128,1024]{2,1,0:T(8,128)(2,1)}, bf16[8,128,1024]{2,1,0:T(8,128)(2,1)S(1)}, u32[]{:S(2)}, u32[]{:S(2)}) collective-permute-start(bf16[8,128,1024]{2,1,0:T(8,128)(2,1)} %get-tuple-element.87), channel_id=1, source_target_pairs={{0,2},{2,0},{4,6},{6,4},{8,10},{10,8},{12,14},{14,12},{16,18},{18,... | collective-permute-start | bytes 6291464 | tf_op jit(solution)/shard_map/ppermute | solution.py:842
  63.3 15.5 %copy-start.27 = (bf16[8,128,1024]{2,1,0:T(8,128)(2,1)S(1)}, bf16[8,128,1024]{2,1,0:T(8,128)(2,1)}, u32[]{:S(2)}) copy-start(bf16[8,128,1024]{2,1,0:T(8,128)(2,1)} %get-tuple-element.86) | copy-start | bytes 6291460
  78.6 4.4 %collective-permute-start.3 = (bf16[8,64,2048]{2,1,0:T(8,128)(2,1)}, bf16[8,64,2048]{2,1,0:T(8,128)(2,1)S(1)}, u32[]{:S(2)}, u32[]{:S(2)}) collective-permute-start(bf16[8,64,2048]{2,1,0:T(8,128)(2,1)} %get-tuple-element.90), channel_id=1, source_target_pairs={{0,2},{2,0},{4,6},{6,4},{8,10},{10,8},{12,14},{14,12},{16,18},{18,... | collective-permute-start | bytes 6291464 | tf_op jit(solution)/shard_map/ppermute | solution.py:842
  78.7 4.3 %copy-start.28 = (bf16[8,64,2048]{2,1,0:T(8,128)(2,1)S(1)}, bf16[8,64,2048]{2,1,0:T(8,128)(2,1)}, u32[]{:S(2)}) copy-start(bf16[8,64,2048]{2,1,0:T(8,128)(2,1)} %get-tuple-element.89) | copy-start | bytes 6291460
  81.1 35.3 %collective-permute-start.4 = (bf16[4,128,1024]{2,1,0:T(8,128)(2,1)}, bf16[4,128,1024]{2,1,0:T(8,128)(2,1)}, u32[]{:S(2)}, u32[]{:S(2)}) collective-permute-start(bf16[4,128,1024]{2,1,0:T(8,128)(2,1)} %get-tuple-element.134), channel_id=1, source_target_pairs={{0,4},{2,6},{4,0},{6,2},{8,12},{10,14},{12,8},{14,10},{16,20},{18,... | collective-permute-start | bytes 3145736 | tf_op jit(solution)/shard_map/ppermute | solution.py:842
  85.2 42.9 %collective-permute-start.5 = (bf16[4,64,2048]{2,1,0:T(8,128)(2,1)}, bf16[4,64,2048]{2,1,0:T(8,128)(2,1)}, u32[]{:S(2)}, u32[]{:S(2)}) collective-permute-start(bf16[4,64,2048]{2,1,0:T(8,128)(2,1)} %get-tuple-element.132), channel_id=1, source_target_pairs={{0,4},{2,6},{4,0},{6,2},{8,12},{10,14},{12,8},{14,10},{16,20},{18,... | collective-permute-start | bytes 3145736 | tf_op jit(solution)/shard_map/ppermute | solution.py:842
  94.2 17.0 %copy-start.16 = (f32[512,1024]{1,0:T(8,128)S(1)}, f32[512,1024]{1,0:T(8,128)}, u32[]{:S(2)}) copy-start(f32[512,1024]{1,0:T(8,128)} %get-tuple-element.93.e_ref) | copy-start | bytes 6291460
  116.0 5.6 %copy-start.6 = (bf16[1024,512]{1,0:T(8,128)(2,1)S(1)}, bf16[1024,512]{1,0:T(8,128)(2,1)}, u32[]{:S(2)}) copy-start(bf16[1024,512]{1,0:T(8,128)(2,1)} %get-tuple-element.92.c_ref.o_ref) | copy-start | bytes 3145732
  116.0 5.6 %copy-start.8 = (bf16[1024,1024]{1,0:T(8,128)(2,1)S(1)}, bf16[1024,1024]{1,0:T(8,128)(2,1)}, u32[]{:S(2)}) copy-start(bf16[1024,1024]{1,0:T(8,128)(2,1)} %get-tuple-element.80.g_ref) | copy-start | bytes 6291460
  116.0 36.0 %collective-permute-start.6 = (bf16[512,1024]{1,0:T(8,128)(2,1)}, bf16[512,1024]{1,0:T(8,128)(2,1)S(1)}, u32[]{:S(2)}, u32[]{:S(2)}) collective-permute-start(bf16[512,1024]{1,0:T(8,128)(2,1)} %send_out.1), channel_id=1, source_target_pairs={{0,1},{1,0},{2,3},{3,2},{4,5},{5,4},{6,7},{7,6},{8,9},{9,8},{10,11... | collective-permute-start | bytes 3145736 | tf_op jit(solution)/shard_map/ppermute | solution.py:967
  118.1 32.8 %collective-permute-start.9 = (bf16[1,128,1024]{2,1,0:T(8,128)(2,1)S(1)}, bf16[1,128,1024]{2,1,0:T(8,128)(2,1)S(1)}, u32[]{:S(2)}, u32[]{:S(2)}) collective-permute-start(bf16[1,128,1024]{2,1,0:T(8,128)(2,1)S(1)} %get-tuple-element.142), channel_id=1, source_target_pairs={{0,24},{2,26},{4,28},{6,30},{8,16},{10,18},{12,20},{14,22},{16,8},... | collective-permute-start | bytes 786440 | tf_op jit(solution)/shard_map/ppermute | solution.py:842
  119.5 31.5 %collective-permute-start.8 = (bf16[1,128,1024]{2,1,0:T(8,128)(2,1)S(1)}, bf16[1,128,1024]{2,1,0:T(8,128)(2,1)S(1)}, u32[]{:S(2)}, u32[]{:S(2)}) collective-permute-start(bf16[1,128,1024]{2,1,0:T(8,128)(2,1)S(1)} %get-tuple-element.143), channel_id=1, source_target_pairs={{0,16},{2,18},{4,20},{6,22},{8,24},{10,26},{12,28},{14,30},{16,0},... | collective-permute-start | bytes 786440 | tf_op jit(solution)/shard_map/ppermute | solution.py:842
  120.5 30.5 %collective-permute-start.7 = (bf16[1,128,1024]{2,1,0:T(8,128)(2,1)S(1)}, bf16[1,128,1024]{2,1,0:T(8,128)(2,1)S(1)}, u32[]{:S(2)}, u32[]{:S(2)}) collective-permute-start(bf16[1,128,1024]{2,1,0:T(8,128)(2,1)S(1)} %get-tuple-element.144), channel_id=1, source_target_pairs={{0,8},{2,10},{4,12},{6,14},{8,0},{10,2},{12,4},{14,6},{16,24},{18,... | collective-permute-start | bytes 786440 | tf_op jit(solution)/shard_map/ppermute | solution.py:842
  121.6 6.5 %copy-start.25 = (bf16[4,64,2048]{2,1,0:T(8,128)(2,1)S(1)}, bf16[4,64,2048]{2,1,0:T(8,128)(2,1)}, u32[]{:S(2)}) copy-start(bf16[4,64,2048]{2,1,0:T(8,128)(2,1)} %get-tuple-element.97) | copy-start | bytes 3145732
  121.6 8.2 %copy-start.18 = (bf16[8,1024,128]{2,1,0:T(8,128)(2,1)S(1)}, bf16[8,1024,128]{2,1,0:T(8,128)(2,1)}, u32[]{:S(2)}) copy-start(bf16[8,1024,128]{2,1,0:T(8,128)(2,1)} %get-tuple-element.99.qe_ref) | copy-start | bytes 6291460
  131.4 20.6 %copy-start.23 = (bf16[8,32,1024]{2,1,0:T(8,128)(2,1)S(1)}, bf16[8,32,1024]{2,1,0:T(8,128)(2,1)}, u32[]{:S(2)}) copy-start(bf16[8,32,1024]{2,1,0:T(8,128)(2,1)} %get-tuple-element.102.refs_0_) | copy-start | bytes 1572868
  131.4 20.6 %copy-start.24 = (bf16[8,32,1024]{2,1,0:T(8,128)(2,1)S(1)}, bf16[8,32,1024]{2,1,0:T(8,128)(2,1)}, u32[]{:S(2)}) copy-start(bf16[8,32,1024]{2,1,0:T(8,128)(2,1)} %get-tuple-element.103.refs_1_) | copy-start | bytes 1572868
  152.0 5.9 %copy-start.12 = (f32[512,1024]{1,0:T(8,128)S(1)}, f32[512,1024]{1,0:T(8,128)}, u32[]{:S(2)}) copy-start(f32[512,1024]{1,0:T(8,128)} %get-tuple-element.85.base_ref) | copy-start | bytes 6291460
  156.5 8.1 %collective-permute-start.10 = (bf16[8,96,1024]{2,1,0:T(8,128)(2,1)}, bf16[8,96,1024]{2,1,0:T(8,128)(2,1)S(1)}, u32[]{:S(2)}, u32[]{:S(2)}) collective-permute-start(bf16[8,96,1024]{2,1,0:T(8,128)(2,1)} %get-tuple-element.105), channel_id=1, source_target_pairs={{0,2},{2,0},{4,6},{6,4},{8,10},{10,8},{12,14},{14,12},{16,18},{18,... | collective-permute-start | bytes 4718600 | tf_op jit(solution)/shard_map/ppermute | solution.py:842
  157.9 6.7 %copy-start.29 = (bf16[8,96,1024]{2,1,0:T(8,128)(2,1)S(1)}, bf16[8,96,1024]{2,1,0:T(8,128)(2,1)}, u32[]{:S(2)}) copy-start(bf16[8,96,1024]{2,1,0:T(8,128)(2,1)} %get-tuple-element.108) | copy-start | bytes 4718596
  163.7 5.7 %copy-start.30 = (bf16[1024]{0:T(1024)(128)(2,1)S(1)}, bf16[1024]{0:T(1024)(128)(2,1)}, u32[]{:S(2)}) copy-start(bf16[1024]{0:T(1024)(128)(2,1)} %param.22) | copy-start | bytes 6148
  163.7 5.7 %copy-start.3 = (bf16[512,1024]{1,0:T(8,128)(2,1)S(1)}, bf16[512,1024]{1,0:T(8,128)(2,1)}, u32[]{:S(2)}) copy-start(bf16[512,1024]{1,0:T(8,128)(2,1)} %t_ref.7) | copy-start | bytes 3145732
  163.7 5.7 %copy-start.11 = (f32[512,1024]{1,0:T(8,128)S(1)}, f32[512,1024]{1,0:T(8,128)}, u32[]{:S(2)}) copy-start(f32[512,1024]{1,0:T(8,128)} %get-tuple-element.110.base_ref) | copy-start | bytes 6291460
  163.7 26.4 %collective-permute-start.15 = (bf16[512,1024]{1,0:T(8,128)(2,1)}, bf16[512,1024]{1,0:T(8,128)(2,1)S(1)}, u32[]{:S(2)}, u32[]{:S(2)}) collective-permute-start(bf16[512,1024]{1,0:T(8,128)(2,1)} %get-tuple-element.107), channel_id=1, source_target_pairs={{0,1},{1,0},{2,3},{3,2},{4,5},{5,4},{6,7},{7,6},{8,9},{9,8},{10,11... | collective-permute-start | bytes 3145736 | tf_op jit(solution)/shard_map/ppermute | solution.py:986
  165.3 23.8 %collective-permute-start.14 = (bf16[4,96,1024]{2,1,0:T(8,128)(2,1)S(1)}, bf16[4,96,1024]{2,1,0:T(8,128)(2,1)S(1)}, u32[]{:S(2)}, u32[]{:S(2)}) collective-permute-start(bf16[4,96,1024]{2,1,0:T(8,128)(2,1)S(1)} %get-tuple-element.136), channel_id=1, source_target_pairs={{0,4},{2,6},{4,0},{6,2},{8,12},{10,14},{12,8},{14,10},{16,20},{18,... | collective-permute-start | bytes 2359304 | tf_op jit(solution)/shard_map/ppermute | solution.py:842
  165.7 18.5 %collective-permute-start.13 = (bf16[1,64,2048]{2,1,0:T(8,128)(2,1)S(1)}, bf16[1,64,2048]{2,1,0:T(8,128)(2,1)S(1)}, u32[]{:S(2)}, u32[]{:S(2)}) collective-permute-start(bf16[1,64,2048]{2,1,0:T(8,128)(2,1)S(1)} %get-tuple-element.138), channel_id=1, source_target_pairs={{0,24},{2,26},{4,28},{6,30},{8,16},{10,18},{12,20},{14,22},{16,8},... | collective-permute-start | bytes 786440 | tf_op jit(solution)/shard_map/ppermute | solution.py:842
  167.0 21.9 %collective-permute-start.12 = (bf16[1,64,2048]{2,1,0:T(8,128)(2,1)S(1)}, bf16[1,64,2048]{2,1,0:T(8,128)(2,1)S(1)}, u32[]{:S(2)}, u32[]{:S(2)}) collective-permute-start(bf16[1,64,2048]{2,1,0:T(8,128)(2,1)S(1)} %get-tuple-element.139), channel_id=1, source_target_pairs={{0,16},{2,18},{4,20},{6,22},{8,24},{10,26},{12,28},{14,30},{16,0},... | collective-permute-start | bytes 786440 | tf_op jit(solution)/shard_map/ppermute | solution.py:842
  168.2 20.7 %collective-permute-start.11 = (bf16[1,64,2048]{2,1,0:T(8,128)(2,1)S(1)}, bf16[1,64,2048]{2,1,0:T(8,128)(2,1)S(1)}, u32[]{:S(2)}, u32[]{:S(2)}) collective-permute-start(bf16[1,64,2048]{2,1,0:T(8,128)(2,1)S(1)} %get-tuple-element.140), channel_id=1, source_target_pairs={{0,8},{2,10},{4,12},{6,14},{8,0},{10,2},{12,4},{14,6},{16,24},{18,... | collective-permute-start | bytes 786440 | tf_op jit(solution)/shard_map/ppermute | solution.py:842
  169.4 5.7 %copy-start.17 = (f32[512,1024]{1,0:T(8,128)S(1)}, f32[512,1024]{1,0:T(8,128)}, u32[]{:S(2)}) copy-start(f32[512,1024]{1,0:T(8,128)} %get-tuple-element.113.e_ref) | copy-start | bytes 6291460
  189.1 11.1 %copy-start.10 = (bf16[512,1024]{1,0:T(8,128)(2,1)S(1)}, bf16[512,1024]{1,0:T(8,128)(2,1)}, u32[]{:S(2)}) copy-start(bf16[512,1024]{1,0:T(8,128)(2,1)} %get-tuple-element.79.go_ref.g_ref) | copy-start | bytes 3145732
  191.1 6.8 %collective-permute-start.17 = (bf16[8,80,512]{2,1,0:T(8,128)(2,1)}, bf16[8,80,512]{2,1,0:T(8,128)(2,1)}, u32[]{:S(2)}, u32[]{:S(2)}) collective-permute-start(bf16[8,80,512]{2,1,0:T(8,128)(2,1)} %get-tuple-element.125), channel_id=1, source_target_pairs={{0,2},{2,0},{4,6},{6,4},{8,10},{10,8},{12,14},{14,12},{16,18},{18,... | collective-permute-start | bytes 1966088 | tf_op jit(solution)/shard_map/ppermute | solution.py:842
  192.5 7.6 %copy-start.13 = (f32[512,1024]{1,0:T(8,128)S(1)}, f32[512,1024]{1,0:T(8,128)}, u32[]{:S(2)}) copy-start(f32[512,1024]{1,0:T(8,128)} %get-tuple-element.111.gn_ref) | copy-start | bytes 6291460
  192.5 15.2 %collective-permute-start.24 = (bf16[1,96,1024]{2,1,0:T(8,128)(2,1)}, bf16[1,96,1024]{2,1,0:T(8,128)(2,1)S(1)}, u32[]{:S(2)}, u32[]{:S(2)}) collective-permute-start(bf16[1,96,1024]{2,1,0:T(8,128)(2,1)} %get-tuple-element.146), channel_id=1, source_target_pairs={{0,24},{2,26},{4,28},{6,30},{8,16},{10,18},{12,20},{14,22},{16,8},... | collective-permute-start | bytes 589832 | tf_op jit(solution)/shard_map/ppermute | solution.py:842
  192.7 17.2 %collective-permute-start.23 = (bf16[1,96,1024]{2,1,0:T(8,128)(2,1)S(1)}, bf16[1,96,1024]{2,1,0:T(8,128)(2,1)S(1)}, u32[]{:S(2)}, u32[]{:S(2)}) collective-permute-start(bf16[1,96,1024]{2,1,0:T(8,128)(2,1)S(1)} %get-tuple-element.147), channel_id=1, source_target_pairs={{0,16},{2,18},{4,20},{6,22},{8,24},{10,26},{12,28},{14,30},{16,0},... | collective-permute-start | bytes 589832 | tf_op jit(solution)/shard_map/ppermute | solution.py:842
  196.7 13.9 %collective-permute-start.22 = (bf16[1,96,1024]{2,1,0:T(8,128)(2,1)S(1)}, bf16[1,96,1024]{2,1,0:T(8,128)(2,1)S(1)}, u32[]{:S(2)}, u32[]{:S(2)}) collective-permute-start(bf16[1,96,1024]{2,1,0:T(8,128)(2,1)S(1)} %get-tuple-element.148), channel_id=1, source_target_pairs={{0,8},{2,10},{4,12},{6,14},{8,0},{10,2},{12,4},{14,6},{16,24},{18,... | collective-permute-start | bytes 589832 | tf_op jit(solution)/shard_map/ppermute | solution.py:842
  196.8 7.0 %collective-permute-start.16 = (bf16[32,2048]{1,0:T(8,128)(2,1)S(1)}, bf16[32,2048]{1,0:T(8,128)(2,1)S(1)}, u32[]{:S(2)}, u32[]{:S(2)}) collective-permute-start(bf16[32,2048]{1,0:T(8,128)(2,1)S(1)} %dynamic-slice_convert_fusion), channel_id=1, source_target_pairs={{0,1},{1,0},{2,3},{3,2},{4,5},{5,4},{6,7},{7,6},{8,9},{9,8},{10,11... | collective-permute-start | bytes 393224 | tf_op jit(solution)/shard_map/ppermute | solution.py:1012
  199.4 11.4 %collective-permute-start.18 = (bf16[4,80,512]{2,1,0:T(8,128)(2,1)S(1)}, bf16[4,80,512]{2,1,0:T(8,128)(2,1)S(1)}, u32[]{:S(2)}, u32[]{:S(2)}) collective-permute-start(bf16[4,80,512]{2,1,0:T(8,128)(2,1)S(1)} %get-tuple-element.150), channel_id=1, source_target_pairs={{0,4},{2,6},{4,0},{6,2},{8,12},{10,14},{12,8},{14,10},{16,20},{18,... | collective-permute-start | bytes 983048 | tf_op jit(solution)/shard_map/ppermute | solution.py:842
  210.8 4.7 %collective-permute-start.21 = (bf16[1,80,512]{2,1,0:T(8,128)(2,1)S(1)}, bf16[1,80,512]{2,1,0:T(8,128)(2,1)S(1)}, u32[]{:S(2)}, u32[]{:S(2)}) collective-permute-start(bf16[1,80,512]{2,1,0:T(8,128)(2,1)S(1)} %get-tuple-element.153), channel_id=1, source_target_pairs={{0,24},{2,26},{4,28},{6,30},{8,16},{10,18},{12,20},{14,22},{16,8},... | collective-permute-start | bytes 245768 | tf_op jit(solution)/shard_map/ppermute | solution.py:842
  211.5 8.2 %collective-permute-start.20 = (bf16[1,80,512]{2,1,0:T(8,128)(2,1)S(1)}, bf16[1,80,512]{2,1,0:T(8,128)(2,1)S(1)}, u32[]{:S(2)}, u32[]{:S(2)}) collective-permute-start(bf16[1,80,512]{2,1,0:T(8,128)(2,1)S(1)} %get-tuple-element.154), channel_id=1, source_target_pairs={{0,16},{2,18},{4,20},{6,22},{8,24},{10,26},{12,28},{14,30},{16,0},... | collective-permute-start | bytes 245768 | tf_op jit(solution)/shard_map/ppermute | solution.py:842
  215.5 4.5 %collective-permute-start.19 = (bf16[1,80,512]{2,1,0:T(8,128)(2,1)S(1)}, bf16[1,80,512]{2,1,0:T(8,128)(2,1)S(1)}, u32[]{:S(2)}, u32[]{:S(2)}) collective-permute-start(bf16[1,80,512]{2,1,0:T(8,128)(2,1)S(1)} %get-tuple-element.152), channel_id=1, source_target_pairs={{0,8},{2,10},{4,12},{6,14},{8,0},{10,2},{12,4},{14,6},{16,24},{18,... | collective-permute-start | bytes 245768 | tf_op jit(solution)/shard_map/ppermute | solution.py:842
  220.1 8.5 %collective-permute-start.25 = (bf16[48,1536]{1,0:T(8,128)(2,1)S(1)}, bf16[48,1536]{1,0:T(8,128)(2,1)S(1)}, u32[]{:S(2)}, u32[]{:S(2)}) collective-permute-start(bf16[48,1536]{1,0:T(8,128)(2,1)S(1)} %maximum_maximum_fusion), channel_id=1, source_target_pairs={{0,1},{1,0},{2,3},{3,2},{4,5},{5,4},{6,7},{7,6},{8,9},{9,8},{10,11... | collective-permute-start | bytes 442376 | tf_op jit(solution)/shard_map/ppermute | solution.py:1033
  221.2 6.8 %collective-permute-start.26 = (bf16[32,1024]{1,0:T(8,128)(2,1)S(1)}, bf16[32,1024]{1,0:T(8,128)(2,1)S(1)}, u32[]{:S(2)}, u32[]{:S(2)}) collective-permute-start(bf16[32,1024]{1,0:T(8,128)(2,1)S(1)} %fusion.3), channel_id=1, source_target_pairs={{0,0},{2,1},{4,2},{6,3},{8,4},{10,5},{12,6},{14,7},{16,8},{18,9},{... | collective-permute-start | bytes 196616 | tf_op jit(solution)/shard_map/ppermute | solution.py:1032
  (11 other events, 18.9 us)
where the time goes:
time: 235 us; the launch traced here: 231 us
  Pallas kernels  144 us (61%)
  starting transfers between devices  34.3 us (15%)
  waiting for transfers between devices  20 us (9%)
  local copies, waits for them, and re-layouts  16.6 us (7%)
  other arithmetic  14.3 us (6%)
    ppermute x20, starting transfers between devices, start(): lax.ppermute(part, 'dp', [(i, i ^ offset) for i in range(self.n_dp)])  24.3 us
    pallas_call x1, Pallas kernels, attend_back_call(): pl.pallas_call(attend_back_kernel, grid_spec=pltpu.PrefetchScalarGridSpec...  19.6 us
    pallas_call x1, Pallas kernels, mlp_own_call(): pl.pallas_call(functools.partial(mlp_own_kernel, splits), grid_spec=pltpu...  19 us
    ppermute x20, waiting for transfers between devices, start(): lax.ppermute(part, 'dp', [(i, i ^ offset) for i in range(self.n_dp)])  18 us
    pallas_call x1, Pallas kernels, attend_call(): pl.pallas_call(attend_kernel, grid_spec=pltpu.PrefetchScalarGridSpec(num_...  17 us
    pallas_call x1, Pallas kernels, mlp_back_call(): pl.pallas_call(functools.partial(mlp_back_kernel, splits, pieces), grid_s...  15.4 us
    unnamed x64, local copies, waits for them, and re-layouts  13.2 us
    pallas_call x1, Pallas kernels, mlp_forward_call(): pl.pallas_call(functools.partial(mlp_forward_kernel, splits), grid_spec=p...  13 us
  transfers between devices with their start and end apart: 27, of which 11 were waited for; matrix products, arithmetic and copies ran while one was open for 7% of the time, Pallas kernels for 55%

commit v1 on v0

--- a/solution.py
+++ b/solution.py
@@ -517,7 +517,7 @@
         compiler_params=params(),
         cost_estimate=cost(8 * rows * D * FF_HALF, 12 * rows * D + 6 * D * FF_HALF + 4 * rows * FF_HALF),
         name="mlp_back",
-    )(info, plan["classes"], plan["order"], normed, slope, grads, gb_own, *([up] * splits), *([down] * splits))
+    )(info, plan["classes"], plan["halved"], normed, slope, grads, gb_own, *([up] * splits), *([down] * splits))
 
 
 def qkv_half_kernel(place_ref, info_ref, x_ref, w_ref, cos_ref, sin_ref, *refs):
@@ -905,6 +905,7 @@
     bits = [1 << i for i in range(n_dp.bit_length() - 1)]
     high_stages = pairs_of_bits(bits[2:])
     low_first = [(1,), (2,)] + high_stages
+    halvings = [(bit,) for bit in bits]
     order = send_order(low_first, me)
     ffb = FF_HALF // n_dp
     fast = ffb == LANES
@@ -931,7 +932,7 @@
                 lax.dynamic_index_in_dim(inner_bias.reshape(n_dp, 2, ffb), j, 1, False).reshape(1, FF_HALF),
             ),
         }
-    plan["order"] = order
+    plan["order"], plan["halved"] = order, send_order(halvings, me)
 
     def pieces_of(grads, table):
         if len(grads) == 2:
@@ -957,7 +958,7 @@
     info = after(info, grads)
     gn_their, inner, *up = mlp_back_call(info, plan, normed, slope, grads, gb_own)
 
-    up = Reduction(*pieces_of(up, order), low_first, n_dp)
+    up = Reduction(*pieces_of(up, plan["halved"]), halvings, n_dp)
     info = after(info, *down.land(gn_their), *up.land(gn_their))
     qkv = qkv_half_call(their, info, 1, normed, qkv_weight, cosine, sine, qkv)
     context, qe = attend_call(info, qkv)
@@ -970,7 +971,7 @@
     dmix = attend_back_call(info, qe, qkv, context, grad_context, cosine, sine)
 
     down_grad = down.finish(dmix)
-    info = after(info, out_received, down_grad)
+    info = after(info, out_received, down_grad, *up.land(dmix))
     small = D // n_dp
     shard = small // 2
     first = qkv_grad_call(info, plan, normed, dmix, 0, 2, proj)
@@ -1005,11 +1006,12 @@
         value = value[: n_dp // 2], value[n_dp // 2 :]
     up.finish(*value)
     landed = first.land(*value)
-    value, up.keep, _ = lax.optimization_barrier((tuple(value), up.keep, (*landed, gn_first)))
+    value, up.keep, _ = lax.optimization_barrier((tuple(value), up.keep, landed))
     value = Reduction(*value, low_first, n_dp)
     up_mine = lax.dynamic_slice_in_dim(up.keep, j * shard, shard, 0)
     up_their = lax.dynamic_slice_in_dim(up.keep, (1 - j) * shard, shard, 0).astype(BF)
     up_their = lax.ppermute(up_their, "branch", other)
+    value.keep, gn_first = lax.optimization_barrier((value.keep, gn_first))
     landed = value.land()
     tokens_grad = finish_grad_call(gn_own, after(gn_first, *landed), tokens, grads_own, gain)
     up_mine, up_their, tokens_grad = lax.optimization_barrier((up_mine, up_their, tokens_grad))

time: 235 us -> 230 us (0.979)
  starting transfers between devices: 34.3 us -> 30.3 us
    ppermute x20 -> x19, waiting for transfers between devices: 18 us -> 14.4 us  [start(): lax.ppermute(part, 'dp', [(i, i ^ offset) for i in range(self.n_dp)])]
    ppermute x1, waiting for transfers between devices: 0.01 us -> 3.04 us  [on_device(): gn_first = lax.ppermute(gn_send[0], 'branch', other)]
    unnamed x64 -> x62, local copies, waits for them, and re-layouts: 13.2 us -> 10.9 us
    ppermute x20 -> x19, starting transfers between devices: 24.3 us -> 22.6 us  [start(): lax.ppermute(part, 'dp', [(i, i ^ offset) for i in range(self.n_dp)])]
    convert_element_type x8 -> x9, other arithmetic: 11.1 us -> 11.3 us  [land(): parts = [part.astype(kind) for part in parts]]
  transfers between devices with their start and end apart: 27 -> 26, of which waited for: 11 -> 9; matrix products, arithmetic and copies ran while one was open for 7% -> 7% of each run, Pallas kernels for 55% -> 57%
where the time goes in v1:
time: 230 us; the launch traced here: 227 us
  Pallas kernels  145 us (63%)
  starting transfers between devices  30.3 us (13%)
  waiting for transfers between devices  20.9 us (9%)
  other arithmetic  14.4 us (6%)
  local copies, waits for them, and re-layouts  14.3 us (6%)
    ppermute x19, starting transfers between devices, start(): lax.ppermute(part, 'dp', [(i, i ^ offset) for i in range(self.n_dp)])  22.6 us
    pallas_call x1, Pallas kernels, attend_back_call(): pl.pallas_call(attend_back_kernel, grid_spec=pltpu.PrefetchScalarGridSpec...  19.6 us
    pallas_call x1, Pallas kernels, mlp_own_call(): pl.pallas_call(functools.partial(mlp_own_kernel, splits), grid_spec=pltpu...  19 us
    pallas_call x1, Pallas kernels, attend_call(): pl.pallas_call(attend_kernel, grid_spec=pltpu.PrefetchScalarGridSpec(num_...  17 us
    pallas_call x1, Pallas kernels, mlp_back_call(): pl.pallas_call(functools.partial(mlp_back_kernel, splits, pieces), grid_s...  15.4 us
    ppermute x19, waiting for transfers between devices, start(): lax.ppermute(part, 'dp', [(i, i ^ offset) for i in range(self.n_dp)])  14.4 us
    pallas_call x1, Pallas kernels, mlp_forward_call(): pl.pallas_call(functools.partial(mlp_forward_kernel, splits), grid_spec=p...  13 us
    pallas_call x2, Pallas kernels, qkv_half_call(): pl.pallas_call(qkv_half_kernel, grid_spec=pltpu.PrefetchScalarGridSpec(nu...  11.9 us
  transfers between devices with their start and end apart: 26, of which 9 were waited for; matrix products, arithmetic and copies ran while one was open for 7% of the time, Pallas kernels for 57%

profile of v1, /device:TPU:11, one launch (start us, length us, event | category | flops | bytes accessed | tf_op | source)
XLA Modules:
  0.0 226.7 jit_solution(10622896099917622664)
XLA Ops:
  1.0 1.2 collective-permute-start.1
  5.9 1.2 copy-done.2
  7.1 1.2 copy-done.19
  8.3 19.0 %mlp_own.1 = (bf16[1024,1024]{1,0:T(8,128)(2,1)S(1)}, bf16[1024,2048]{1,0:T(8,128)(2,1)}, bf16[512,1024]{1,0:T(8,128)(2,1)}, bf16[512,2048]{1,0:T(8,128)(2,1)}, ...) custom-call(s32[2]{0:T(128)S(1)} %pad_add_fusion.info_ref, s32[4]{0:T(128)S(1)} %get-tuple-element.177.cls_ref, ...), custom_call_target="tpu_custom_call" | custom-call | flops 8589934 | bytes 14680 | tf_op jit(solution)/shard_map/mlp_own/pallas_call | solution.py:324
  27.6 6.0 %qkv.2.refs_0_ = bf16[3,1024,512]{2,1,0:T(8,128)(2,1)} custom-call(s32[1]{0:T(128)} %bitcast.place_ref, s32[2]{0:T(128)S(1)} %pad_add_fusion.info_ref, bf16[1024,1024]{1,0:T(8,128)(2,1)S(1)} %get-tuple-element.74.x_ref.refs_12_, bf16[1024,3072]{1,0:T(8,128)(2,1)} %wv_ref.3, f32[1024,128]{1,0:T(8,128)S(1)} %bitcast.27, f32[1024,128]{1,0:T(8,128)S(1)} %negate_select_fusion.sin_ref), custom_call_target="tpu_custom_call" | custom-call | flops 1610612 | bytes 5767 | tf_op jit(solution)/shard_map/qkv/pallas_call | solution.py:548
  33.6 13.0 %mlp_forward.1 = (bf16[1024,1024]{1,0:T(8,128)(2,1)S(1)}, bf16[1024,2048]{1,0:T(8,128)(2,1)}, bf16[512,2048]{1,0:T(8,128)(2,1)}, f32[512,1024]{1,0:T(8,128)}) custom-call(s32[2]{0:T(128)S(1)} %pad_add_fusion.info_ref, s32[4]{0:T(128)S(1)} %get-tuple-element.177.cls_ref, ...), custom_call_target="tpu_custom_call", output_to_operand_aliasing={{0}: (17, {}), {1}: (18, {})} | custom-call | flops 4294967 | bytes 14680 | tf_op jit(solution)/shard_map/mlp_forward/pallas_call | solution.py:375
  47.5 2.2 copy-done.4
  49.7 10.4 %down_grad.1 = (bf16[1024,1024]{1,0:T(8,128)(2,1)}, bf16[8,128,1024]{2,1,0:T(8,128)(2,1)}, bf16[8,128,1024]{2,1,0:T(8,128)(2,1)}) custom-call(s32[2]{0:T(128)S(1)} %pad_add_fusion.info_ref, s32[4]{0:T(128)S(1)} %get-tuple-element.177.cls_ref, s32[4]{0:T(128)S(1)} %get-tuple-element.176.sub_ref, bf16[1024,2048]{1,0:T(8,128)(2,1)S(1)} %copy-done.4, ...), custom_call_target="tpu_custom_call" | custom-call | flops 4294967 | bytes 12582 | tf_op jit(solution)/shard_map/down_grad/pallas_call | solution.py:446
  60.1 1.6 collective-permute-start.2
  61.7 1.6 copy-done.7
  63.3 15.4 %mlp_back.1 = (f32[512,1024]{1,0:T(8,128)}, f32[1,2048]{1,0:T(1,128)S(1)}, bf16[8,64,2048]{2,1,0:T(8,128)(2,1)}, bf16[8,64,2048]{2,1,0:T(8,128)(2,1)}) custom-call(s32[2]{0:T(128)S(1)} %pad_add_fusion.info_ref, s32[4]{0:T(128)S(1)} %get-tuple-element.177.cls_ref, s32[16]{0:T(128)S(1)} %get-tuple-element.173.ord_ref, ...), custom_call_target="tpu_custom_call" | custom-call | flops 8589934 | bytes 23068 | tf_op jit(solution)/shard_map/mlp_back/pallas_call | solution.py:501
  78.8 2.3 %add_convert_fusion.2 = (bf16[4,128,1024]{2,1,0:T(8,128)(2,1)}, bf16[4,128,1024]{2,1,0:T(8,128)(2,1)}) fusion(bf16[8,128,1024]{2,1,0:T(8,128)(2,1)S(1)} %collective-permute-done.2, bf16[8,128,1024]{2,1,0:T(8,128)(2,1)S(1)} %copy-done.25), kind=kLoop, calls=%fused_computation.2 | loop fusion | flops 4194304 | bytes 6291456 | tf_op jit(solution)/shard_map/convert_element_type | solution.py:861
  81.1 1.2 collective-permute-start.4
  83.1 2.1 add_convert_fusion
  85.2 1.2 collective-permute-start.5
  86.5 5.9 %qkv.3.q_ref.k_ref.v_ref = bf16[3,1024,512]{2,1,0:T(8,128)(2,1)} custom-call(s32[1]{0:T(128)} %bitcast.3.place_ref, s32[2]{0:T(128)S(1)} %pad_add_fusion.info_ref, bf16[1024,1024]{1,0:T(8,128)(2,1)S(1)} %get-tuple-element.86.x_ref, bf16[1024,3072]{1,0:T(8,128)(2,1)} %wv_ref.3, f32[1024,128]{1,0:T(8,128)S(1)} %bitcast.28, ...), custom_call_target="tpu_custom_call", output_to_operand_aliasing={{}: (6, {})} | custom-call | flops 1610612 | bytes 5767 | tf_op jit(solution)/shard_map/qkv/pallas_call | solution.py:548
  92.4 1.9 copy-done
  94.2 17.0 %attend.1 = (bf16[1024,512]{1,0:T(8,128)(2,1)}, bf16[8,1024,128]{2,1,0:T(8,128)(2,1)}) custom-call(s32[2]{0:T(128)S(1)} %pad_add_fusion.info_ref, bf16[3,1024,512]{2,1,0:T(8,128)(2,1)S(1)} %copy-done, bf16[3,1024,512]{2,1,0:T(8,128)(2,1)S(1)} %copy-done, bf16[3,1024,512]{2,1,0:T(8,128)(2,1)S(1)} %copy-done), custom_call_target="tpu_custom_call" | custom-call | flops 10737418 | bytes 3145 | tf_op jit(solution)/shard_map/attend/pallas_call | solution.py:141
  111.3 1.2 copy-done.5
  112.5 3.5 %send_out.1 = bf16[512,1024]{1,0:T(8,128)(2,1)} custom-call(s32[1]{0:T(128)} %bitcast.3.place_ref, s32[2]{0:T(128)S(1)} %pad_add_fusion.info_ref, bf16[1024,512]{1,0:T(8,128)(2,1)S(1)} %copy-done.5, bf16[1024,1024]{1,0:T(8,128)(2,1)} %w_ref.9, f32[512,1024]{1,0:T(8,128)S(1)} %copy-done.16), custom_call_target="tpu_custom_call" | custom-call | flops 536870 | bytes 5242 | tf_op jit(solution)/shard_map/send_out/pallas_call | solution.py:583
  116.4 1.8 add_convert_fusion.12
  118.1 1.3 collective-permute-start.9
  119.5 1.1 collective-permute-start.8
  120.6 1.1 collective-permute-start.7
  121.7 6.3 %proj_back.1 = (bf16[1024,512]{1,0:T(8,128)(2,1)}, bf16[8,32,1024]{2,1,0:T(8,128)(2,1)}, bf16[8,32,1024]{2,1,0:T(8,128)(2,1)}) custom-call(s32[2]{0:T(128)S(1)} %pad_add_fusion.info_ref, s32[16]{0:T(128)S(1)} %get-tuple-element.172.ord_ref, bf16[1024,1024]{1,0:T(8,128)(2,1)S(1)} %copy-done.8, bf16[1024,512]{1,0:T(8,128)(2,1)S(1)} %copy-done.6, ...), custom_call_target="tpu_custom_call" | custom-call | flops 2147483 | bytes 6291 | tf_op jit(solution)/shard_map/proj_back/pallas_call | solution.py:637
  128.2 1.7 add_convert_fusion.6
  130.2 1.2 copy-done.20
  131.5 19.6 %attend_back.1.own_ref.their_ref.d_ref = bf16[3,1024,512]{2,1,0:T(8,128)(2,1)S(1)} custom-call(s32[2]{0:T(128)S(1)} %pad_add_fusion.info_ref, bf16[8,1024,128]{2,1,0:T(8,128)(2,1)S(1)} %copy-done.18, bf16[3,1024,512]{2,1,0:T(8,128)(2,1)S(1)} %copy-done.1, bf16[3,1024,512]{2,1,0:T(8,128)(2,1)S(1)} %copy-done.1, bf16[1024,512]{1,0:T(8,128)(2,1)S(1)} %copy-done.6, ...), custom_call_target="tpu_custom_call" | custom-call | flops 12884901 | bytes 4194 | tf_op jit(solution)/shard_map/attend_back/pallas_call | solution.py:217
  152.4 4.5 %qkv_grad.2 = (bf16[8,96,1024]{2,1,0:T(8,128)(2,1)}, bf16[8,96,1024]{2,1,0:T(8,128)(2,1)}) custom-call(s32[2]{0:T(128)S(1)} %pad_add_fusion.info_ref, s32[16]{0:T(128)S(1)} %get-tuple-element.172.ord_ref, bf16[1024,1024]{1,0:T(8,128)(2,1)S(1)} %get-tuple-element.86.x_ref, bf16[3,1024,512]{2,1,0:T(8,128)(2,1)S(1)} %attend_back.1.own_ref.their_ref.d_ref, ...), custom_call_target="tpu_custom_call" | custom-call | flops 2147483 | bytes 6291 | tf_op jit(solution)/shard_map/qkv_grad/pallas_call | solution.py:720
  157.0 1.8 collective-permute-start.11
  158.8 5.8 %grad_normed.2 = (bf16[512,1024]{1,0:T(8,128)(2,1)}, f32[2,1024]{1,0:T(2,128)S(1)}) custom-call(s32[1]{0:T(128)} %bitcast.3.place_ref, s32[2]{0:T(128)S(1)} %pad_add_fusion.info_ref, bf16[3,1024,512]{2,1,0:T(8,128)(2,1)S(1)} %attend_back.1.own_ref.their_ref.d_ref, bf16[1024,3072]{1,0:T(8,128)(2,1)} %wv_ref.3, bf16[1024,3072]{1,0:T(8,128)(2,1)} %wv_ref.3, ...), custom_call_target="tpu_custom_call" | custom-call | flops 1610612 | bytes 8912 | tf_op jit(solution)/shard_map/grad_normed/pallas_call | solution.py:766
  166.3 2.2 collective-permute-start.12
  169.1 5.8 %grad_normed.3 = (f32[512,1024]{1,0:T(8,128)}, f32[2,1024]{1,0:T(2,128)S(1)}) custom-call(s32[1]{0:T(128)} %bitcast.place_ref, s32[2]{0:T(128)S(1)} %pad_add_fusion.info_ref, bf16[3,1024,512]{2,1,0:T(8,128)(2,1)S(1)} %attend_back.1.own_ref.their_ref.d_ref, bf16[1024,3072]{1,0:T(8,128)(2,1)} %wv_ref.3, bf16[1024,3072]{1,0:T(8,128)(2,1)} %wv_ref.3, ...), custom_call_target="tpu_custom_call" | custom-call | flops 1610612 | bytes 8912 | tf_op jit(solution)/shard_map/grad_normed/pallas_call | solution.py:766
  174.8 3.7 %finish_out.1 = bf16[512,1024]{1,0:T(8,128)(2,1)} custom-call(s32[1]{0:T(128)} %bitcast.place_ref, s32[2]{0:T(128)S(1)} %pad_add_fusion.info_ref, bf16[1024,512]{1,0:T(8,128)(2,1)S(1)} %copy-done.6, bf16[1024,1024]{1,0:T(8,128)(2,1)} %w_ref.9, f32[512,1024]{1,0:T(8,128)S(1)} %copy-done.17, bf16[512,1024]{1,0:T(8,128)(2,1)S(1)} %copy-done.3, ...), custom_call_target="tpu_custom_call" | custom-call | flops 536870 | bytes 5242 | tf_op jit(solution)/shard_map/finish_out/pallas_call | solution.py:583
  178.5 3.0 %qkv_grad.3 = (bf16[8,80,512]{2,1,0:T(8,128)(2,1)}, bf16[8,80,512]{2,1,0:T(8,128)(2,1)}) custom-call(s32[2]{0:T(128)S(1)} %pad_add_fusion.info_ref, s32[16]{0:T(128)S(1)} %get-tuple-element.172.ord_ref, bf16[1024,1024]{1,0:T(8,128)(2,1)S(1)} %get-tuple-element.86.x_ref, bf16[3,1024,512]{2,1,0:T(8,128)(2,1)S(1)} %attend_back.1.own_ref.their_ref.d_ref, ...), custom_call_target="tpu_custom_call" | custom-call | flops 1073741 | bytes 4194 | tf_op jit(solution)/shard_map/qkv_grad/pallas_call | solution.py:720
  181.5 3.2 %collective-permute-done.13 = bf16[4,96,1024]{2,1,0:T(8,128)(2,1)S(1)} collective-permute-done((bf16[4,96,1024]{2,1,0:T(8,128)(2,1)S(1)}, bf16[4,96,1024]{2,1,0:T(8,128)(2,1)S(1)}, u32[]{:S(2)}, u32[]{:S(2)}) %collective-permute-start.13) | collective-permute-done | bytes 786464 | tf_op jit(solution)/shard_map/ppermute | solution.py:842
  186.4 2.4 %collective-permute-start.23 = (bf16[1,96,1024]{2,1,0:T(8,128)(2,1)}, bf16[1,96,1024]{2,1,0:T(8,128)(2,1)S(1)}, u32[]{:S(2)}, u32[]{:S(2)}) collective-permute-start(bf16[1,96,1024]{2,1,0:T(8,128)(2,1)} %get-tuple-element.150), channel_id=1, source_target_pairs={{0,24},{2,26},{4,28},{6,30},{8,16},{10,18},{12,20},{14,22},{16,8},... | collective-permute-start | bytes 589832 | tf_op jit(solution)/shard_map/ppermute | solution.py:842
  190.0 3.0 %collective-permute-done.15.r_ref = bf16[512,1024]{1,0:T(8,128)(2,1)} collective-permute-done((bf16[512,1024]{1,0:T(8,128)(2,1)}, bf16[512,1024]{1,0:T(8,128)(2,1)}, u32[]{:S(2)}, u32[]{:S(2)}) %collective-permute-start.15) | collective-permute-done | bytes 1048608 | tf_op jit(solution)/shard_map/ppermute | solution.py:987
  193.5 1.4 add_convert_fusion.8
  196.0 3.5 %finish_grad.1 = f32[512,1024]{1,0:T(8,128)} custom-call(f32[512,1024]{1,0:T(8,128)S(1)} %copy-done.13, bf16[512,1024]{1,0:T(8,128)(2,1)} %collective-permute-done.15.r_ref, bf16[512,1024]{1,0:T(8,128)(2,1)S(1)} %copy-done.3, bf16[512,1024]{1,0:T(8,128)(2,1)S(1)} %copy-done.10, bf16[1,1024]{1,0:T(2,128)(2,1)S(1)} %reshape.129.gain_ref), custom_call_target="tpu_custom_call" | custom-call | flops 10485 | bytes 7340 | tf_op jit(solution)/shard_map/finish_grad/pallas_call | solution.py:822
  199.6 1.4 assemble.2
  200.9 1.8 collective-permute-done.23
  202.7 3.3 %collective-permute-done.22 = bf16[1,96,1024]{2,1,0:T(8,128)(2,1)S(1)} collective-permute-done((bf16[1,96,1024]{2,1,0:T(8,128)(2,1)S(1)}, bf16[1,96,1024]{2,1,0:T(8,128)(2,1)S(1)}, u32[]{:S(2)}, u32[]{:S(2)}) %collective-permute-start.22) | collective-permute-done | bytes 196640 | tf_op jit(solution)/shard_map/ppermute | solution.py:842
  206.5 4.0 %collective-permute-start.19 = (bf16[1,80,512]{2,1,0:T(8,128)(2,1)S(1)}, bf16[1,80,512]{2,1,0:T(8,128)(2,1)S(1)}, u32[]{:S(2)}, u32[]{:S(2)}) collective-permute-start(bf16[1,80,512]{2,1,0:T(8,128)(2,1)S(1)} %get-tuple-element.160), channel_id=1, source_target_pairs={{0,16},{2,18},{4,20},{6,22},{8,24},{10,26},{12,28},{14,30},{16,0},... | collective-permute-start | bytes 245768 | tf_op jit(solution)/shard_map/ppermute | solution.py:842
  210.6 5.2 %collective-permute-done.19 = bf16[1,80,512]{2,1,0:T(8,128)(2,1)S(1)} collective-permute-done((bf16[1,80,512]{2,1,0:T(8,128)(2,1)S(1)}, bf16[1,80,512]{2,1,0:T(8,128)(2,1)S(1)}, u32[]{:S(2)}, u32[]{:S(2)}) %collective-permute-start.19) | collective-permute-done | bytes 81952 | tf_op jit(solution)/shard_map/ppermute | solution.py:842
  216.9 4.1 %collective-permute-start.25 = (bf16[32,1024]{1,0:T(8,128)(2,1)S(1)}, bf16[32,1024]{1,0:T(8,128)(2,1)S(1)}, u32[]{:S(2)}, u32[]{:S(2)}) collective-permute-start(bf16[32,1024]{1,0:T(8,128)(2,1)S(1)} %fusion.3), channel_id=1, source_target_pairs={{0,0},{2,1},{4,2},{6,3},{8,4},{10,5},{12,6},{14,7},{16,8},{18,9},{... | collective-permute-start | bytes 196616 | tf_op jit(solution)/shard_map/ppermute | solution.py:1034
  221.6 2.5 %collective-permute-done.25 = bf16[32,1024]{1,0:T(8,128)(2,1)S(1)} collective-permute-done((bf16[32,1024]{1,0:T(8,128)(2,1)S(1)}, bf16[32,1024]{1,0:T(8,128)(2,1)S(1)}, u32[]{:S(2)}, u32[]{:S(2)}) %collective-permute-start.25) | collective-permute-done | bytes 65568 | tf_op jit(solution)/shard_map/ppermute | solution.py:1034
  225.4 1.3 assemble.3
  (131 shorter events, 17.6 us)
Async XLA Ops:
  0.6 32.9 %collective-permute-start = (bf16[512,1024]{1,0:T(8,128)(2,1)}, bf16[512,1024]{1,0:T(8,128)(2,1)}, u32[]{:S(2)}, u32[]{:S(2)}) collective-permute-start(bf16[512,1024]{1,0:T(8,128)(2,1)} %t_ref.7), channel_id=1, source_target_pairs={{0,1},{1,0},{2,3},{3,2},{4,5},{5,4},{6,7},{7,6},{8,9},{9,8},{10,11... | collective-permute-start | bytes 3145736 | tf_op jit(solution)/shard_map/ppermute | solution.py:899
  1.0 46.6 %collective-permute-start.1 = (bf16[512,1024]{1,0:T(8,128)(2,1)}, bf16[512,1024]{1,0:T(8,128)(2,1)}, u32[]{:S(2)}, u32[]{:S(2)}) collective-permute-start(bf16[512,1024]{1,0:T(8,128)(2,1)} %c_ref.1), channel_id=1, source_target_pairs={{0,1},{1,0},{2,3},{3,2},{4,5},{5,4},{6,7},{7,6},{8,9},{9,8},{10,11... | collective-permute-start | bytes 3145736 | tf_op jit(solution)/shard_map/ppermute | solution.py:900
  33.6 14.0 %copy-start.9 = (bf16[512,1024]{1,0:T(8,128)(2,1)S(1)}, bf16[512,1024]{1,0:T(8,128)(2,1)}, u32[]{:S(2)}) copy-start(bf16[512,1024]{1,0:T(8,128)(2,1)} %get-tuple-element.82.go_ref.g_ref) | copy-start | bytes 3145732
  49.7 12.0 %copy-start.29 = (s32[16]{0:T(128)S(1)}, s32[16]{0:T(128)}, u32[]{:S(2)}) copy-start(s32[16]{0:T(128)} %constant.77.clone) | copy-start | bytes 196
  49.7 12.0 %copy-start.30 = (s32[16]{0:T(128)S(1)}, s32[16]{0:T(128)}, u32[]{:S(2)}) copy-start(s32[16]{0:T(128)} %constant.79.clone) | copy-start | bytes 196
  49.7 12.0 %copy-start.14 = (bf16[512,2048]{1,0:T(8,128)(2,1)S(1)}, bf16[512,2048]{1,0:T(8,128)(2,1)}, u32[]{:S(2)}) copy-start(bf16[512,2048]{1,0:T(8,128)(2,1)} %get-tuple-element.87.gb_ref) | copy-start | bytes 6291460
  49.7 12.0 %copy-start.15 = (bf16[512,2048]{1,0:T(8,128)(2,1)S(1)}, bf16[512,2048]{1,0:T(8,128)(2,1)}, u32[]{:S(2)}) copy-start(bf16[512,2048]{1,0:T(8,128)(2,1)} %get-tuple-element.79.slope_ref) | copy-start | bytes 6291460
  60.1 18.6 %collective-permute-start.2 = (bf16[8,128,1024]{2,1,0:T(8,128)(2,1)}, bf16[8,128,1024]{2,1,0:T(8,128)(2,1)S(1)}, u32[]{:S(2)}, u32[]{:S(2)}) collective-permute-start(bf16[8,128,1024]{2,1,0:T(8,128)(2,1)} %get-tuple-element.90), channel_id=1, source_target_pairs={{0,2},{2,0},{4,6},{6,4},{8,10},{10,8},{12,14},{14,12},{16,18},{18,... | collective-permute-start | bytes 6291464 | tf_op jit(solution)/shard_map/ppermute | solution.py:842
  63.3 15.5 %copy-start.25 = (bf16[8,128,1024]{2,1,0:T(8,128)(2,1)S(1)}, bf16[8,128,1024]{2,1,0:T(8,128)(2,1)}, u32[]{:S(2)}) copy-start(bf16[8,128,1024]{2,1,0:T(8,128)(2,1)} %get-tuple-element.89) | copy-start | bytes 6291460
  78.7 4.4 %collective-permute-start.3 = (bf16[8,64,2048]{2,1,0:T(8,128)(2,1)}, bf16[8,64,2048]{2,1,0:T(8,128)(2,1)S(1)}, u32[]{:S(2)}, u32[]{:S(2)}) collective-permute-start(bf16[8,64,2048]{2,1,0:T(8,128)(2,1)} %get-tuple-element.93), channel_id=1, source_target_pairs={{0,2},{2,0},{4,6},{6,4},{8,10},{10,8},{12,14},{14,12},{16,18},{18,... | collective-permute-start | bytes 6291464 | tf_op jit(solution)/shard_map/ppermute | solution.py:842
  78.8 4.3 %copy-start.26 = (bf16[8,64,2048]{2,1,0:T(8,128)(2,1)S(1)}, bf16[8,64,2048]{2,1,0:T(8,128)(2,1)}, u32[]{:S(2)}) copy-start(bf16[8,64,2048]{2,1,0:T(8,128)(2,1)} %get-tuple-element.92) | copy-start | bytes 6291460
  81.1 35.2 %collective-permute-start.4 = (bf16[4,128,1024]{2,1,0:T(8,128)(2,1)}, bf16[4,128,1024]{2,1,0:T(8,128)(2,1)}, u32[]{:S(2)}, u32[]{:S(2)}) collective-permute-start(bf16[4,128,1024]{2,1,0:T(8,128)(2,1)} %get-tuple-element.140), channel_id=1, source_target_pairs={{0,4},{2,6},{4,0},{6,2},{8,12},{10,14},{12,8},{14,10},{16,20},{18,... | collective-permute-start | bytes 3145736 | tf_op jit(solution)/shard_map/ppermute | solution.py:842
  85.2 42.9 %collective-permute-start.5 = (bf16[4,64,2048]{2,1,0:T(8,128)(2,1)}, bf16[4,64,2048]{2,1,0:T(8,128)(2,1)}, u32[]{:S(2)}, u32[]{:S(2)}) collective-permute-start(bf16[4,64,2048]{2,1,0:T(8,128)(2,1)} %get-tuple-element.138), channel_id=1, source_target_pairs={{0,4},{2,6},{4,0},{6,2},{8,12},{10,14},{12,8},{14,10},{16,20},{18,... | collective-permute-start | bytes 3145736 | tf_op jit(solution)/shard_map/ppermute | solution.py:842
  94.2 17.0 %copy-start.16 = (f32[512,1024]{1,0:T(8,128)S(1)}, f32[512,1024]{1,0:T(8,128)}, u32[]{:S(2)}) copy-start(f32[512,1024]{1,0:T(8,128)} %get-tuple-element.96.e_ref) | copy-start | bytes 6291460
  112.5 3.9 %copy-start.24 = (bf16[4,128,1024]{2,1,0:T(8,128)(2,1)S(1)}, bf16[4,128,1024]{2,1,0:T(8,128)(2,1)}, u32[]{:S(2)}) copy-start(bf16[4,128,1024]{2,1,0:T(8,128)(2,1)} %get-tuple-element.97) | copy-start | bytes 3145732
  116.0 5.6 %copy-start.6 = (bf16[1024,512]{1,0:T(8,128)(2,1)S(1)}, bf16[1024,512]{1,0:T(8,128)(2,1)}, u32[]{:S(2)}) copy-start(bf16[1024,512]{1,0:T(8,128)(2,1)} %get-tuple-element.95.c_ref.o_ref) | copy-start | bytes 3145732
  116.0 5.6 %copy-start.8 = (bf16[1024,1024]{1,0:T(8,128)(2,1)S(1)}, bf16[1024,1024]{1,0:T(8,128)(2,1)}, u32[]{:S(2)}) copy-start(bf16[1024,1024]{1,0:T(8,128)(2,1)} %get-tuple-element.83.g_ref) | copy-start | bytes 6291460
  116.0 36.2 %collective-permute-start.6 = (bf16[512,1024]{1,0:T(8,128)(2,1)}, bf16[512,1024]{1,0:T(8,128)(2,1)S(1)}, u32[]{:S(2)}, u32[]{:S(2)}) collective-permute-start(bf16[512,1024]{1,0:T(8,128)(2,1)} %send_out.1), channel_id=1, source_target_pairs={{0,1},{1,0},{2,3},{3,2},{4,5},{5,4},{6,7},{7,6},{8,9},{9,8},{10,11... | collective-permute-start | bytes 3145736 | tf_op jit(solution)/shard_map/ppermute | solution.py:968
  118.1 32.9 %collective-permute-start.9 = (bf16[1,128,1024]{2,1,0:T(8,128)(2,1)S(1)}, bf16[1,128,1024]{2,1,0:T(8,128)(2,1)S(1)}, u32[]{:S(2)}, u32[]{:S(2)}) collective-permute-start(bf16[1,128,1024]{2,1,0:T(8,128)(2,1)S(1)} %get-tuple-element.146), channel_id=1, source_target_pairs={{0,24},{2,26},{4,28},{6,30},{8,16},{10,18},{12,20},{14,22},{16,8},... | collective-permute-start | bytes 786440 | tf_op jit(solution)/shard_map/ppermute | solution.py:842
  119.5 31.6 %collective-permute-start.8 = (bf16[1,128,1024]{2,1,0:T(8,128)(2,1)S(1)}, bf16[1,128,1024]{2,1,0:T(8,128)(2,1)S(1)}, u32[]{:S(2)}, u32[]{:S(2)}) collective-permute-start(bf16[1,128,1024]{2,1,0:T(8,128)(2,1)S(1)} %get-tuple-element.147), channel_id=1, source_target_pairs={{0,16},{2,18},{4,20},{6,22},{8,24},{10,26},{12,28},{14,30},{16,0},... | collective-permute-start | bytes 786440 | tf_op jit(solution)/shard_map/ppermute | solution.py:842
  120.6 30.5 %collective-permute-start.7 = (bf16[1,128,1024]{2,1,0:T(8,128)(2,1)S(1)}, bf16[1,128,1024]{2,1,0:T(8,128)(2,1)S(1)}, u32[]{:S(2)}, u32[]{:S(2)}) collective-permute-start(bf16[1,128,1024]{2,1,0:T(8,128)(2,1)S(1)} %get-tuple-element.148), channel_id=1, source_target_pairs={{0,8},{2,10},{4,12},{6,14},{8,0},{10,2},{12,4},{14,6},{16,24},{18,... | collective-permute-start | bytes 786440 | tf_op jit(solution)/shard_map/ppermute | solution.py:842
  121.7 6.5 %copy-start.23 = (bf16[4,64,2048]{2,1,0:T(8,128)(2,1)S(1)}, bf16[4,64,2048]{2,1,0:T(8,128)(2,1)}, u32[]{:S(2)}) copy-start(bf16[4,64,2048]{2,1,0:T(8,128)(2,1)} %get-tuple-element.100) | copy-start | bytes 3145732
  121.7 8.5 %copy-start.18 = (bf16[8,1024,128]{2,1,0:T(8,128)(2,1)S(1)}, bf16[8,1024,128]{2,1,0:T(8,128)(2,1)}, u32[]{:S(2)}) copy-start(bf16[8,1024,128]{2,1,0:T(8,128)(2,1)} %get-tuple-element.102.qe_ref) | copy-start | bytes 6291460
  128.0 2.2 copy-start.1
  129.9 22.2 %collective-permute-start.10 = (bf16[2,64,2048]{2,1,0:T(8,128)(2,1)S(1)}, bf16[2,64,2048]{2,1,0:T(8,128)(2,1)S(1)}, u32[]{:S(2)}, u32[]{:S(2)}) collective-permute-start(bf16[2,64,2048]{2,1,0:T(8,128)(2,1)S(1)} %get-tuple-element.144), channel_id=1, source_target_pairs={{0,8},{2,10},{4,12},{6,14},{8,0},{10,2},{12,4},{14,6},{16,24},{18,... | collective-permute-start | bytes 1572872 | tf_op jit(solution)/shard_map/ppermute | solution.py:842
  152.4 6.4 %copy-start.12 = (f32[512,1024]{1,0:T(8,128)S(1)}, f32[512,1024]{1,0:T(8,128)}, u32[]{:S(2)}) copy-start(f32[512,1024]{1,0:T(8,128)} %get-tuple-element.88.base_ref) | copy-start | bytes 6291460
  157.0 7.7 %collective-permute-start.11 = (bf16[8,96,1024]{2,1,0:T(8,128)(2,1)}, bf16[8,96,1024]{2,1,0:T(8,128)(2,1)S(1)}, u32[]{:S(2)}, u32[]{:S(2)}) collective-permute-start(bf16[8,96,1024]{2,1,0:T(8,128)(2,1)} %get-tuple-element.109), channel_id=1, source_target_pairs={{0,2},{2,0},{4,6},{6,4},{8,10},{10,8},{12,14},{14,12},{16,18},{18,... | collective-permute-start | bytes 4718600 | tf_op jit(solution)/shard_map/ppermute | solution.py:842
  158.8 5.8 %copy-start.27 = (bf16[8,96,1024]{2,1,0:T(8,128)(2,1)S(1)}, bf16[8,96,1024]{2,1,0:T(8,128)(2,1)}, u32[]{:S(2)}) copy-start(bf16[8,96,1024]{2,1,0:T(8,128)(2,1)} %get-tuple-element.112) | copy-start | bytes 4718596
  164.6 3.9 %copy-start.28 = (bf16[1024]{0:T(1024)(128)(2,1)S(1)}, bf16[1024]{0:T(1024)(128)(2,1)}, u32[]{:S(2)}) copy-start(bf16[1024]{0:T(1024)(128)(2,1)} %param.23) | copy-start | bytes 6148
  164.6 4.4 %copy-start.3 = (bf16[512,1024]{1,0:T(8,128)(2,1)S(1)}, bf16[512,1024]{1,0:T(8,128)(2,1)}, u32[]{:S(2)}) copy-start(bf16[512,1024]{1,0:T(8,128)(2,1)} %t_ref.7) | copy-start | bytes 3145732
  164.7 4.4 %copy-start.11 = (f32[512,1024]{1,0:T(8,128)S(1)}, f32[512,1024]{1,0:T(8,128)}, u32[]{:S(2)}) copy-start(f32[512,1024]{1,0:T(8,128)} %get-tuple-element.114.base_ref) | copy-start | bytes 6291460
  165.4 19.3 %collective-permute-start.13 = (bf16[4,96,1024]{2,1,0:T(8,128)(2,1)S(1)}, bf16[4,96,1024]{2,1,0:T(8,128)(2,1)S(1)}, u32[]{:S(2)}, u32[]{:S(2)}) collective-permute-start(bf16[4,96,1024]{2,1,0:T(8,128)(2,1)S(1)} %get-tuple-element.142), channel_id=1, source_target_pairs={{0,4},{2,6},{4,0},{6,2},{8,12},{10,14},{12,8},{14,10},{16,20},{18,... | collective-permute-start | bytes 2359304 | tf_op jit(solution)/shard_map/ppermute | solution.py:842
  166.3 15.1 %collective-permute-start.12 = (bf16[1,64,2048]{2,1,0:T(8,128)(2,1)S(1)}, bf16[1,64,2048]{2,1,0:T(8,128)(2,1)S(1)}, u32[]{:S(2)}, u32[]{:S(2)}) collective-permute-start(bf16[1,64,2048]{2,1,0:T(8,128)(2,1)S(1)} %get-tuple-element.156), channel_id=1, source_target_pairs={{0,16},{2,18},{4,20},{6,22},{8,24},{10,26},{12,28},{14,30},{16,0},... | collective-permute-start | bytes 786440 | tf_op jit(solution)/shard_map/ppermute | solution.py:842
  168.6 24.5 %collective-permute-start.15 = (bf16[512,1024]{1,0:T(8,128)(2,1)}, bf16[512,1024]{1,0:T(8,128)(2,1)}, u32[]{:S(2)}, u32[]{:S(2)}) collective-permute-start(bf16[512,1024]{1,0:T(8,128)(2,1)} %get-tuple-element.111), channel_id=1, source_target_pairs={{0,1},{1,0},{2,3},{3,2},{4,5},{5,4},{6,7},{7,6},{8,9},{9,8},{10,11... | collective-permute-start | bytes 3145736 | tf_op jit(solution)/shard_map/ppermute | solution.py:987
  169.0 5.8 %copy-start.17 = (f32[512,1024]{1,0:T(8,128)S(1)}, f32[512,1024]{1,0:T(8,128)}, u32[]{:S(2)}) copy-start(f32[512,1024]{1,0:T(8,128)} %get-tuple-element.117.e_ref) | copy-start | bytes 6291460
  181.5 14.5 %copy-start.10 = (bf16[512,1024]{1,0:T(8,128)(2,1)S(1)}, bf16[512,1024]{1,0:T(8,128)(2,1)}, u32[]{:S(2)}) copy-start(bf16[512,1024]{1,0:T(8,128)(2,1)} %get-tuple-element.82.go_ref.g_ref) | copy-start | bytes 3145732
  185.7 7.8 %collective-permute-start.16 = (bf16[8,80,512]{2,1,0:T(8,128)(2,1)}, bf16[8,80,512]{2,1,0:T(8,128)(2,1)}, u32[]{:S(2)}, u32[]{:S(2)}) collective-permute-start(bf16[8,80,512]{2,1,0:T(8,128)(2,1)} %get-tuple-element.131), channel_id=1, source_target_pairs={{0,2},{2,0},{4,6},{6,4},{8,10},{10,8},{12,14},{14,12},{16,18},{18,... | collective-permute-start | bytes 1966088 | tf_op jit(solution)/shard_map/ppermute | solution.py:842
  186.4 9.6 %copy-start.13 = (f32[512,1024]{1,0:T(8,128)S(1)}, f32[512,1024]{1,0:T(8,128)}, u32[]{:S(2)}) copy-start(f32[512,1024]{1,0:T(8,128)} %get-tuple-element.115.gn_ref) | copy-start | bytes 6291460
  186.4 16.3 %collective-permute-start.23 = (bf16[1,96,1024]{2,1,0:T(8,128)(2,1)}, bf16[1,96,1024]{2,1,0:T(8,128)(2,1)S(1)}, u32[]{:S(2)}, u32[]{:S(2)}) collective-permute-start(bf16[1,96,1024]{2,1,0:T(8,128)(2,1)} %get-tuple-element.150), channel_id=1, source_target_pairs={{0,24},{2,26},{4,28},{6,30},{8,16},{10,18},{12,20},{14,22},{16,8},... | collective-permute-start | bytes 589832 | tf_op jit(solution)/shard_map/ppermute | solution.py:842
  188.8 17.2 %collective-permute-start.22 = (bf16[1,96,1024]{2,1,0:T(8,128)(2,1)S(1)}, bf16[1,96,1024]{2,1,0:T(8,128)(2,1)S(1)}, u32[]{:S(2)}, u32[]{:S(2)}) collective-permute-start(bf16[1,96,1024]{2,1,0:T(8,128)(2,1)S(1)} %get-tuple-element.151), channel_id=1, source_target_pairs={{0,16},{2,18},{4,20},{6,22},{8,24},{10,26},{12,28},{14,30},{16,0},... | collective-permute-start | bytes 589832 | tf_op jit(solution)/shard_map/ppermute | solution.py:842
  189.5 16.5 %collective-permute-start.21 = (bf16[1,96,1024]{2,1,0:T(8,128)(2,1)S(1)}, bf16[1,96,1024]{2,1,0:T(8,128)(2,1)S(1)}, u32[]{:S(2)}, u32[]{:S(2)}) collective-permute-start(bf16[1,96,1024]{2,1,0:T(8,128)(2,1)S(1)} %get-tuple-element.152), channel_id=1, source_target_pairs={{0,8},{2,10},{4,12},{6,14},{8,0},{10,2},{12,4},{14,6},{16,24},{18,... | collective-permute-start | bytes 589832 | tf_op jit(solution)/shard_map/ppermute | solution.py:842
  193.1 6.5 %collective-permute-start.14 = (bf16[32,2048]{1,0:T(8,128)(2,1)S(1)}, bf16[32,2048]{1,0:T(8,128)(2,1)S(1)}, u32[]{:S(2)}, u32[]{:S(2)}) collective-permute-start(bf16[32,2048]{1,0:T(8,128)(2,1)S(1)} %dynamic-slice_convert_fusion), channel_id=1, source_target_pairs={{0,1},{1,0},{2,3},{3,2},{4,5},{5,4},{6,7},{7,6},{8,9},{9,8},{10,11... | collective-permute-start | bytes 393224 | tf_op jit(solution)/shard_map/ppermute | solution.py:1013
  195.0 11.2 %collective-permute-start.17 = (bf16[4,80,512]{2,1,0:T(8,128)(2,1)S(1)}, bf16[4,80,512]{2,1,0:T(8,128)(2,1)S(1)}, u32[]{:S(2)}, u32[]{:S(2)}) collective-permute-start(bf16[4,80,512]{2,1,0:T(8,128)(2,1)S(1)} %get-tuple-element.154), channel_id=1, source_target_pairs={{0,4},{2,6},{4,0},{6,2},{8,12},{10,14},{12,8},{14,10},{16,20},{18,... | collective-permute-start | bytes 983048 | tf_op jit(solution)/shard_map/ppermute | solution.py:842
  206.2 4.4 %collective-permute-start.20 = (bf16[1,80,512]{2,1,0:T(8,128)(2,1)S(1)}, bf16[1,80,512]{2,1,0:T(8,128)(2,1)S(1)}, u32[]{:S(2)}, u32[]{:S(2)}) collective-permute-start(bf16[1,80,512]{2,1,0:T(8,128)(2,1)S(1)} %get-tuple-element.159), channel_id=1, source_target_pairs={{0,24},{2,26},{4,28},{6,30},{8,16},{10,18},{12,20},{14,22},{16,8},... | collective-permute-start | bytes 245768 | tf_op jit(solution)/shard_map/ppermute | solution.py:842
  206.5 9.3 %collective-permute-start.19 = (bf16[1,80,512]{2,1,0:T(8,128)(2,1)S(1)}, bf16[1,80,512]{2,1,0:T(8,128)(2,1)S(1)}, u32[]{:S(2)}, u32[]{:S(2)}) collective-permute-start(bf16[1,80,512]{2,1,0:T(8,128)(2,1)S(1)} %get-tuple-element.160), channel_id=1, source_target_pairs={{0,16},{2,18},{4,20},{6,22},{8,24},{10,26},{12,28},{14,30},{16,0},... | collective-permute-start | bytes 245768 | tf_op jit(solution)/shard_map/ppermute | solution.py:842
  210.5 5.4 %collective-permute-start.18 = (bf16[1,80,512]{2,1,0:T(8,128)(2,1)S(1)}, bf16[1,80,512]{2,1,0:T(8,128)(2,1)S(1)}, u32[]{:S(2)}, u32[]{:S(2)}) collective-permute-start(bf16[1,80,512]{2,1,0:T(8,128)(2,1)S(1)} %get-tuple-element.158), channel_id=1, source_target_pairs={{0,8},{2,10},{4,12},{6,14},{8,0},{10,2},{12,4},{14,6},{16,24},{18,... | collective-permute-start | bytes 245768 | tf_op jit(solution)/shard_map/ppermute | solution.py:842
  216.0 8.7 %collective-permute-start.24 = (bf16[48,1536]{1,0:T(8,128)(2,1)S(1)}, bf16[48,1536]{1,0:T(8,128)(2,1)S(1)}, u32[]{:S(2)}, u32[]{:S(2)}) collective-permute-start(bf16[48,1536]{1,0:T(8,128)(2,1)S(1)} %maximum_maximum_fusion), channel_id=1, source_target_pairs={{0,1},{1,0},{2,3},{3,2},{4,5},{5,4},{6,7},{7,6},{8,9},{9,8},{10,11... | collective-permute-start | bytes 442376 | tf_op jit(solution)/shard_map/ppermute | solution.py:1035
  216.9 7.2 %collective-permute-start.25 = (bf16[32,1024]{1,0:T(8,128)(2,1)S(1)}, bf16[32,1024]{1,0:T(8,128)(2,1)S(1)}, u32[]{:S(2)}, u32[]{:S(2)}) collective-permute-start(bf16[32,1024]{1,0:T(8,128)(2,1)S(1)} %fusion.3), channel_id=1, source_target_pairs={{0,0},{2,1},{4,2},{6,3},{8,4},{10,5},{12,6},{14,7},{16,8},{18,9},{... | collective-permute-start | bytes 196616 | tf_op jit(solution)/shard_map/ppermute | solution.py:1034
  (9 other events, 13.1 us)

commit v2 on v1

--- a/solution.py
+++ b/solution.py
@@ -35,6 +35,10 @@
 
 def in_hbm(shape, dtype):
     return pltpu.HBM(tuple(shape), dtype)
+
+
+def stay(x):
+    return pltpu.with_memory_space_constraint(x, pltpu.HBM)
 
 
 def dot_nn(a, b):
@@ -953,15 +957,15 @@
     info = after(info, qkv)
     normed, hidden, slope, expanded_their = mlp_forward_call(info, plan, tokens_their, gain, shift, normed, hidden)
     info = after(info, slope)
-    grads, *down = down_grad_call(info, plan, hidden, grads_own, cotangent_their)
+    grads, *down = down_grad_call(info, plan, stay(hidden), grads_own, cotangent_their)
     down = Reduction(*pieces_of(down, order), low_first, n_dp)
     info = after(info, grads)
-    gn_their, inner, *up = mlp_back_call(info, plan, normed, slope, grads, gb_own)
+    gn_their, inner, *up = mlp_back_call(info, plan, normed, stay(slope), grads, stay(gb_own))
 
     up = Reduction(*pieces_of(up, plan["halved"]), halvings, n_dp)
     info = after(info, *down.land(gn_their), *up.land(gn_their))
     qkv = qkv_half_call(their, info, 1, normed, qkv_weight, cosine, sine, qkv)
-    context, qe = attend_call(info, qkv)
+    context, qe = attend_call(info, stay(qkv))
     out_their = out_call(their, info, context, proj_weight, expanded_their)
 
     info = after(info, *down.land(out_their))

time: 230 us -> 227 us (0.987)
  local copies, waits for them, and re-layouts: 14.3 us -> 10.2 us
    unnamed x62 -> x54, local copies, waits for them, and re-layouts: 10.9 us -> 6.79 us
  transfers between devices with their start and end apart: 26 -> 26, of which waited for: 9 -> 9; matrix products, arithmetic and copies ran while one was open for 7% -> 7% of each run, Pallas kernels for 57% -> 58%
where the time goes in v2:
time: 227 us; the launch traced here: 223 us
  Pallas kernels  146 us (64%)
  starting transfers between devices  29.8 us (13%)
  waiting for transfers between devices  21.7 us (10%)
  other arithmetic  14.3 us (6%)
  local copies, waits for them, and re-layouts  10.2 us (4%)
    ppermute x19, starting transfers between devices, start(): lax.ppermute(part, 'dp', [(i, i ^ offset) for i in range(self.n_dp)])  22.1 us
    pallas_call x1, Pallas kernels, attend_back_call(): pl.pallas_call(attend_back_kernel, grid_spec=pltpu.PrefetchScalarGridSpec...  19.6 us
    pallas_call x1, Pallas kernels, mlp_own_call(): pl.pallas_call(functools.partial(mlp_own_kernel, splits), grid_spec=pltpu...  19 us
    pallas_call x1, Pallas kernels, attend_call(): pl.pallas_call(attend_kernel, grid_spec=pltpu.PrefetchScalarGridSpec(num_...  17.7 us
    ppermute x19, waiting for transfers between devices, start(): lax.ppermute(part, 'dp', [(i, i ^ offset) for i in range(self.n_dp)])  15.7 us
    pallas_call x1, Pallas kernels, mlp_back_call(): pl.pallas_call(functools.partial(mlp_back_kernel, splits, pieces), grid_s...  15.6 us
    pallas_call x1, Pallas kernels, mlp_forward_call(): pl.pallas_call(functools.partial(mlp_forward_kernel, splits), grid_spec=p...  13 us
    pallas_call x2, Pallas kernels, qkv_half_call(): pl.pallas_call(qkv_half_kernel, grid_spec=pltpu.PrefetchScalarGridSpec(nu...  11.8 us
  transfers between devices with their start and end apart: 26, of which 9 were waited for; matrix products, arithmetic and copies ran while one was open for 7% of the time, Pallas kernels for 58%

profile of v2, /device:TPU:11, one launch (start us, length us, event | category | flops | bytes accessed | tf_op | source)
XLA Modules:
  0.0 223.3 jit_solution(14364769353664223278)
XLA Ops:
  1.0 1.2 collective-permute-start.1
  5.9 1.2 copy-done.1
  7.1 1.2 copy-done.15
  8.3 19.0 %mlp_own.1 = (bf16[1024,1024]{1,0:T(8,128)(2,1)S(1)}, bf16[1024,2048]{1,0:T(8,128)(2,1)}, bf16[512,1024]{1,0:T(8,128)(2,1)}, bf16[512,2048]{1,0:T(8,128)(2,1)}, ...) custom-call(s32[2]{0:T(128)S(1)} %pad_add_fusion.info_ref, s32[4]{0:T(128)S(1)} %get-tuple-element.177.cls_ref, ...), custom_call_target="tpu_custom_call" | custom-call | flops 8589934 | bytes 14680 | tf_op jit(solution)/shard_map/mlp_own/pallas_call | solution.py:328
  27.6 6.0 %qkv.2.refs_0_ = bf16[3,1024,512]{2,1,0:T(8,128)(2,1)} custom-call(s32[1]{0:T(128)} %bitcast.place_ref, s32[2]{0:T(128)S(1)} %pad_add_fusion.info_ref, bf16[1024,1024]{1,0:T(8,128)(2,1)S(1)} %get-tuple-element.74.x_ref.refs_12_, bf16[1024,3072]{1,0:T(8,128)(2,1)} %wv_ref.3, f32[1024,128]{1,0:T(8,128)S(1)} %bitcast.27, f32[1024,128]{1,0:T(8,128)S(1)} %negate_select_fusion.sin_ref), custom_call_target="tpu_custom_call" | custom-call | flops 1610612 | bytes 5767 | tf_op jit(solution)/shard_map/qkv/pallas_call | solution.py:552
  33.6 13.0 %mlp_forward.1 = (bf16[1024,1024]{1,0:T(8,128)(2,1)S(1)}, bf16[1024,2048]{1,0:T(8,128)(2,1)}, bf16[512,2048]{1,0:T(8,128)(2,1)}, f32[512,1024]{1,0:T(8,128)}) custom-call(s32[2]{0:T(128)S(1)} %pad_add_fusion.info_ref, s32[4]{0:T(128)S(1)} %get-tuple-element.177.cls_ref, ...), custom_call_target="tpu_custom_call", output_to_operand_aliasing={{0}: (17, {}), {1}: (18, {})} | custom-call | flops 4294967 | bytes 14680 | tf_op jit(solution)/shard_map/mlp_forward/pallas_call | solution.py:379
  47.5 10.2 %down_grad.1 = (bf16[1024,1024]{1,0:T(8,128)(2,1)}, bf16[8,128,1024]{2,1,0:T(8,128)(2,1)}, bf16[8,128,1024]{2,1,0:T(8,128)(2,1)}) custom-call(s32[2]{0:T(128)S(1)} %pad_add_fusion.info_ref, s32[4]{0:T(128)S(1)} %get-tuple-element.177.cls_ref, s32[4]{0:T(128)S(1)} %get-tuple-element.176.sub_ref, bf16[1024,2048]{1,0:T(8,128)(2,1)} %get-tuple-element.81.h_ref, ...), custom_call_target="tpu_custom_call" | custom-call | flops 4294967 | bytes 12582 | tf_op jit(solution)/shard_map/down_grad/pallas_call | solution.py:450
  57.7 1.5 collective-permute-start.2
  59.3 1.6 copy-done.5
  60.9 15.6 %mlp_back.1 = (f32[512,1024]{1,0:T(8,128)}, f32[1,2048]{1,0:T(1,128)S(1)}, bf16[8,64,2048]{2,1,0:T(8,128)(2,1)}, bf16[8,64,2048]{2,1,0:T(8,128)(2,1)}) custom-call(s32[2]{0:T(128)S(1)} %pad_add_fusion.info_ref, s32[4]{0:T(128)S(1)} %get-tuple-element.177.cls_ref, s32[16]{0:T(128)S(1)} %get-tuple-element.173.ord_ref, ...), custom_call_target="tpu_custom_call" | custom-call | flops 8589934 | bytes 23068 | tf_op jit(solution)/shard_map/mlp_back/pallas_call | solution.py:505
  76.5 2.4 %add_convert_fusion.2 = (bf16[4,128,1024]{2,1,0:T(8,128)(2,1)}, bf16[4,128,1024]{2,1,0:T(8,128)(2,1)}) fusion(bf16[8,128,1024]{2,1,0:T(8,128)(2,1)S(1)} %collective-permute-done.2, bf16[8,128,1024]{2,1,0:T(8,128)(2,1)S(1)} %copy-done.21), kind=kLoop, calls=%fused_computation.2 | loop fusion | flops 4194304 | bytes 6291456 | tf_op jit(solution)/shard_map/convert_element_type | solution.py:865
  78.9 1.2 collective-permute-start.4
  80.9 2.2 add_convert_fusion
  83.1 1.2 collective-permute-start.5
  84.3 5.9 %qkv.3.q_ref.k_ref.v_ref = bf16[3,1024,512]{2,1,0:T(8,128)(2,1)} custom-call(s32[1]{0:T(128)} %bitcast.3.place_ref, s32[2]{0:T(128)S(1)} %pad_add_fusion.info_ref, bf16[1024,1024]{1,0:T(8,128)(2,1)S(1)} %get-tuple-element.86.x_ref, bf16[1024,3072]{1,0:T(8,128)(2,1)} %wv_ref.3, f32[1024,128]{1,0:T(8,128)S(1)} %bitcast.28, ...), custom_call_target="tpu_custom_call", output_to_operand_aliasing={{}: (6, {})} | custom-call | flops 1610612 | bytes 5767 | tf_op jit(solution)/shard_map/qkv/pallas_call | solution.py:552
  90.1 17.7 %attend.1 = (bf16[1024,512]{1,0:T(8,128)(2,1)}, bf16[8,1024,128]{2,1,0:T(8,128)(2,1)}) custom-call(s32[2]{0:T(128)S(1)} %pad_add_fusion.info_ref, bf16[3,1024,512]{2,1,0:T(8,128)(2,1)} %qkv.3.q_ref.k_ref.v_ref, bf16[3,1024,512]{2,1,0:T(8,128)(2,1)} %qkv.3.q_ref.k_ref.v_ref, bf16[3,1024,512]{2,1,0:T(8,128)(2,1)} %qkv.3.q_ref.k_ref.v_ref), custom_call_target="tpu_custom_call" | custom-call | flops 10737418 | bytes 3145 | tf_op jit(solution)/shard_map/attend/pallas_call | solution.py:145
  107.8 1.2 copy-done.3
  109.1 3.5 %send_out.1 = bf16[512,1024]{1,0:T(8,128)(2,1)} custom-call(s32[1]{0:T(128)} %bitcast.3.place_ref, s32[2]{0:T(128)S(1)} %pad_add_fusion.info_ref, bf16[1024,512]{1,0:T(8,128)(2,1)S(1)} %copy-done.3, bf16[1024,1024]{1,0:T(8,128)(2,1)} %w_ref.9, f32[512,1024]{1,0:T(8,128)S(1)} %copy-done.12), custom_call_target="tpu_custom_call" | custom-call | flops 536870 | bytes 5242 | tf_op jit(solution)/shard_map/send_out/pallas_call | solution.py:587
  112.9 1.8 add_convert_fusion.12
  114.7 1.3 collective-permute-start.9
  116.0 1.1 collective-permute-start.8
  117.1 1.1 collective-permute-start.7
  118.3 6.3 %proj_back.1 = (bf16[1024,512]{1,0:T(8,128)(2,1)}, bf16[8,32,1024]{2,1,0:T(8,128)(2,1)}, bf16[8,32,1024]{2,1,0:T(8,128)(2,1)}) custom-call(s32[2]{0:T(128)S(1)} %pad_add_fusion.info_ref, s32[16]{0:T(128)S(1)} %get-tuple-element.172.ord_ref, bf16[1024,1024]{1,0:T(8,128)(2,1)S(1)} %copy-done.6, bf16[1024,512]{1,0:T(8,128)(2,1)S(1)} %copy-done.4, ...), custom_call_target="tpu_custom_call" | custom-call | flops 2147483 | bytes 6291 | tf_op jit(solution)/shard_map/proj_back/pallas_call | solution.py:641
  124.6 1.4 collective-permute-done.5
  126.0 1.6 add_convert_fusion.6
  127.8 1.2 copy-done.16
  129.0 19.6 %attend_back.1.own_ref.their_ref.d_ref = bf16[3,1024,512]{2,1,0:T(8,128)(2,1)S(1)} custom-call(s32[2]{0:T(128)S(1)} %pad_add_fusion.info_ref, bf16[8,1024,128]{2,1,0:T(8,128)(2,1)S(1)} %copy-done.14, bf16[3,1024,512]{2,1,0:T(8,128)(2,1)S(1)} %copy-done, bf16[3,1024,512]{2,1,0:T(8,128)(2,1)S(1)} %copy-done, bf16[1024,512]{1,0:T(8,128)(2,1)S(1)} %copy-done.4, ...), custom_call_target="tpu_custom_call" | custom-call | flops 12884901 | bytes 4194 | tf_op jit(solution)/shard_map/attend_back/pallas_call | solution.py:221
  150.0 4.6 %qkv_grad.2 = (bf16[8,96,1024]{2,1,0:T(8,128)(2,1)}, bf16[8,96,1024]{2,1,0:T(8,128)(2,1)}) custom-call(s32[2]{0:T(128)S(1)} %pad_add_fusion.info_ref, s32[16]{0:T(128)S(1)} %get-tuple-element.172.ord_ref, bf16[1024,1024]{1,0:T(8,128)(2,1)S(1)} %get-tuple-element.86.x_ref, bf16[3,1024,512]{2,1,0:T(8,128)(2,1)S(1)} %attend_back.1.own_ref.their_ref.d_ref, ...), custom_call_target="tpu_custom_call" | custom-call | flops 2147483 | bytes 6291 | tf_op jit(solution)/shard_map/qkv_grad/pallas_call | solution.py:724
  154.6 1.6 collective-permute-start.11
  156.2 5.7 %grad_normed.2 = (bf16[512,1024]{1,0:T(8,128)(2,1)}, f32[2,1024]{1,0:T(2,128)S(1)}) custom-call(s32[1]{0:T(128)} %bitcast.3.place_ref, s32[2]{0:T(128)S(1)} %pad_add_fusion.info_ref, bf16[3,1024,512]{2,1,0:T(8,128)(2,1)S(1)} %attend_back.1.own_ref.their_ref.d_ref, bf16[1024,3072]{1,0:T(8,128)(2,1)} %wv_ref.3, bf16[1024,3072]{1,0:T(8,128)(2,1)} %wv_ref.3, ...), custom_call_target="tpu_custom_call" | custom-call | flops 1610612 | bytes 8912 | tf_op jit(solution)/shard_map/grad_normed/pallas_call | solution.py:770
  162.6 1.3 collective-permute-start.13
  163.9 2.3 %collective-permute-start.12 = (bf16[1,64,2048]{2,1,0:T(8,128)(2,1)S(1)}, bf16[1,64,2048]{2,1,0:T(8,128)(2,1)S(1)}, u32[]{:S(2)}, u32[]{:S(2)}) collective-permute-start(bf16[1,64,2048]{2,1,0:T(8,128)(2,1)S(1)} %get-tuple-element.156), channel_id=1, source_target_pairs={{0,16},{2,18},{4,20},{6,22},{8,24},{10,26},{12,28},{14,30},{16,0},... | collective-permute-start | bytes 786440 | tf_op jit(solution)/shard_map/ppermute | solution.py:846
  166.5 5.8 %grad_normed.3 = (f32[512,1024]{1,0:T(8,128)}, f32[2,1024]{1,0:T(2,128)S(1)}) custom-call(s32[1]{0:T(128)} %bitcast.place_ref, s32[2]{0:T(128)S(1)} %pad_add_fusion.info_ref, bf16[3,1024,512]{2,1,0:T(8,128)(2,1)S(1)} %attend_back.1.own_ref.their_ref.d_ref, bf16[1024,3072]{1,0:T(8,128)(2,1)} %wv_ref.3, bf16[1024,3072]{1,0:T(8,128)(2,1)} %wv_ref.3, ...), custom_call_target="tpu_custom_call" | custom-call | flops 1610612 | bytes 8912 | tf_op jit(solution)/shard_map/grad_normed/pallas_call | solution.py:770
  172.3 3.7 %finish_out.1 = bf16[512,1024]{1,0:T(8,128)(2,1)} custom-call(s32[1]{0:T(128)} %bitcast.place_ref, s32[2]{0:T(128)S(1)} %pad_add_fusion.info_ref, bf16[1024,512]{1,0:T(8,128)(2,1)S(1)} %copy-done.4, bf16[1024,1024]{1,0:T(8,128)(2,1)} %w_ref.9, f32[512,1024]{1,0:T(8,128)S(1)} %copy-done.13, bf16[512,1024]{1,0:T(8,128)(2,1)S(1)} %copy-done.2, ...), custom_call_target="tpu_custom_call" | custom-call | flops 536870 | bytes 5242 | tf_op jit(solution)/shard_map/finish_out/pallas_call | solution.py:587
  176.0 3.0 %qkv_grad.3 = (bf16[8,80,512]{2,1,0:T(8,128)(2,1)}, bf16[8,80,512]{2,1,0:T(8,128)(2,1)}) custom-call(s32[2]{0:T(128)S(1)} %pad_add_fusion.info_ref, s32[16]{0:T(128)S(1)} %get-tuple-element.172.ord_ref, bf16[1024,1024]{1,0:T(8,128)(2,1)S(1)} %get-tuple-element.86.x_ref, bf16[3,1024,512]{2,1,0:T(8,128)(2,1)S(1)} %attend_back.1.own_ref.their_ref.d_ref, ...), custom_call_target="tpu_custom_call" | custom-call | flops 1073741 | bytes 4194 | tf_op jit(solution)/shard_map/qkv_grad/pallas_call | solution.py:724
  179.0 3.0 %collective-permute-done.13 = bf16[4,96,1024]{2,1,0:T(8,128)(2,1)S(1)} collective-permute-done((bf16[4,96,1024]{2,1,0:T(8,128)(2,1)S(1)}, bf16[4,96,1024]{2,1,0:T(8,128)(2,1)S(1)}, u32[]{:S(2)}, u32[]{:S(2)}) %collective-permute-start.13) | collective-permute-done | bytes 786464 | tf_op jit(solution)/shard_map/ppermute | solution.py:846
  183.6 2.4 %collective-permute-start.23 = (bf16[1,96,1024]{2,1,0:T(8,128)(2,1)}, bf16[1,96,1024]{2,1,0:T(8,128)(2,1)S(1)}, u32[]{:S(2)}, u32[]{:S(2)}) collective-permute-start(bf16[1,96,1024]{2,1,0:T(8,128)(2,1)} %get-tuple-element.150), channel_id=1, source_target_pairs={{0,24},{2,26},{4,28},{6,30},{8,16},{10,18},{12,20},{14,22},{16,8},... | collective-permute-start | bytes 589832 | tf_op jit(solution)/shard_map/ppermute | solution.py:846
  187.3 3.5 %collective-permute-done.15.r_ref = bf16[512,1024]{1,0:T(8,128)(2,1)} collective-permute-done((bf16[512,1024]{1,0:T(8,128)(2,1)}, bf16[512,1024]{1,0:T(8,128)(2,1)}, u32[]{:S(2)}, u32[]{:S(2)}) %collective-permute-start.15) | collective-permute-done | bytes 1048608 | tf_op jit(solution)/shard_map/ppermute | solution.py:991
  191.0 1.4 add_convert_fusion.8
  192.9 3.5 %finish_grad.1 = f32[512,1024]{1,0:T(8,128)} custom-call(f32[512,1024]{1,0:T(8,128)S(1)} %copy-done.11, bf16[512,1024]{1,0:T(8,128)(2,1)} %collective-permute-done.15.r_ref, bf16[512,1024]{1,0:T(8,128)(2,1)S(1)} %copy-done.2, bf16[512,1024]{1,0:T(8,128)(2,1)S(1)} %copy-done.8, bf16[1,1024]{1,0:T(2,128)(2,1)S(1)} %reshape.129.gain_ref), custom_call_target="tpu_custom_call" | custom-call | flops 10485 | bytes 7340 | tf_op jit(solution)/shard_map/finish_grad/pallas_call | solution.py:826
  196.5 1.4 assemble.2
  197.9 2.1 collective-permute-done.23
  200.0 3.3 %collective-permute-done.22 = bf16[1,96,1024]{2,1,0:T(8,128)(2,1)S(1)} collective-permute-done((bf16[1,96,1024]{2,1,0:T(8,128)(2,1)S(1)}, bf16[1,96,1024]{2,1,0:T(8,128)(2,1)S(1)}, u32[]{:S(2)}, u32[]{:S(2)}) %collective-permute-start.22) | collective-permute-done | bytes 196640 | tf_op jit(solution)/shard_map/ppermute | solution.py:846
  203.7 4.0 %collective-permute-start.19 = (bf16[1,80,512]{2,1,0:T(8,128)(2,1)S(1)}, bf16[1,80,512]{2,1,0:T(8,128)(2,1)S(1)}, u32[]{:S(2)}, u32[]{:S(2)}) collective-permute-start(bf16[1,80,512]{2,1,0:T(8,128)(2,1)S(1)} %get-tuple-element.160), channel_id=1, source_target_pairs={{0,16},{2,18},{4,20},{6,22},{8,24},{10,26},{12,28},{14,30},{16,0},... | collective-permute-start | bytes 245768 | tf_op jit(solution)/shard_map/ppermute | solution.py:846
  207.8 5.2 %collective-permute-done.19 = bf16[1,80,512]{2,1,0:T(8,128)(2,1)S(1)} collective-permute-done((bf16[1,80,512]{2,1,0:T(8,128)(2,1)S(1)}, bf16[1,80,512]{2,1,0:T(8,128)(2,1)S(1)}, u32[]{:S(2)}, u32[]{:S(2)}) %collective-permute-start.19) | collective-permute-done | bytes 81952 | tf_op jit(solution)/shard_map/ppermute | solution.py:846
  213.8 4.8 %collective-permute-start.25 = (bf16[32,1024]{1,0:T(8,128)(2,1)S(1)}, bf16[32,1024]{1,0:T(8,128)(2,1)S(1)}, u32[]{:S(2)}, u32[]{:S(2)}) collective-permute-start(bf16[32,1024]{1,0:T(8,128)(2,1)S(1)} %fusion.3), channel_id=1, source_target_pairs={{0,0},{2,1},{4,2},{6,3},{8,4},{10,5},{12,6},{14,7},{16,8},{18,9},{... | collective-permute-start | bytes 196616 | tf_op jit(solution)/shard_map/ppermute | solution.py:1038
  219.2 1.5 collective-permute-done.25
  222.0 1.3 assemble.3
  (123 shorter events, 15.1 us)
Async XLA Ops:
  0.6 32.9 %collective-permute-start = (bf16[512,1024]{1,0:T(8,128)(2,1)}, bf16[512,1024]{1,0:T(8,128)(2,1)}, u32[]{:S(2)}, u32[]{:S(2)}) collective-permute-start(bf16[512,1024]{1,0:T(8,128)(2,1)} %t_ref.7), channel_id=1, source_target_pairs={{0,1},{1,0},{2,3},{3,2},{4,5},{5,4},{6,7},{7,6},{8,9},{9,8},{10,11... | collective-permute-start | bytes 3145736 | tf_op jit(solution)/shard_map/ppermute | solution.py:903
  1.0 46.6 %collective-permute-start.1 = (bf16[512,1024]{1,0:T(8,128)(2,1)}, bf16[512,1024]{1,0:T(8,128)(2,1)}, u32[]{:S(2)}, u32[]{:S(2)}) collective-permute-start(bf16[512,1024]{1,0:T(8,128)(2,1)} %c_ref.1), channel_id=1, source_target_pairs={{0,1},{1,0},{2,3},{3,2},{4,5},{5,4},{6,7},{7,6},{8,9},{9,8},{10,11... | collective-permute-start | bytes 3145736 | tf_op jit(solution)/shard_map/ppermute | solution.py:904
  33.6 14.0 %copy-start.7 = (bf16[512,1024]{1,0:T(8,128)(2,1)S(1)}, bf16[512,1024]{1,0:T(8,128)(2,1)}, u32[]{:S(2)}) copy-start(bf16[512,1024]{1,0:T(8,128)(2,1)} %get-tuple-element.82.go_ref.g_ref) | copy-start | bytes 3145732
  47.5 11.8 %copy-start.25 = (s32[16]{0:T(128)S(1)}, s32[16]{0:T(128)}, u32[]{:S(2)}) copy-start(s32[16]{0:T(128)} %constant.77.clone) | copy-start | bytes 196
  47.5 11.8 %copy-start.26 = (s32[16]{0:T(128)S(1)}, s32[16]{0:T(128)}, u32[]{:S(2)}) copy-start(s32[16]{0:T(128)} %constant.79.clone) | copy-start | bytes 196
  57.7 18.8 %collective-permute-start.2 = (bf16[8,128,1024]{2,1,0:T(8,128)(2,1)}, bf16[8,128,1024]{2,1,0:T(8,128)(2,1)S(1)}, u32[]{:S(2)}, u32[]{:S(2)}) collective-permute-start(bf16[8,128,1024]{2,1,0:T(8,128)(2,1)} %get-tuple-element.90), channel_id=1, source_target_pairs={{0,2},{2,0},{4,6},{6,4},{8,10},{10,8},{12,14},{14,12},{16,18},{18,... | collective-permute-start | bytes 6291464 | tf_op jit(solution)/shard_map/ppermute | solution.py:846
  59.3 1.6 copy-start.5
  60.9 15.7 %copy-start.21 = (bf16[8,128,1024]{2,1,0:T(8,128)(2,1)S(1)}, bf16[8,128,1024]{2,1,0:T(8,128)(2,1)}, u32[]{:S(2)}) copy-start(bf16[8,128,1024]{2,1,0:T(8,128)(2,1)} %get-tuple-element.89) | copy-start | bytes 6291460
  76.4 4.4 %collective-permute-start.3 = (bf16[8,64,2048]{2,1,0:T(8,128)(2,1)}, bf16[8,64,2048]{2,1,0:T(8,128)(2,1)S(1)}, u32[]{:S(2)}, u32[]{:S(2)}) collective-permute-start(bf16[8,64,2048]{2,1,0:T(8,128)(2,1)} %get-tuple-element.93), channel_id=1, source_target_pairs={{0,2},{2,0},{4,6},{6,4},{8,10},{10,8},{12,14},{14,12},{16,18},{18,... | collective-permute-start | bytes 6291464 | tf_op jit(solution)/shard_map/ppermute | solution.py:846
  76.5 4.4 %copy-start.22 = (bf16[8,64,2048]{2,1,0:T(8,128)(2,1)S(1)}, bf16[8,64,2048]{2,1,0:T(8,128)(2,1)}, u32[]{:S(2)}) copy-start(bf16[8,64,2048]{2,1,0:T(8,128)(2,1)} %get-tuple-element.92) | copy-start | bytes 6291460
  78.9 34.0 %collective-permute-start.4 = (bf16[4,128,1024]{2,1,0:T(8,128)(2,1)}, bf16[4,128,1024]{2,1,0:T(8,128)(2,1)}, u32[]{:S(2)}, u32[]{:S(2)}) collective-permute-start(bf16[4,128,1024]{2,1,0:T(8,128)(2,1)} %get-tuple-element.140), channel_id=1, source_target_pairs={{0,4},{2,6},{4,0},{6,2},{8,12},{10,14},{12,8},{14,10},{16,20},{18,... | collective-permute-start | bytes 3145736 | tf_op jit(solution)/shard_map/ppermute | solution.py:846
  83.1 42.9 %collective-permute-start.5 = (bf16[4,64,2048]{2,1,0:T(8,128)(2,1)}, bf16[4,64,2048]{2,1,0:T(8,128)(2,1)}, u32[]{:S(2)}, u32[]{:S(2)}) collective-permute-start(bf16[4,64,2048]{2,1,0:T(8,128)(2,1)} %get-tuple-element.138), channel_id=1, source_target_pairs={{0,4},{2,6},{4,0},{6,2},{8,12},{10,14},{12,8},{14,10},{16,20},{18,... | collective-permute-start | bytes 3145736 | tf_op jit(solution)/shard_map/ppermute | solution.py:846
  90.1 17.7 %copy-start.12 = (f32[512,1024]{1,0:T(8,128)S(1)}, f32[512,1024]{1,0:T(8,128)}, u32[]{:S(2)}) copy-start(f32[512,1024]{1,0:T(8,128)} %get-tuple-element.96.e_ref) | copy-start | bytes 6291460
  109.1 3.8 %copy-start.20 = (bf16[4,128,1024]{2,1,0:T(8,128)(2,1)S(1)}, bf16[4,128,1024]{2,1,0:T(8,128)(2,1)}, u32[]{:S(2)}) copy-start(bf16[4,128,1024]{2,1,0:T(8,128)(2,1)} %get-tuple-element.97) | copy-start | bytes 3145732
  112.6 5.7 %copy-start.4 = (bf16[1024,512]{1,0:T(8,128)(2,1)S(1)}, bf16[1024,512]{1,0:T(8,128)(2,1)}, u32[]{:S(2)}) copy-start(bf16[1024,512]{1,0:T(8,128)(2,1)} %get-tuple-element.95.c_ref.o_ref) | copy-start | bytes 3145732
  112.6 5.7 %copy-start.6 = (bf16[1024,1024]{1,0:T(8,128)(2,1)S(1)}, bf16[1024,1024]{1,0:T(8,128)(2,1)}, u32[]{:S(2)}) copy-start(bf16[1024,1024]{1,0:T(8,128)(2,1)} %get-tuple-element.83.g_ref) | copy-start | bytes 6291460
  112.6 37.2 %collective-permute-start.6 = (bf16[512,1024]{1,0:T(8,128)(2,1)}, bf16[512,1024]{1,0:T(8,128)(2,1)S(1)}, u32[]{:S(2)}, u32[]{:S(2)}) collective-permute-start(bf16[512,1024]{1,0:T(8,128)(2,1)} %send_out.1), channel_id=1, source_target_pairs={{0,1},{1,0},{2,3},{3,2},{4,5},{5,4},{6,7},{7,6},{8,9},{9,8},{10,11... | collective-permute-start | bytes 3145736 | tf_op jit(solution)/shard_map/ppermute | solution.py:972
  114.7 34.0 %collective-permute-start.9 = (bf16[1,128,1024]{2,1,0:T(8,128)(2,1)S(1)}, bf16[1,128,1024]{2,1,0:T(8,128)(2,1)S(1)}, u32[]{:S(2)}, u32[]{:S(2)}) collective-permute-start(bf16[1,128,1024]{2,1,0:T(8,128)(2,1)S(1)} %get-tuple-element.146), channel_id=1, source_target_pairs={{0,24},{2,26},{4,28},{6,30},{8,16},{10,18},{12,20},{14,22},{16,8},... | collective-permute-start | bytes 786440 | tf_op jit(solution)/shard_map/ppermute | solution.py:846
  116.0 32.6 %collective-permute-start.8 = (bf16[1,128,1024]{2,1,0:T(8,128)(2,1)S(1)}, bf16[1,128,1024]{2,1,0:T(8,128)(2,1)S(1)}, u32[]{:S(2)}, u32[]{:S(2)}) collective-permute-start(bf16[1,128,1024]{2,1,0:T(8,128)(2,1)S(1)} %get-tuple-element.147), channel_id=1, source_target_pairs={{0,16},{2,18},{4,20},{6,22},{8,24},{10,26},{12,28},{14,30},{16,0},... | collective-permute-start | bytes 786440 | tf_op jit(solution)/shard_map/ppermute | solution.py:846
  117.1 31.5 %collective-permute-start.7 = (bf16[1,128,1024]{2,1,0:T(8,128)(2,1)S(1)}, bf16[1,128,1024]{2,1,0:T(8,128)(2,1)S(1)}, u32[]{:S(2)}, u32[]{:S(2)}) collective-permute-start(bf16[1,128,1024]{2,1,0:T(8,128)(2,1)S(1)} %get-tuple-element.148), channel_id=1, source_target_pairs={{0,8},{2,10},{4,12},{6,14},{8,0},{10,2},{12,4},{14,6},{16,24},{18,... | collective-permute-start | bytes 786440 | tf_op jit(solution)/shard_map/ppermute | solution.py:846
  118.3 7.7 %copy-start.19 = (bf16[4,64,2048]{2,1,0:T(8,128)(2,1)S(1)}, bf16[4,64,2048]{2,1,0:T(8,128)(2,1)}, u32[]{:S(2)}) copy-start(bf16[4,64,2048]{2,1,0:T(8,128)(2,1)} %get-tuple-element.100) | copy-start | bytes 3145732
  118.3 9.5 %copy-start.14 = (bf16[8,1024,128]{2,1,0:T(8,128)(2,1)S(1)}, bf16[8,1024,128]{2,1,0:T(8,128)(2,1)}, u32[]{:S(2)}) copy-start(bf16[8,1024,128]{2,1,0:T(8,128)(2,1)} %get-tuple-element.102.qe_ref) | copy-start | bytes 6291460
  124.6 3.2 %copy-start = (bf16[3,1024,512]{2,1,0:T(8,128)(2,1)S(1)}, bf16[3,1024,512]{2,1,0:T(8,128)(2,1)}, u32[]{:S(2)}) copy-start(bf16[3,1024,512]{2,1,0:T(8,128)(2,1)} %qkv.3.q_ref.k_ref.v_ref) | copy-start | bytes 9437188
  127.6 22.1 %collective-permute-start.10 = (bf16[2,64,2048]{2,1,0:T(8,128)(2,1)S(1)}, bf16[2,64,2048]{2,1,0:T(8,128)(2,1)S(1)}, u32[]{:S(2)}, u32[]{:S(2)}) collective-permute-start(bf16[2,64,2048]{2,1,0:T(8,128)(2,1)S(1)} %get-tuple-element.144), channel_id=1, source_target_pairs={{0,8},{2,10},{4,12},{6,14},{8,0},{10,2},{12,4},{14,6},{16,24},{18,... | collective-permute-start | bytes 1572872 | tf_op jit(solution)/shard_map/ppermute | solution.py:846
  148.6 1.4 copy-start.18
  150.0 6.2 %copy-start.10 = (f32[512,1024]{1,0:T(8,128)S(1)}, f32[512,1024]{1,0:T(8,128)}, u32[]{:S(2)}) copy-start(f32[512,1024]{1,0:T(8,128)} %get-tuple-element.88.base_ref) | copy-start | bytes 6291460
  154.6 7.3 %collective-permute-start.11 = (bf16[8,96,1024]{2,1,0:T(8,128)(2,1)}, bf16[8,96,1024]{2,1,0:T(8,128)(2,1)S(1)}, u32[]{:S(2)}, u32[]{:S(2)}) collective-permute-start(bf16[8,96,1024]{2,1,0:T(8,128)(2,1)} %get-tuple-element.109), channel_id=1, source_target_pairs={{0,2},{2,0},{4,6},{6,4},{8,10},{10,8},{12,14},{14,12},{16,18},{18,... | collective-permute-start | bytes 4718600 | tf_op jit(solution)/shard_map/ppermute | solution.py:846
  156.2 5.8 %copy-start.23 = (bf16[8,96,1024]{2,1,0:T(8,128)(2,1)S(1)}, bf16[8,96,1024]{2,1,0:T(8,128)(2,1)}, u32[]{:S(2)}) copy-start(bf16[8,96,1024]{2,1,0:T(8,128)(2,1)} %get-tuple-element.112) | copy-start | bytes 4718596
  161.9 4.3 %copy-start.24 = (bf16[1024]{0:T(1024)(128)(2,1)S(1)}, bf16[1024]{0:T(1024)(128)(2,1)}, u32[]{:S(2)}) copy-start(bf16[1024]{0:T(1024)(128)(2,1)} %param.23) | copy-start | bytes 6148
  161.9 4.6 %copy-start.2 = (bf16[512,1024]{1,0:T(8,128)(2,1)S(1)}, bf16[512,1024]{1,0:T(8,128)(2,1)}, u32[]{:S(2)}) copy-start(bf16[512,1024]{1,0:T(8,128)(2,1)} %t_ref.7) | copy-start | bytes 3145732
  161.9 4.6 %copy-start.9 = (f32[512,1024]{1,0:T(8,128)S(1)}, f32[512,1024]{1,0:T(8,128)}, u32[]{:S(2)}) copy-start(f32[512,1024]{1,0:T(8,128)} %get-tuple-element.114.base_ref) | copy-start | bytes 6291460
  162.6 19.3 %collective-permute-start.13 = (bf16[4,96,1024]{2,1,0:T(8,128)(2,1)S(1)}, bf16[4,96,1024]{2,1,0:T(8,128)(2,1)S(1)}, u32[]{:S(2)}, u32[]{:S(2)}) collective-permute-start(bf16[4,96,1024]{2,1,0:T(8,128)(2,1)S(1)} %get-tuple-element.142), channel_id=1, source_target_pairs={{0,4},{2,6},{4,0},{6,2},{8,12},{10,14},{12,8},{14,10},{16,20},{18,... | collective-permute-start | bytes 2359304 | tf_op jit(solution)/shard_map/ppermute | solution.py:846
  163.9 15.0 %collective-permute-start.12 = (bf16[1,64,2048]{2,1,0:T(8,128)(2,1)S(1)}, bf16[1,64,2048]{2,1,0:T(8,128)(2,1)S(1)}, u32[]{:S(2)}, u32[]{:S(2)}) collective-permute-start(bf16[1,64,2048]{2,1,0:T(8,128)(2,1)S(1)} %get-tuple-element.156), channel_id=1, source_target_pairs={{0,16},{2,18},{4,20},{6,22},{8,24},{10,26},{12,28},{14,30},{16,0},... | collective-permute-start | bytes 786440 | tf_op jit(solution)/shard_map/ppermute | solution.py:846
  166.2 24.5 %collective-permute-start.15 = (bf16[512,1024]{1,0:T(8,128)(2,1)}, bf16[512,1024]{1,0:T(8,128)(2,1)}, u32[]{:S(2)}, u32[]{:S(2)}) collective-permute-start(bf16[512,1024]{1,0:T(8,128)(2,1)} %get-tuple-element.111), channel_id=1, source_target_pairs={{0,1},{1,0},{2,3},{3,2},{4,5},{5,4},{6,7},{7,6},{8,9},{9,8},{10,11... | collective-permute-start | bytes 3145736 | tf_op jit(solution)/shard_map/ppermute | solution.py:991
  166.5 5.8 %copy-start.13 = (f32[512,1024]{1,0:T(8,128)S(1)}, f32[512,1024]{1,0:T(8,128)}, u32[]{:S(2)}) copy-start(f32[512,1024]{1,0:T(8,128)} %get-tuple-element.117.e_ref) | copy-start | bytes 6291460
  179.0 13.9 %copy-start.8 = (bf16[512,1024]{1,0:T(8,128)(2,1)S(1)}, bf16[512,1024]{1,0:T(8,128)(2,1)}, u32[]{:S(2)}) copy-start(bf16[512,1024]{1,0:T(8,128)(2,1)} %get-tuple-element.82.go_ref.g_ref) | copy-start | bytes 3145732
  182.9 8.1 %collective-permute-start.16 = (bf16[8,80,512]{2,1,0:T(8,128)(2,1)}, bf16[8,80,512]{2,1,0:T(8,128)(2,1)}, u32[]{:S(2)}, u32[]{:S(2)}) collective-permute-start(bf16[8,80,512]{2,1,0:T(8,128)(2,1)} %get-tuple-element.131), channel_id=1, source_target_pairs={{0,2},{2,0},{4,6},{6,4},{8,10},{10,8},{12,14},{14,12},{16,18},{18,... | collective-permute-start | bytes 1966088 | tf_op jit(solution)/shard_map/ppermute | solution.py:846
  183.6 9.3 %copy-start.11 = (f32[512,1024]{1,0:T(8,128)S(1)}, f32[512,1024]{1,0:T(8,128)}, u32[]{:S(2)}) copy-start(f32[512,1024]{1,0:T(8,128)} %get-tuple-element.115.gn_ref) | copy-start | bytes 6291460
  183.6 16.3 %collective-permute-start.23 = (bf16[1,96,1024]{2,1,0:T(8,128)(2,1)}, bf16[1,96,1024]{2,1,0:T(8,128)(2,1)S(1)}, u32[]{:S(2)}, u32[]{:S(2)}) collective-permute-start(bf16[1,96,1024]{2,1,0:T(8,128)(2,1)} %get-tuple-element.150), channel_id=1, source_target_pairs={{0,24},{2,26},{4,28},{6,30},{8,16},{10,18},{12,20},{14,22},{16,8},... | collective-permute-start | bytes 589832 | tf_op jit(solution)/shard_map/ppermute | solution.py:846
  186.1 17.2 %collective-permute-start.22 = (bf16[1,96,1024]{2,1,0:T(8,128)(2,1)S(1)}, bf16[1,96,1024]{2,1,0:T(8,128)(2,1)S(1)}, u32[]{:S(2)}, u32[]{:S(2)}) collective-permute-start(bf16[1,96,1024]{2,1,0:T(8,128)(2,1)S(1)} %get-tuple-element.151), channel_id=1, source_target_pairs={{0,16},{2,18},{4,20},{6,22},{8,24},{10,26},{12,28},{14,30},{16,0},... | collective-permute-start | bytes 589832 | tf_op jit(solution)/shard_map/ppermute | solution.py:846
  187.0 16.2 %collective-permute-start.21 = (bf16[1,96,1024]{2,1,0:T(8,128)(2,1)S(1)}, bf16[1,96,1024]{2,1,0:T(8,128)(2,1)S(1)}, u32[]{:S(2)}, u32[]{:S(2)}) collective-permute-start(bf16[1,96,1024]{2,1,0:T(8,128)(2,1)S(1)} %get-tuple-element.152), channel_id=1, source_target_pairs={{0,8},{2,10},{4,12},{6,14},{8,0},{10,2},{12,4},{14,6},{16,24},{18,... | collective-permute-start | bytes 589832 | tf_op jit(solution)/shard_map/ppermute | solution.py:846
  190.8 5.7 %collective-permute-start.14 = (bf16[32,2048]{1,0:T(8,128)(2,1)S(1)}, bf16[32,2048]{1,0:T(8,128)(2,1)S(1)}, u32[]{:S(2)}, u32[]{:S(2)}) collective-permute-start(bf16[32,2048]{1,0:T(8,128)(2,1)S(1)} %dynamic-slice_convert_fusion), channel_id=1, source_target_pairs={{0,1},{1,0},{2,3},{3,2},{4,5},{5,4},{6,7},{7,6},{8,9},{9,8},{10,11... | collective-permute-start | bytes 393224 | tf_op jit(solution)/shard_map/ppermute | solution.py:1017
  192.5 10.9 %collective-permute-start.17 = (bf16[4,80,512]{2,1,0:T(8,128)(2,1)S(1)}, bf16[4,80,512]{2,1,0:T(8,128)(2,1)S(1)}, u32[]{:S(2)}, u32[]{:S(2)}) collective-permute-start(bf16[4,80,512]{2,1,0:T(8,128)(2,1)S(1)} %get-tuple-element.154), channel_id=1, source_target_pairs={{0,4},{2,6},{4,0},{6,2},{8,12},{10,14},{12,8},{14,10},{16,20},{18,... | collective-permute-start | bytes 983048 | tf_op jit(solution)/shard_map/ppermute | solution.py:846
  203.5 4.4 %collective-permute-start.20 = (bf16[1,80,512]{2,1,0:T(8,128)(2,1)S(1)}, bf16[1,80,512]{2,1,0:T(8,128)(2,1)S(1)}, u32[]{:S(2)}, u32[]{:S(2)}) collective-permute-start(bf16[1,80,512]{2,1,0:T(8,128)(2,1)S(1)} %get-tuple-element.159), channel_id=1, source_target_pairs={{0,24},{2,26},{4,28},{6,30},{8,16},{10,18},{12,20},{14,22},{16,8},... | collective-permute-start | bytes 245768 | tf_op jit(solution)/shard_map/ppermute | solution.py:846
  203.7 9.3 %collective-permute-start.19 = (bf16[1,80,512]{2,1,0:T(8,128)(2,1)S(1)}, bf16[1,80,512]{2,1,0:T(8,128)(2,1)S(1)}, u32[]{:S(2)}, u32[]{:S(2)}) collective-permute-start(bf16[1,80,512]{2,1,0:T(8,128)(2,1)S(1)} %get-tuple-element.160), channel_id=1, source_target_pairs={{0,16},{2,18},{4,20},{6,22},{8,24},{10,26},{12,28},{14,30},{16,0},... | collective-permute-start | bytes 245768 | tf_op jit(solution)/shard_map/ppermute | solution.py:846
  207.7 5.4 %collective-permute-start.18 = (bf16[1,80,512]{2,1,0:T(8,128)(2,1)S(1)}, bf16[1,80,512]{2,1,0:T(8,128)(2,1)S(1)}, u32[]{:S(2)}, u32[]{:S(2)}) collective-permute-start(bf16[1,80,512]{2,1,0:T(8,128)(2,1)S(1)} %get-tuple-element.158), channel_id=1, source_target_pairs={{0,8},{2,10},{4,12},{6,14},{8,0},{10,2},{12,4},{14,6},{16,24},{18,... | collective-permute-start | bytes 245768 | tf_op jit(solution)/shard_map/ppermute | solution.py:846
  213.3 8.1 %collective-permute-start.24 = (bf16[48,1536]{1,0:T(8,128)(2,1)S(1)}, bf16[48,1536]{1,0:T(8,128)(2,1)S(1)}, u32[]{:S(2)}, u32[]{:S(2)}) collective-permute-start(bf16[48,1536]{1,0:T(8,128)(2,1)S(1)} %maximum_maximum_fusion), channel_id=1, source_target_pairs={{0,1},{1,0},{2,3},{3,2},{4,5},{5,4},{6,7},{7,6},{8,9},{9,8},{10,11... | collective-permute-start | bytes 442376 | tf_op jit(solution)/shard_map/ppermute | solution.py:1039
  213.8 6.9 %collective-permute-start.25 = (bf16[32,1024]{1,0:T(8,128)(2,1)S(1)}, bf16[32,1024]{1,0:T(8,128)(2,1)S(1)}, u32[]{:S(2)}, u32[]{:S(2)}) collective-permute-start(bf16[32,1024]{1,0:T(8,128)(2,1)S(1)} %fusion.3), channel_id=1, source_target_pairs={{0,0},{2,1},{4,2},{6,3},{8,4},{10,5},{12,6},{14,7},{16,8},{18,9},{... | collective-permute-start | bytes 196616 | tf_op jit(solution)/shard_map/ppermute | solution.py:1038
  (5 other events, 6.1 us)

commit v3 on v2

--- a/solution.py
+++ b/solution.py
@@ -966,13 +966,13 @@
     info = after(info, *down.land(gn_their), *up.land(gn_their))
     qkv = qkv_half_call(their, info, 1, normed, qkv_weight, cosine, sine, qkv)
     context, qe = attend_call(info, stay(qkv))
-    out_their = out_call(their, info, context, proj_weight, expanded_their)
+    out_their = out_call(their, info, stay(context), proj_weight, expanded_their)
 
     info = after(info, *down.land(out_their))
     out_received = lax.ppermute(out_their, "branch", other)
     grad_context, *proj = proj_back_call(info, plan, order, grads, context, proj_weight)
     info = after(info, *up.land(grad_context))
-    dmix = attend_back_call(info, qe, qkv, context, grad_context, cosine, sine)
+    dmix = attend_back_call(info, qe, qkv, stay(context), stay(grad_context), cosine, sine)
 
     down_grad = down.finish(dmix)
     info = after(info, out_received, down_grad, *up.land(dmix))

time: 227 us -> 227 us (level)
  local copies, waits for them, and re-layouts: 10.2 us -> 7.76 us
    unnamed x54 -> x52, local copies, waits for them, and re-layouts: 6.79 us -> 4.35 us
  transfers between devices with their start and end apart: 26 -> 26, of which waited for: 9 -> 9; matrix products, arithmetic and copies ran while one was open for 7% -> 7% of each run, Pallas kernels for 58% -> 59%
where the time goes in v3:
time: 227 us; the launch traced here: 223 us
  Pallas kernels  147 us (65%)
  starting transfers between devices  29.8 us (13%)
  waiting for transfers between devices  22.4 us (10%)
  other arithmetic  14.3 us (6%)
  local copies, waits for them, and re-layouts  7.76 us (3%)
    ppermute x19, starting transfers between devices, start(): lax.ppermute(part, 'dp', [(i, i ^ offset) for i in range(self.n_dp)])  22.1 us
    pallas_call x1, Pallas kernels, attend_back_call(): pl.pallas_call(attend_back_kernel, grid_spec=pltpu.PrefetchScalarGridSpec...  20.2 us
    pallas_call x1, Pallas kernels, mlp_own_call(): pl.pallas_call(functools.partial(mlp_own_kernel, splits), grid_spec=pltpu...  19 us
    pallas_call x1, Pallas kernels, attend_call(): pl.pallas_call(attend_kernel, grid_spec=pltpu.PrefetchScalarGridSpec(num_...  17.7 us
    ppermute x19, waiting for transfers between devices, start(): lax.ppermute(part, 'dp', [(i, i ^ offset) for i in range(self.n_dp)])  16.6 us
    pallas_call x1, Pallas kernels, mlp_back_call(): pl.pallas_call(functools.partial(mlp_back_kernel, splits, pieces), grid_s...  15.5 us
    pallas_call x1, Pallas kernels, mlp_forward_call(): pl.pallas_call(functools.partial(mlp_forward_kernel, splits), grid_spec=p...  13 us
    pallas_call x2, Pallas kernels, qkv_half_call(): pl.pallas_call(qkv_half_kernel, grid_spec=pltpu.PrefetchScalarGridSpec(nu...  11.8 us
  transfers between devices with their start and end apart: 26, of which 9 were waited for; matrix products, arithmetic and copies ran while one was open for 7% of the time, Pallas kernels for 59%

profile of v3, /device:TPU:11, one launch (start us, length us, event | category | flops | bytes accessed | tf_op | source)
XLA Modules:
  0.0 222.5 jit_solution(9055040943322794669)
XLA Ops:
  1.0 1.2 collective-permute-start.1
  5.9 1.2 copy-done.1
  7.1 1.2 copy-done.15
  8.3 19.0 %mlp_own.1 = (bf16[1024,1024]{1,0:T(8,128)(2,1)S(1)}, bf16[1024,2048]{1,0:T(8,128)(2,1)}, bf16[512,1024]{1,0:T(8,128)(2,1)}, bf16[512,2048]{1,0:T(8,128)(2,1)}, ...) custom-call(s32[2]{0:T(128)S(1)} %pad_add_fusion.info_ref, s32[4]{0:T(128)S(1)} %get-tuple-element.177.cls_ref, ...), custom_call_target="tpu_custom_call" | custom-call | flops 8589934 | bytes 14680 | tf_op jit(solution)/shard_map/mlp_own/pallas_call | solution.py:328
  27.6 5.9 %qkv.2.refs_0_ = bf16[3,1024,512]{2,1,0:T(8,128)(2,1)} custom-call(s32[1]{0:T(128)} %bitcast.place_ref, s32[2]{0:T(128)S(1)} %pad_add_fusion.info_ref, bf16[1024,1024]{1,0:T(8,128)(2,1)S(1)} %get-tuple-element.74.x_ref.refs_12_, bf16[1024,3072]{1,0:T(8,128)(2,1)} %wv_ref.3, f32[1024,128]{1,0:T(8,128)S(1)} %bitcast.27, f32[1024,128]{1,0:T(8,128)S(1)} %negate_select_fusion.sin_ref), custom_call_target="tpu_custom_call" | custom-call | flops 1610612 | bytes 5767 | tf_op jit(solution)/shard_map/qkv/pallas_call | solution.py:552
  33.6 13.0 %mlp_forward.1 = (bf16[1024,1024]{1,0:T(8,128)(2,1)S(1)}, bf16[1024,2048]{1,0:T(8,128)(2,1)}, bf16[512,2048]{1,0:T(8,128)(2,1)}, f32[512,1024]{1,0:T(8,128)}) custom-call(s32[2]{0:T(128)S(1)} %pad_add_fusion.info_ref, s32[4]{0:T(128)S(1)} %get-tuple-element.177.cls_ref, ...), custom_call_target="tpu_custom_call", output_to_operand_aliasing={{0}: (17, {}), {1}: (18, {})} | custom-call | flops 4294967 | bytes 14680 | tf_op jit(solution)/shard_map/mlp_forward/pallas_call | solution.py:379
  46.5 1.0 collective-permute-done.1.c_ref
  47.5 10.2 %down_grad.1 = (bf16[1024,1024]{1,0:T(8,128)(2,1)}, bf16[8,128,1024]{2,1,0:T(8,128)(2,1)}, bf16[8,128,1024]{2,1,0:T(8,128)(2,1)}) custom-call(s32[2]{0:T(128)S(1)} %pad_add_fusion.info_ref, s32[4]{0:T(128)S(1)} %get-tuple-element.177.cls_ref, s32[4]{0:T(128)S(1)} %get-tuple-element.176.sub_ref, bf16[1024,2048]{1,0:T(8,128)(2,1)} %get-tuple-element.81.h_ref, ...), custom_call_target="tpu_custom_call" | custom-call | flops 4294967 | bytes 12582 | tf_op jit(solution)/shard_map/down_grad/pallas_call | solution.py:450
  57.7 1.5 collective-permute-start.2
  59.3 1.6 copy-done.5
  60.9 15.5 %mlp_back.1 = (f32[512,1024]{1,0:T(8,128)}, f32[1,2048]{1,0:T(1,128)S(1)}, bf16[8,64,2048]{2,1,0:T(8,128)(2,1)}, bf16[8,64,2048]{2,1,0:T(8,128)(2,1)}) custom-call(s32[2]{0:T(128)S(1)} %pad_add_fusion.info_ref, s32[4]{0:T(128)S(1)} %get-tuple-element.177.cls_ref, s32[16]{0:T(128)S(1)} %get-tuple-element.173.ord_ref, ...), custom_call_target="tpu_custom_call" | custom-call | flops 8589934 | bytes 23068 | tf_op jit(solution)/shard_map/mlp_back/pallas_call | solution.py:505
  76.5 2.4 %add_convert_fusion.2 = (bf16[4,128,1024]{2,1,0:T(8,128)(2,1)}, bf16[4,128,1024]{2,1,0:T(8,128)(2,1)}) fusion(bf16[8,128,1024]{2,1,0:T(8,128)(2,1)S(1)} %collective-permute-done.2, bf16[8,128,1024]{2,1,0:T(8,128)(2,1)S(1)} %copy-done.20), kind=kLoop, calls=%fused_computation.2 | loop fusion | flops 4194304 | bytes 6291456 | tf_op jit(solution)/shard_map/convert_element_type | solution.py:865
  78.9 1.3 collective-permute-start.4
  80.8 2.2 add_convert_fusion
  83.0 1.3 collective-permute-start.5
  84.3 5.9 %qkv.3.q_ref.k_ref.v_ref = bf16[3,1024,512]{2,1,0:T(8,128)(2,1)} custom-call(s32[1]{0:T(128)} %bitcast.3.place_ref, s32[2]{0:T(128)S(1)} %pad_add_fusion.info_ref, bf16[1024,1024]{1,0:T(8,128)(2,1)S(1)} %get-tuple-element.86.x_ref, bf16[1024,3072]{1,0:T(8,128)(2,1)} %wv_ref.3, f32[1024,128]{1,0:T(8,128)S(1)} %bitcast.28, ...), custom_call_target="tpu_custom_call", output_to_operand_aliasing={{}: (6, {})} | custom-call | flops 1610612 | bytes 5767 | tf_op jit(solution)/shard_map/qkv/pallas_call | solution.py:552
  90.2 17.7 %attend.1 = (bf16[1024,512]{1,0:T(8,128)(2,1)}, bf16[8,1024,128]{2,1,0:T(8,128)(2,1)}) custom-call(s32[2]{0:T(128)S(1)} %pad_add_fusion.info_ref, bf16[3,1024,512]{2,1,0:T(8,128)(2,1)} %qkv.3.q_ref.k_ref.v_ref, bf16[3,1024,512]{2,1,0:T(8,128)(2,1)} %qkv.3.q_ref.k_ref.v_ref, bf16[3,1024,512]{2,1,0:T(8,128)(2,1)} %qkv.3.q_ref.k_ref.v_ref), custom_call_target="tpu_custom_call" | custom-call | flops 10737418 | bytes 3145 | tf_op jit(solution)/shard_map/attend/pallas_call | solution.py:145
  107.9 3.6 %send_out.1 = bf16[512,1024]{1,0:T(8,128)(2,1)} custom-call(s32[1]{0:T(128)} %bitcast.3.place_ref, s32[2]{0:T(128)S(1)} %pad_add_fusion.info_ref, bf16[1024,512]{1,0:T(8,128)(2,1)} %get-tuple-element.95.c_ref.o_ref, bf16[1024,1024]{1,0:T(8,128)(2,1)} %w_ref.9, f32[512,1024]{1,0:T(8,128)S(1)} %copy-done.12), custom_call_target="tpu_custom_call" | custom-call | flops 536870 | bytes 5242 | tf_op jit(solution)/shard_map/send_out/pallas_call | solution.py:587
  111.8 1.8 add_convert_fusion.12
  113.6 1.4 collective-permute-start.9
  114.9 1.1 collective-permute-start.8
  116.0 1.1 collective-permute-start.7
  117.1 6.4 %proj_back.1 = (bf16[1024,512]{1,0:T(8,128)(2,1)}, bf16[8,32,1024]{2,1,0:T(8,128)(2,1)}, bf16[8,32,1024]{2,1,0:T(8,128)(2,1)}) custom-call(s32[2]{0:T(128)S(1)} %pad_add_fusion.info_ref, s32[16]{0:T(128)S(1)} %get-tuple-element.172.ord_ref, bf16[1024,1024]{1,0:T(8,128)(2,1)S(1)} %copy-done.6, bf16[1024,512]{1,0:T(8,128)(2,1)S(1)} %copy-done.3, ...), custom_call_target="tpu_custom_call" | custom-call | flops 2147483 | bytes 6291 | tf_op jit(solution)/shard_map/proj_back/pallas_call | solution.py:641
  123.5 2.5 %collective-permute-done.5 = bf16[4,64,2048]{2,1,0:T(8,128)(2,1)} collective-permute-done((bf16[4,64,2048]{2,1,0:T(8,128)(2,1)}, bf16[4,64,2048]{2,1,0:T(8,128)(2,1)}, u32[]{:S(2)}, u32[]{:S(2)}) %collective-permute-start.5) | collective-permute-done | bytes 1048608 | tf_op jit(solution)/shard_map/ppermute | solution.py:846
  126.0 1.6 add_convert_fusion.6
  127.8 20.2 %attend_back.1.own_ref.their_ref.d_ref = bf16[3,1024,512]{2,1,0:T(8,128)(2,1)S(1)} custom-call(s32[2]{0:T(128)S(1)} %pad_add_fusion.info_ref, bf16[8,1024,128]{2,1,0:T(8,128)(2,1)S(1)} %copy-done.14, bf16[3,1024,512]{2,1,0:T(8,128)(2,1)S(1)} %copy-done, bf16[3,1024,512]{2,1,0:T(8,128)(2,1)S(1)} %copy-done, bf16[1024,512]{1,0:T(8,128)(2,1)} %get-tuple-element.95.c_ref.o_ref, ...), custom_call_target="tpu_custom_call" | custom-call | flops 12884901 | bytes 4194 | tf_op jit(solution)/shard_map/attend_back/pallas_call | solution.py:221
  149.4 4.5 %qkv_grad.2 = (bf16[8,96,1024]{2,1,0:T(8,128)(2,1)}, bf16[8,96,1024]{2,1,0:T(8,128)(2,1)}) custom-call(s32[2]{0:T(128)S(1)} %pad_add_fusion.info_ref, s32[16]{0:T(128)S(1)} %get-tuple-element.172.ord_ref, bf16[1024,1024]{1,0:T(8,128)(2,1)S(1)} %get-tuple-element.86.x_ref, bf16[3,1024,512]{2,1,0:T(8,128)(2,1)S(1)} %attend_back.1.own_ref.their_ref.d_ref, ...), custom_call_target="tpu_custom_call" | custom-call | flops 2147483 | bytes 6291 | tf_op jit(solution)/shard_map/qkv_grad/pallas_call | solution.py:724
  154.0 1.6 collective-permute-start.11
  155.6 5.7 %grad_normed.2 = (bf16[512,1024]{1,0:T(8,128)(2,1)}, f32[2,1024]{1,0:T(2,128)S(1)}) custom-call(s32[1]{0:T(128)} %bitcast.3.place_ref, s32[2]{0:T(128)S(1)} %pad_add_fusion.info_ref, bf16[3,1024,512]{2,1,0:T(8,128)(2,1)S(1)} %attend_back.1.own_ref.their_ref.d_ref, bf16[1024,3072]{1,0:T(8,128)(2,1)} %wv_ref.3, bf16[1024,3072]{1,0:T(8,128)(2,1)} %wv_ref.3, ...), custom_call_target="tpu_custom_call" | custom-call | flops 1610612 | bytes 8912 | tf_op jit(solution)/shard_map/grad_normed/pallas_call | solution.py:770
  162.0 1.3 collective-permute-start.13
  163.4 2.3 %collective-permute-start.12 = (bf16[1,64,2048]{2,1,0:T(8,128)(2,1)S(1)}, bf16[1,64,2048]{2,1,0:T(8,128)(2,1)S(1)}, u32[]{:S(2)}, u32[]{:S(2)}) collective-permute-start(bf16[1,64,2048]{2,1,0:T(8,128)(2,1)S(1)} %get-tuple-element.156), channel_id=1, source_target_pairs={{0,16},{2,18},{4,20},{6,22},{8,24},{10,26},{12,28},{14,30},{16,0},... | collective-permute-start | bytes 786440 | tf_op jit(solution)/shard_map/ppermute | solution.py:846
  166.0 6.0 %grad_normed.3 = (f32[512,1024]{1,0:T(8,128)}, f32[2,1024]{1,0:T(2,128)S(1)}) custom-call(s32[1]{0:T(128)} %bitcast.place_ref, s32[2]{0:T(128)S(1)} %pad_add_fusion.info_ref, bf16[3,1024,512]{2,1,0:T(8,128)(2,1)S(1)} %attend_back.1.own_ref.their_ref.d_ref, bf16[1024,3072]{1,0:T(8,128)(2,1)} %wv_ref.3, bf16[1024,3072]{1,0:T(8,128)(2,1)} %wv_ref.3, ...), custom_call_target="tpu_custom_call" | custom-call | flops 1610612 | bytes 8912 | tf_op jit(solution)/shard_map/grad_normed/pallas_call | solution.py:770
  172.0 3.6 %finish_out.1 = bf16[512,1024]{1,0:T(8,128)(2,1)} custom-call(s32[1]{0:T(128)} %bitcast.place_ref, s32[2]{0:T(128)S(1)} %pad_add_fusion.info_ref, bf16[1024,512]{1,0:T(8,128)(2,1)S(1)} %copy-done.4, bf16[1024,1024]{1,0:T(8,128)(2,1)} %w_ref.9, f32[512,1024]{1,0:T(8,128)S(1)} %copy-done.13, bf16[512,1024]{1,0:T(8,128)(2,1)S(1)} %copy-done.2, ...), custom_call_target="tpu_custom_call" | custom-call | flops 536870 | bytes 5242 | tf_op jit(solution)/shard_map/finish_out/pallas_call | solution.py:587
  175.7 2.9 %qkv_grad.3 = (bf16[8,80,512]{2,1,0:T(8,128)(2,1)}, bf16[8,80,512]{2,1,0:T(8,128)(2,1)}) custom-call(s32[2]{0:T(128)S(1)} %pad_add_fusion.info_ref, s32[16]{0:T(128)S(1)} %get-tuple-element.172.ord_ref, bf16[1024,1024]{1,0:T(8,128)(2,1)S(1)} %get-tuple-element.86.x_ref, bf16[3,1024,512]{2,1,0:T(8,128)(2,1)S(1)} %attend_back.1.own_ref.their_ref.d_ref, ...), custom_call_target="tpu_custom_call" | custom-call | flops 1073741 | bytes 4194 | tf_op jit(solution)/shard_map/qkv_grad/pallas_call | solution.py:724
  178.7 2.7 %collective-permute-done.13 = bf16[4,96,1024]{2,1,0:T(8,128)(2,1)S(1)} collective-permute-done((bf16[4,96,1024]{2,1,0:T(8,128)(2,1)S(1)}, bf16[4,96,1024]{2,1,0:T(8,128)(2,1)S(1)}, u32[]{:S(2)}, u32[]{:S(2)}) %collective-permute-start.13) | collective-permute-done | bytes 786464 | tf_op jit(solution)/shard_map/ppermute | solution.py:846
  181.4 1.0 add_convert_fusion.16
  183.0 2.4 %collective-permute-start.23 = (bf16[1,96,1024]{2,1,0:T(8,128)(2,1)}, bf16[1,96,1024]{2,1,0:T(8,128)(2,1)S(1)}, u32[]{:S(2)}, u32[]{:S(2)}) collective-permute-start(bf16[1,96,1024]{2,1,0:T(8,128)(2,1)} %get-tuple-element.150), channel_id=1, source_target_pairs={{0,24},{2,26},{4,28},{6,30},{8,16},{10,18},{12,20},{14,22},{16,8},... | collective-permute-start | bytes 589832 | tf_op jit(solution)/shard_map/ppermute | solution.py:846
  186.7 3.5 %collective-permute-done.15.r_ref = bf16[512,1024]{1,0:T(8,128)(2,1)} collective-permute-done((bf16[512,1024]{1,0:T(8,128)(2,1)}, bf16[512,1024]{1,0:T(8,128)(2,1)}, u32[]{:S(2)}, u32[]{:S(2)}) %collective-permute-start.15) | collective-permute-done | bytes 1048608 | tf_op jit(solution)/shard_map/ppermute | solution.py:991
  190.5 1.4 add_convert_fusion.8
  192.2 3.5 %finish_grad.1 = f32[512,1024]{1,0:T(8,128)} custom-call(f32[512,1024]{1,0:T(8,128)S(1)} %copy-done.11, bf16[512,1024]{1,0:T(8,128)(2,1)} %collective-permute-done.15.r_ref, bf16[512,1024]{1,0:T(8,128)(2,1)S(1)} %copy-done.2, bf16[512,1024]{1,0:T(8,128)(2,1)S(1)} %copy-done.8, bf16[1,1024]{1,0:T(2,128)(2,1)S(1)} %reshape.129.gain_ref), custom_call_target="tpu_custom_call" | custom-call | flops 10485 | bytes 7340 | tf_op jit(solution)/shard_map/finish_grad/pallas_call | solution.py:826
  195.8 1.4 assemble.2
  197.1 2.2 %collective-permute-done.23 = bf16[1,96,1024]{2,1,0:T(8,128)(2,1)S(1)} collective-permute-done((bf16[1,96,1024]{2,1,0:T(8,128)(2,1)}, bf16[1,96,1024]{2,1,0:T(8,128)(2,1)S(1)}, u32[]{:S(2)}, u32[]{:S(2)}) %collective-permute-start.23) | collective-permute-done | bytes 196640 | tf_op jit(solution)/shard_map/ppermute | solution.py:846
  199.4 3.3 %collective-permute-done.22 = bf16[1,96,1024]{2,1,0:T(8,128)(2,1)S(1)} collective-permute-done((bf16[1,96,1024]{2,1,0:T(8,128)(2,1)S(1)}, bf16[1,96,1024]{2,1,0:T(8,128)(2,1)S(1)}, u32[]{:S(2)}, u32[]{:S(2)}) %collective-permute-start.22) | collective-permute-done | bytes 196640 | tf_op jit(solution)/shard_map/ppermute | solution.py:846
  203.1 4.0 %collective-permute-start.19 = (bf16[1,80,512]{2,1,0:T(8,128)(2,1)S(1)}, bf16[1,80,512]{2,1,0:T(8,128)(2,1)S(1)}, u32[]{:S(2)}, u32[]{:S(2)}) collective-permute-start(bf16[1,80,512]{2,1,0:T(8,128)(2,1)S(1)} %get-tuple-element.160), channel_id=1, source_target_pairs={{0,16},{2,18},{4,20},{6,22},{8,24},{10,26},{12,28},{14,30},{16,0},... | collective-permute-start | bytes 245768 | tf_op jit(solution)/shard_map/ppermute | solution.py:846
  207.2 5.2 %collective-permute-done.19 = bf16[1,80,512]{2,1,0:T(8,128)(2,1)S(1)} collective-permute-done((bf16[1,80,512]{2,1,0:T(8,128)(2,1)S(1)}, bf16[1,80,512]{2,1,0:T(8,128)(2,1)S(1)}, u32[]{:S(2)}, u32[]{:S(2)}) %collective-permute-start.19) | collective-permute-done | bytes 81952 | tf_op jit(solution)/shard_map/ppermute | solution.py:846
  213.0 5.0 %collective-permute-start.25 = (bf16[32,1024]{1,0:T(8,128)(2,1)S(1)}, bf16[32,1024]{1,0:T(8,128)(2,1)S(1)}, u32[]{:S(2)}, u32[]{:S(2)}) collective-permute-start(bf16[32,1024]{1,0:T(8,128)(2,1)S(1)} %fusion.3), channel_id=1, source_target_pairs={{0,0},{2,1},{4,2},{6,3},{8,4},{10,5},{12,6},{14,7},{16,8},{18,9},{... | collective-permute-start | bytes 196616 | tf_op jit(solution)/shard_map/ppermute | solution.py:1038
  218.6 1.3 collective-permute-done.25
  221.2 1.3 assemble.3
  (121 shorter events, 12.8 us)
Async XLA Ops:
  0.6 32.9 %collective-permute-start = (bf16[512,1024]{1,0:T(8,128)(2,1)}, bf16[512,1024]{1,0:T(8,128)(2,1)}, u32[]{:S(2)}, u32[]{:S(2)}) collective-permute-start(bf16[512,1024]{1,0:T(8,128)(2,1)} %t_ref.7), channel_id=1, source_target_pairs={{0,1},{1,0},{2,3},{3,2},{4,5},{5,4},{6,7},{7,6},{8,9},{9,8},{10,11... | collective-permute-start | bytes 3145736 | tf_op jit(solution)/shard_map/ppermute | solution.py:903
  1.0 46.6 %collective-permute-start.1 = (bf16[512,1024]{1,0:T(8,128)(2,1)}, bf16[512,1024]{1,0:T(8,128)(2,1)}, u32[]{:S(2)}, u32[]{:S(2)}) collective-permute-start(bf16[512,1024]{1,0:T(8,128)(2,1)} %c_ref.1), channel_id=1, source_target_pairs={{0,1},{1,0},{2,3},{3,2},{4,5},{5,4},{6,7},{7,6},{8,9},{9,8},{10,11... | collective-permute-start | bytes 3145736 | tf_op jit(solution)/shard_map/ppermute | solution.py:904
  33.6 14.0 %copy-start.7 = (bf16[512,1024]{1,0:T(8,128)(2,1)S(1)}, bf16[512,1024]{1,0:T(8,128)(2,1)}, u32[]{:S(2)}) copy-start(bf16[512,1024]{1,0:T(8,128)(2,1)} %get-tuple-element.82.go_ref.g_ref) | copy-start | bytes 3145732
  47.5 11.8 %copy-start.24 = (s32[16]{0:T(128)S(1)}, s32[16]{0:T(128)}, u32[]{:S(2)}) copy-start(s32[16]{0:T(128)} %constant.77.clone) | copy-start | bytes 196
  47.5 11.8 %copy-start.25 = (s32[16]{0:T(128)S(1)}, s32[16]{0:T(128)}, u32[]{:S(2)}) copy-start(s32[16]{0:T(128)} %constant.79.clone) | copy-start | bytes 196
  57.7 18.8 %collective-permute-start.2 = (bf16[8,128,1024]{2,1,0:T(8,128)(2,1)}, bf16[8,128,1024]{2,1,0:T(8,128)(2,1)S(1)}, u32[]{:S(2)}, u32[]{:S(2)}) collective-permute-start(bf16[8,128,1024]{2,1,0:T(8,128)(2,1)} %get-tuple-element.90), channel_id=1, source_target_pairs={{0,2},{2,0},{4,6},{6,4},{8,10},{10,8},{12,14},{14,12},{16,18},{18,... | collective-permute-start | bytes 6291464 | tf_op jit(solution)/shard_map/ppermute | solution.py:846
  59.3 1.6 copy-start.5
  60.9 15.7 %copy-start.20 = (bf16[8,128,1024]{2,1,0:T(8,128)(2,1)S(1)}, bf16[8,128,1024]{2,1,0:T(8,128)(2,1)}, u32[]{:S(2)}) copy-start(bf16[8,128,1024]{2,1,0:T(8,128)(2,1)} %get-tuple-element.89) | copy-start | bytes 6291460
  76.4 4.4 %collective-permute-start.3 = (bf16[8,64,2048]{2,1,0:T(8,128)(2,1)}, bf16[8,64,2048]{2,1,0:T(8,128)(2,1)S(1)}, u32[]{:S(2)}, u32[]{:S(2)}) collective-permute-start(bf16[8,64,2048]{2,1,0:T(8,128)(2,1)} %get-tuple-element.93), channel_id=1, source_target_pairs={{0,2},{2,0},{4,6},{6,4},{8,10},{10,8},{12,14},{14,12},{16,18},{18,... | collective-permute-start | bytes 6291464 | tf_op jit(solution)/shard_map/ppermute | solution.py:846
  76.5 4.3 %copy-start.21 = (bf16[8,64,2048]{2,1,0:T(8,128)(2,1)S(1)}, bf16[8,64,2048]{2,1,0:T(8,128)(2,1)}, u32[]{:S(2)}) copy-start(bf16[8,64,2048]{2,1,0:T(8,128)(2,1)} %get-tuple-element.92) | copy-start | bytes 6291460
  78.9 32.9 %collective-permute-start.4 = (bf16[4,128,1024]{2,1,0:T(8,128)(2,1)}, bf16[4,128,1024]{2,1,0:T(8,128)(2,1)}, u32[]{:S(2)}, u32[]{:S(2)}) collective-permute-start(bf16[4,128,1024]{2,1,0:T(8,128)(2,1)} %get-tuple-element.140), channel_id=1, source_target_pairs={{0,4},{2,6},{4,0},{6,2},{8,12},{10,14},{12,8},{14,10},{16,20},{18,... | collective-permute-start | bytes 3145736 | tf_op jit(solution)/shard_map/ppermute | solution.py:846
  83.0 42.9 %collective-permute-start.5 = (bf16[4,64,2048]{2,1,0:T(8,128)(2,1)}, bf16[4,64,2048]{2,1,0:T(8,128)(2,1)}, u32[]{:S(2)}, u32[]{:S(2)}) collective-permute-start(bf16[4,64,2048]{2,1,0:T(8,128)(2,1)} %get-tuple-element.138), channel_id=1, source_target_pairs={{0,4},{2,6},{4,0},{6,2},{8,12},{10,14},{12,8},{14,10},{16,20},{18,... | collective-permute-start | bytes 3145736 | tf_op jit(solution)/shard_map/ppermute | solution.py:846
  90.2 17.7 %copy-start.12 = (f32[512,1024]{1,0:T(8,128)S(1)}, f32[512,1024]{1,0:T(8,128)}, u32[]{:S(2)}) copy-start(f32[512,1024]{1,0:T(8,128)} %get-tuple-element.96.e_ref) | copy-start | bytes 6291460
  107.9 3.9 %copy-start.19 = (bf16[4,128,1024]{2,1,0:T(8,128)(2,1)S(1)}, bf16[4,128,1024]{2,1,0:T(8,128)(2,1)}, u32[]{:S(2)}) copy-start(bf16[4,128,1024]{2,1,0:T(8,128)(2,1)} %get-tuple-element.97) | copy-start | bytes 3145732
  111.5 5.6 %copy-start.3 = (bf16[1024,512]{1,0:T(8,128)(2,1)S(1)}, bf16[1024,512]{1,0:T(8,128)(2,1)}, u32[]{:S(2)}) copy-start(bf16[1024,512]{1,0:T(8,128)(2,1)} %get-tuple-element.95.c_ref.o_ref) | copy-start | bytes 3145732
  111.5 5.6 %copy-start.6 = (bf16[1024,1024]{1,0:T(8,128)(2,1)S(1)}, bf16[1024,1024]{1,0:T(8,128)(2,1)}, u32[]{:S(2)}) copy-start(bf16[1024,1024]{1,0:T(8,128)(2,1)} %get-tuple-element.83.g_ref) | copy-start | bytes 6291460
  111.5 37.7 %collective-permute-start.6 = (bf16[512,1024]{1,0:T(8,128)(2,1)}, bf16[512,1024]{1,0:T(8,128)(2,1)S(1)}, u32[]{:S(2)}, u32[]{:S(2)}) collective-permute-start(bf16[512,1024]{1,0:T(8,128)(2,1)} %send_out.1), channel_id=1, source_target_pairs={{0,1},{1,0},{2,3},{3,2},{4,5},{5,4},{6,7},{7,6},{8,9},{9,8},{10,11... | collective-permute-start | bytes 3145736 | tf_op jit(solution)/shard_map/ppermute | solution.py:972
  113.6 34.5 %collective-permute-start.9 = (bf16[1,128,1024]{2,1,0:T(8,128)(2,1)S(1)}, bf16[1,128,1024]{2,1,0:T(8,128)(2,1)S(1)}, u32[]{:S(2)}, u32[]{:S(2)}) collective-permute-start(bf16[1,128,1024]{2,1,0:T(8,128)(2,1)S(1)} %get-tuple-element.146), channel_id=1, source_target_pairs={{0,24},{2,26},{4,28},{6,30},{8,16},{10,18},{12,20},{14,22},{16,8},... | collective-permute-start | bytes 786440 | tf_op jit(solution)/shard_map/ppermute | solution.py:846
  114.9 33.2 %collective-permute-start.8 = (bf16[1,128,1024]{2,1,0:T(8,128)(2,1)S(1)}, bf16[1,128,1024]{2,1,0:T(8,128)(2,1)S(1)}, u32[]{:S(2)}, u32[]{:S(2)}) collective-permute-start(bf16[1,128,1024]{2,1,0:T(8,128)(2,1)S(1)} %get-tuple-element.147), channel_id=1, source_target_pairs={{0,16},{2,18},{4,20},{6,22},{8,24},{10,26},{12,28},{14,30},{16,0},... | collective-permute-start | bytes 786440 | tf_op jit(solution)/shard_map/ppermute | solution.py:846
  116.0 32.1 %collective-permute-start.7 = (bf16[1,128,1024]{2,1,0:T(8,128)(2,1)S(1)}, bf16[1,128,1024]{2,1,0:T(8,128)(2,1)S(1)}, u32[]{:S(2)}, u32[]{:S(2)}) collective-permute-start(bf16[1,128,1024]{2,1,0:T(8,128)(2,1)S(1)} %get-tuple-element.148), channel_id=1, source_target_pairs={{0,8},{2,10},{4,12},{6,14},{8,0},{10,2},{12,4},{14,6},{16,24},{18,... | collective-permute-start | bytes 786440 | tf_op jit(solution)/shard_map/ppermute | solution.py:846
  117.1 8.9 %copy-start.18 = (bf16[4,64,2048]{2,1,0:T(8,128)(2,1)S(1)}, bf16[4,64,2048]{2,1,0:T(8,128)(2,1)}, u32[]{:S(2)}) copy-start(bf16[4,64,2048]{2,1,0:T(8,128)(2,1)} %get-tuple-element.100) | copy-start | bytes 3145732
  117.1 10.7 %copy-start.14 = (bf16[8,1024,128]{2,1,0:T(8,128)(2,1)S(1)}, bf16[8,1024,128]{2,1,0:T(8,128)(2,1)}, u32[]{:S(2)}) copy-start(bf16[8,1024,128]{2,1,0:T(8,128)(2,1)} %get-tuple-element.102.qe_ref) | copy-start | bytes 6291460
  123.5 4.3 %copy-start = (bf16[3,1024,512]{2,1,0:T(8,128)(2,1)S(1)}, bf16[3,1024,512]{2,1,0:T(8,128)(2,1)}, u32[]{:S(2)}) copy-start(bf16[3,1024,512]{2,1,0:T(8,128)(2,1)} %qkv.3.q_ref.k_ref.v_ref) | copy-start | bytes 9437188
  127.6 21.5 %collective-permute-start.10 = (bf16[2,64,2048]{2,1,0:T(8,128)(2,1)S(1)}, bf16[2,64,2048]{2,1,0:T(8,128)(2,1)S(1)}, u32[]{:S(2)}, u32[]{:S(2)}) collective-permute-start(bf16[2,64,2048]{2,1,0:T(8,128)(2,1)S(1)} %get-tuple-element.144), channel_id=1, source_target_pairs={{0,8},{2,10},{4,12},{6,14},{8,0},{10,2},{12,4},{14,6},{16,24},{18,... | collective-permute-start | bytes 1572872 | tf_op jit(solution)/shard_map/ppermute | solution.py:846
  149.4 6.1 %copy-start.10 = (f32[512,1024]{1,0:T(8,128)S(1)}, f32[512,1024]{1,0:T(8,128)}, u32[]{:S(2)}) copy-start(f32[512,1024]{1,0:T(8,128)} %get-tuple-element.88.base_ref) | copy-start | bytes 6291460
  154.0 7.3 %collective-permute-start.11 = (bf16[8,96,1024]{2,1,0:T(8,128)(2,1)}, bf16[8,96,1024]{2,1,0:T(8,128)(2,1)S(1)}, u32[]{:S(2)}, u32[]{:S(2)}) collective-permute-start(bf16[8,96,1024]{2,1,0:T(8,128)(2,1)} %get-tuple-element.109), channel_id=1, source_target_pairs={{0,2},{2,0},{4,6},{6,4},{8,10},{10,8},{12,14},{14,12},{16,18},{18,... | collective-permute-start | bytes 4718600 | tf_op jit(solution)/shard_map/ppermute | solution.py:846
  155.6 5.8 %copy-start.22 = (bf16[8,96,1024]{2,1,0:T(8,128)(2,1)S(1)}, bf16[8,96,1024]{2,1,0:T(8,128)(2,1)}, u32[]{:S(2)}) copy-start(bf16[8,96,1024]{2,1,0:T(8,128)(2,1)} %get-tuple-element.112) | copy-start | bytes 4718596
  161.3 4.4 %copy-start.23 = (bf16[1024]{0:T(1024)(128)(2,1)S(1)}, bf16[1024]{0:T(1024)(128)(2,1)}, u32[]{:S(2)}) copy-start(bf16[1024]{0:T(1024)(128)(2,1)} %param.23) | copy-start | bytes 6148
  161.3 4.7 %copy-start.2 = (bf16[512,1024]{1,0:T(8,128)(2,1)S(1)}, bf16[512,1024]{1,0:T(8,128)(2,1)}, u32[]{:S(2)}) copy-start(bf16[512,1024]{1,0:T(8,128)(2,1)} %t_ref.7) | copy-start | bytes 3145732
  161.3 4.7 %copy-start.9 = (f32[512,1024]{1,0:T(8,128)S(1)}, f32[512,1024]{1,0:T(8,128)}, u32[]{:S(2)}) copy-start(f32[512,1024]{1,0:T(8,128)} %get-tuple-element.114.base_ref) | copy-start | bytes 6291460
  162.0 19.3 %collective-permute-start.13 = (bf16[4,96,1024]{2,1,0:T(8,128)(2,1)S(1)}, bf16[4,96,1024]{2,1,0:T(8,128)(2,1)S(1)}, u32[]{:S(2)}, u32[]{:S(2)}) collective-permute-start(bf16[4,96,1024]{2,1,0:T(8,128)(2,1)S(1)} %get-tuple-element.142), channel_id=1, source_target_pairs={{0,4},{2,6},{4,0},{6,2},{8,12},{10,14},{12,8},{14,10},{16,20},{18,... | collective-permute-start | bytes 2359304 | tf_op jit(solution)/shard_map/ppermute | solution.py:846
  163.4 15.3 %collective-permute-start.12 = (bf16[1,64,2048]{2,1,0:T(8,128)(2,1)S(1)}, bf16[1,64,2048]{2,1,0:T(8,128)(2,1)S(1)}, u32[]{:S(2)}, u32[]{:S(2)}) collective-permute-start(bf16[1,64,2048]{2,1,0:T(8,128)(2,1)S(1)} %get-tuple-element.156), channel_id=1, source_target_pairs={{0,16},{2,18},{4,20},{6,22},{8,24},{10,26},{12,28},{14,30},{16,0},... | collective-permute-start | bytes 786440 | tf_op jit(solution)/shard_map/ppermute | solution.py:846
  165.7 24.5 %collective-permute-start.15 = (bf16[512,1024]{1,0:T(8,128)(2,1)}, bf16[512,1024]{1,0:T(8,128)(2,1)}, u32[]{:S(2)}, u32[]{:S(2)}) collective-permute-start(bf16[512,1024]{1,0:T(8,128)(2,1)} %get-tuple-element.111), channel_id=1, source_target_pairs={{0,1},{1,0},{2,3},{3,2},{4,5},{5,4},{6,7},{7,6},{8,9},{9,8},{10,11... | collective-permute-start | bytes 3145736 | tf_op jit(solution)/shard_map/ppermute | solution.py:991
  166.0 6.0 %copy-start.4 = (bf16[1024,512]{1,0:T(8,128)(2,1)S(1)}, bf16[1024,512]{1,0:T(8,128)(2,1)}, u32[]{:S(2)}) copy-start(bf16[1024,512]{1,0:T(8,128)(2,1)} %get-tuple-element.95.c_ref.o_ref) | copy-start | bytes 3145732
  166.0 6.0 %copy-start.13 = (f32[512,1024]{1,0:T(8,128)S(1)}, f32[512,1024]{1,0:T(8,128)}, u32[]{:S(2)}) copy-start(f32[512,1024]{1,0:T(8,128)} %get-tuple-element.117.e_ref) | copy-start | bytes 6291460
  178.7 13.5 %copy-start.8 = (bf16[512,1024]{1,0:T(8,128)(2,1)S(1)}, bf16[512,1024]{1,0:T(8,128)(2,1)}, u32[]{:S(2)}) copy-start(bf16[512,1024]{1,0:T(8,128)(2,1)} %get-tuple-element.82.go_ref.g_ref) | copy-start | bytes 3145732
  182.4 8.1 %collective-permute-start.16 = (bf16[8,80,512]{2,1,0:T(8,128)(2,1)}, bf16[8,80,512]{2,1,0:T(8,128)(2,1)}, u32[]{:S(2)}, u32[]{:S(2)}) collective-permute-start(bf16[8,80,512]{2,1,0:T(8,128)(2,1)} %get-tuple-element.131), channel_id=1, source_target_pairs={{0,2},{2,0},{4,6},{6,4},{8,10},{10,8},{12,14},{14,12},{16,18},{18,... | collective-permute-start | bytes 1966088 | tf_op jit(solution)/shard_map/ppermute | solution.py:846
  183.0 9.2 %copy-start.11 = (f32[512,1024]{1,0:T(8,128)S(1)}, f32[512,1024]{1,0:T(8,128)}, u32[]{:S(2)}) copy-start(f32[512,1024]{1,0:T(8,128)} %get-tuple-element.115.gn_ref) | copy-start | bytes 6291460
  183.0 16.3 %collective-permute-start.23 = (bf16[1,96,1024]{2,1,0:T(8,128)(2,1)}, bf16[1,96,1024]{2,1,0:T(8,128)(2,1)S(1)}, u32[]{:S(2)}, u32[]{:S(2)}) collective-permute-start(bf16[1,96,1024]{2,1,0:T(8,128)(2,1)} %get-tuple-element.150), channel_id=1, source_target_pairs={{0,24},{2,26},{4,28},{6,30},{8,16},{10,18},{12,20},{14,22},{16,8},... | collective-permute-start | bytes 589832 | tf_op jit(solution)/shard_map/ppermute | solution.py:846
  185.5 17.2 %collective-permute-start.22 = (bf16[1,96,1024]{2,1,0:T(8,128)(2,1)S(1)}, bf16[1,96,1024]{2,1,0:T(8,128)(2,1)S(1)}, u32[]{:S(2)}, u32[]{:S(2)}) collective-permute-start(bf16[1,96,1024]{2,1,0:T(8,128)(2,1)S(1)} %get-tuple-element.151), channel_id=1, source_target_pairs={{0,16},{2,18},{4,20},{6,22},{8,24},{10,26},{12,28},{14,30},{16,0},... | collective-permute-start | bytes 589832 | tf_op jit(solution)/shard_map/ppermute | solution.py:846
  186.4 16.2 %collective-permute-start.21 = (bf16[1,96,1024]{2,1,0:T(8,128)(2,1)S(1)}, bf16[1,96,1024]{2,1,0:T(8,128)(2,1)S(1)}, u32[]{:S(2)}, u32[]{:S(2)}) collective-permute-start(bf16[1,96,1024]{2,1,0:T(8,128)(2,1)S(1)} %get-tuple-element.152), channel_id=1, source_target_pairs={{0,8},{2,10},{4,12},{6,14},{8,0},{10,2},{12,4},{14,6},{16,24},{18,... | collective-permute-start | bytes 589832 | tf_op jit(solution)/shard_map/ppermute | solution.py:846
  190.2 5.6 %collective-permute-start.14 = (bf16[32,2048]{1,0:T(8,128)(2,1)S(1)}, bf16[32,2048]{1,0:T(8,128)(2,1)S(1)}, u32[]{:S(2)}, u32[]{:S(2)}) collective-permute-start(bf16[32,2048]{1,0:T(8,128)(2,1)S(1)} %dynamic-slice_convert_fusion), channel_id=1, source_target_pairs={{0,1},{1,0},{2,3},{3,2},{4,5},{5,4},{6,7},{7,6},{8,9},{9,8},{10,11... | collective-permute-start | bytes 393224 | tf_op jit(solution)/shard_map/ppermute | solution.py:1017
  191.9 10.9 %collective-permute-start.17 = (bf16[4,80,512]{2,1,0:T(8,128)(2,1)S(1)}, bf16[4,80,512]{2,1,0:T(8,128)(2,1)S(1)}, u32[]{:S(2)}, u32[]{:S(2)}) collective-permute-start(bf16[4,80,512]{2,1,0:T(8,128)(2,1)S(1)} %get-tuple-element.154), channel_id=1, source_target_pairs={{0,4},{2,6},{4,0},{6,2},{8,12},{10,14},{12,8},{14,10},{16,20},{18,... | collective-permute-start | bytes 983048 | tf_op jit(solution)/shard_map/ppermute | solution.py:846
  202.9 4.4 %collective-permute-start.20 = (bf16[1,80,512]{2,1,0:T(8,128)(2,1)S(1)}, bf16[1,80,512]{2,1,0:T(8,128)(2,1)S(1)}, u32[]{:S(2)}, u32[]{:S(2)}) collective-permute-start(bf16[1,80,512]{2,1,0:T(8,128)(2,1)S(1)} %get-tuple-element.159), channel_id=1, source_target_pairs={{0,24},{2,26},{4,28},{6,30},{8,16},{10,18},{12,20},{14,22},{16,8},... | collective-permute-start | bytes 245768 | tf_op jit(solution)/shard_map/ppermute | solution.py:846
  203.1 9.3 %collective-permute-start.19 = (bf16[1,80,512]{2,1,0:T(8,128)(2,1)S(1)}, bf16[1,80,512]{2,1,0:T(8,128)(2,1)S(1)}, u32[]{:S(2)}, u32[]{:S(2)}) collective-permute-start(bf16[1,80,512]{2,1,0:T(8,128)(2,1)S(1)} %get-tuple-element.160), channel_id=1, source_target_pairs={{0,16},{2,18},{4,20},{6,22},{8,24},{10,26},{12,28},{14,30},{16,0},... | collective-permute-start | bytes 245768 | tf_op jit(solution)/shard_map/ppermute | solution.py:846
  207.1 5.4 %collective-permute-start.18 = (bf16[1,80,512]{2,1,0:T(8,128)(2,1)S(1)}, bf16[1,80,512]{2,1,0:T(8,128)(2,1)S(1)}, u32[]{:S(2)}, u32[]{:S(2)}) collective-permute-start(bf16[1,80,512]{2,1,0:T(8,128)(2,1)S(1)} %get-tuple-element.158), channel_id=1, source_target_pairs={{0,8},{2,10},{4,12},{6,14},{8,0},{10,2},{12,4},{14,6},{16,24},{18,... | collective-permute-start | bytes 245768 | tf_op jit(solution)/shard_map/ppermute | solution.py:846
  212.7 7.9 %collective-permute-start.24 = (bf16[48,1536]{1,0:T(8,128)(2,1)S(1)}, bf16[48,1536]{1,0:T(8,128)(2,1)S(1)}, u32[]{:S(2)}, u32[]{:S(2)}) collective-permute-start(bf16[48,1536]{1,0:T(8,128)(2,1)S(1)} %maximum_maximum_fusion), channel_id=1, source_target_pairs={{0,1},{1,0},{2,3},{3,2},{4,5},{5,4},{6,7},{7,6},{8,9},{9,8},{10,11... | collective-permute-start | bytes 442376 | tf_op jit(solution)/shard_map/ppermute | solution.py:1039
  213.0 6.9 %collective-permute-start.25 = (bf16[32,1024]{1,0:T(8,128)(2,1)S(1)}, bf16[32,1024]{1,0:T(8,128)(2,1)S(1)}, u32[]{:S(2)}, u32[]{:S(2)}) collective-permute-start(bf16[32,1024]{1,0:T(8,128)(2,1)S(1)} %fusion.3), channel_id=1, source_target_pairs={{0,0},{2,1},{4,2},{6,3},{8,4},{10,5},{12,6},{14,7},{16,8},{18,9},{... | collective-permute-start | bytes 196616 | tf_op jit(solution)/shard_map/ppermute | solution.py:1038
  (4 other events, 5.0 us)
